TPU v7x, 128 devices: a whole 4x4x4 slice. The times are simulated.
128 devices in a mesh: ends: 2 (over z_hi), dp: 8 (over y, core), tp: 8 (over z_lo, x).
Axes of the slice: x: 4, y: 4, z: 4 (z_hi: 2, z_lo: 2; z = z_hi * 2 + z_lo), core: 2. Of those that a mesh axis runs over, the one named last changes fastest.
Arguments:
- grad: bfloat16 [2, 8, 16384, 3072], P('ends', 'dp', 'tp'), may hold values from -1800 to 1800
- master: float32 [8, 2048, 3072], P('tp', ('ends', 'dp')), may hold values from -3 to 3
- moment: float32 [8, 2048, 3072], P('tp', ('ends', 'dp')), may hold values from -3 to 3
- second: float32 [8, 2048, 3072], P('tp', ('ends', 'dp')), may hold values from 0.01 to 1
Outputs:
- weights: bfloat16 [16384, 3072], P('tp')
- master_out: float32 [8, 2048, 3072], P('tp', ('ends', 'dp'))
- moment_out: float32 [8, 2048, 3072], P('tp', ('ends', 'dp'))
- second_out: float32 [8, 2048, 3072], P('tp', ('ends', 'dp'))
All inputs are finite; a program needn't handle non-finite values.
Results may differ from a plain program's by a relative error of at most 0.0034.
Values may be sent and summed in bfloat16 or wider, within the bound.
No kernel may reach another device: no remote copies, remote signals or barrier semaphores. Data moves between devices by JAX's collectives and lax.ppermute only.
A program may use at most 128 MiB of HBM per device.

v0:
```python
import jax
import jax.numpy as jnp
from jax import lax
from jax.sharding import Mesh
from jax.sharding import PartitionSpec as P

STEP = 10
ENDS_DP = ("ends", "dp_0", "dp_1")
ENDS_DP_TP = ("ends", "dp_0", "dp_1", "tp_0", "tp_1")
TP = ("tp_0", "tp_1")
DP = ("dp_0", "dp_1")


def one_axis_at_a_time(x, axes):
    for axis in axes:
        x = lax.psum(x, axis)
    return x


def per_device(grad, master, moment, second):
    rows_tp = grad.shape[2]
    width = grad.shape[3]
    local = grad[0, 0].astype(jnp.float32)
    summed = lax.psum_scatter(
        local.astype(jnp.bfloat16), ENDS_DP, scatter_dimension=0, tiled=True
    ).astype(jnp.float32)
    squares = one_axis_at_a_time(jnp.sum(summed * summed), ENDS_DP_TP)
    vocab_total = rows_tp * lax.axis_size(TP)
    factor = jnp.minimum(
        jnp.float32(1.0), jnp.sqrt(jnp.float32(vocab_total * width)) / (jnp.sqrt(squares) + 1e-06)
    )
    clipped = factor * summed
    moment_out = 0.9 * moment[0] + 0.1 * clipped
    second_out = 0.999 * second[0] + 0.001 * clipped * clipped
    update = moment_out / (1.0 - 0.9**STEP) / (jnp.sqrt(second_out / (1.0 - 0.999**STEP)) + 1e-08)
    master_out = master[0] - 0.01 * (update + 0.1 * master[0])
    rounded = master_out.astype(jnp.bfloat16)
    weights = lax.all_gather(rounded, ENDS_DP, axis=0, tiled=True)
    return (weights, master_out[None], moment_out[None], second_out[None])


def solution(mesh):
    finer = Mesh(
        mesh.devices.reshape(mesh.shape["ends"], 4, 2, 2, 4),
        ("ends", "dp_0", "dp_1", "tp_0", "tp_1"),
    )
    return jax.shard_map(
        per_device,
        mesh=finer,
        in_specs=(
            P("ends", DP, TP, None),
            P(TP, ENDS_DP, None),
            P(TP, ENDS_DP, None),
            P(TP, ENDS_DP, None),
        ),
        out_specs=(P(TP, None), P(TP, ENDS_DP, None), P(TP, ENDS_DP, None), P(TP, ENDS_DP, None)),
        check_vma=False,
    )
```

profile of v0, /device:TPU:1, one launch (start us, length us, event | category | flops | bytes accessed | tf_op | source)
XLA Modules:
  0.0 287.3 jit_solution(16388377666645234331)
XLA Ops:
  7.2 0.0 reduce-scatter.2.cloned.1.call-start
  7.2 0.0 copy-start
  7.2 0.0 copy-start.1
  7.2 0.7 reduce-scatter.2.cloned.1.call-update
  7.9 0.0 all-gather.2.cloned.1.call-start
  7.9 129.3 %reduce-scatter.2.cloned.1.call-done = bf16[128,3072]{1,0:T(8,128)(2,1)} async-done(((bf16[2048,3072]{1,0:T(8,128)(2,1)}), bf16[128,3072]{1,0:T(8,128)(2,1)}) %reduce-scatter.2.cloned.1.call-update) | async-done | bytes 786448 | tf_op jit(solution)/shard_map/reduce_scatter | solution.py:24
  137.3 2.1 fusion.2
  139.4 5.9 %psum.35 = f32[]{:T(128)} all-reduce(f32[]{:T(128)} %fusion.2), channel_id=1, replica_groups=mesh['ends'=2,'dp_0'=4,'dp_1'=2,'tp_0'=2,'tp_1'=4] {'ends'}, use_global_device_ids=true, to_apply=%region_2.0 | all-reduce | flops 1 | bytes 8 | tf_op jit(solution)/shard_map/psum | solution.py:16
  145.3 7.5 %psum.36 = f32[]{:T(128)} all-reduce(f32[]{:T(128)} %psum.35), channel_id=1, replica_groups=mesh['ends'=2,'dp_0'=4,'dp_1'=2,'tp_0'=2,'tp_1'=4] {'dp_0'}, use_global_device_ids=true, to_apply=%region_3.0 | all-reduce | flops 1 | bytes 8 | tf_op jit(solution)/shard_map/psum | solution.py:16
  152.8 8.2 %psum.37 = f32[]{:T(128)} all-reduce(f32[]{:T(128)} %psum.36), channel_id=1, replica_groups=mesh['ends'=2,'dp_0'=4,'dp_1'=2,'tp_0'=2,'tp_1'=4] {'dp_1'}, use_global_device_ids=true, to_apply=%region_4.0 | all-reduce | flops 1 | bytes 8 | tf_op jit(solution)/shard_map/psum | solution.py:16
  161.0 4.4 %psum.38 = f32[]{:T(128)} all-reduce(f32[]{:T(128)} %psum.37), channel_id=1, replica_groups=mesh['ends'=2,'dp_0'=4,'dp_1'=2,'tp_0'=2,'tp_1'=4] {'tp_0'}, use_global_device_ids=true, to_apply=%region_5.0 | all-reduce | flops 1 | bytes 8 | tf_op jit(solution)/shard_map/psum | solution.py:16
  165.4 9.0 %psum.39 = f32[]{:T(128)} all-reduce(f32[]{:T(128)} %psum.38), channel_id=1, replica_groups=mesh['ends'=2,'dp_0'=4,'dp_1'=2,'tp_0'=2,'tp_1'=4] {'tp_1'}, use_global_device_ids=true, to_apply=%region_6.0 | all-reduce | flops 1 | bytes 8 | tf_op jit(solution)/shard_map/psum | solution.py:16
  175.1 0.0 copy-done
  175.2 0.0 copy-done.1
  175.2 5.4 %fusion.8 = (bf16[128,3072]{1,0:T(8,128)(2,1)}, f32[128,3072]{1,0:T(8,128)}, f32[1,128,3072]{2,1,0:T(8,128)}, f32[1,128,3072]{2,1,0:T(8,128)}) fusion(f32[1,128,3072]{2,1,0:T(8,128)S(1)} %copy-done, bf16[128,3072]{1,0:T(8,128)(2,1)} %reduce-scatter.2.cloned.1.call-done, f32[]{:T(128)S(6)} %min_shard_map.3, f32[1,128,3072]{2,1,0:T(8,128)S(1)} %copy-done.1, ...), kind=kLoop, calls=%fused_computation.13 | loop fusion | flops 7077888 | bytes 11010052 | tf_op jit(solution)/shard_map/convert_element_type | solution.py:37
  180.5 0.0 all-gather.2.cloned.1.call-update
  180.6 89.3 %all-gather.2.cloned.1.call-done = bf16[2048,3072]{1,0:T(8,128)(2,1)} async-done(((bf16[128,3072]{1,0:T(8,128)(2,1)}), bf16[2048,3072]{1,0:T(8,128)(2,1)}) %all-gather.2.cloned.1.call-update) | async-done | bytes 12582928 | tf_op jit(solution)/shard_map/all_gather | solution.py:38
  269.9 10.5 %copy.9 = bf16[2048,3072]{1,0:T(8,128)(2,1)} copy(bf16[2048,3072]{1,0:T(8,128)(2,1)} %all-gather.2.cloned.1.call-done) | data formatting | bytes 25165824
Async XLA Ops:
  7.2 130.1 %reduce-scatter.2.cloned.1.call-start = ((), (), s32[]{:S(2)}) async-start(), calls=%async_computation.1 | async-start | bytes 13369344 | tf_op jit(solution)/shard_map/reduce_scatter | solution.py:24
  7.2 167.9 %copy-start = (f32[1,128,3072]{2,1,0:T(8,128)S(1)}, f32[1,128,3072]{2,1,0:T(8,128)}, u32[]{:S(2)}) copy-start(f32[1,128,3072]{2,1,0:T(8,128)} %param.7) | copy-start | bytes 4718596
  7.2 167.9 %copy-start.1 = (f32[1,128,3072]{2,1,0:T(8,128)S(1)}, f32[1,128,3072]{2,1,0:T(8,128)}, u32[]{:S(2)}) copy-start(f32[1,128,3072]{2,1,0:T(8,128)} %param.6) | copy-start | bytes 4718596
  7.9 262.0 %all-gather.2.cloned.1.call-start = ((), (), s32[]{:S(2)}) async-start(), calls=%async_computation.2 | async-start | bytes 13369344 | tf_op jit(solution)/shard_map/all_gather | solution.py:38
Sparse Core Ops, SparseCore 0:
  12.4 124.8 reduce-scatter.1
  180.7 89.1 all-gather.1
where the time goes:
time: 288 us; the launch traced here: 287 us
  waiting for transfers between devices  219 us (76%)
  blocking collectives  35 us (12%)
  between operations  14.8 us (5%)
  local copies, waits for them, and re-layouts  10.5 us (4%)
  other arithmetic  7.52 us (3%)
    reduce_scatter x1, waiting for transfers between devices, per_device(): lax.psum_scatter(local.astype(jnp.bfloat16), ENDS_DP, scatter_dimension=0...  129 us
    all_gather x1, waiting for transfers between devices, per_device(): weights = lax.all_gather(rounded, ENDS_DP, axis=0, tiled=True)  89.3 us
    psum x5, blocking collectives, one_axis_at_a_time(): x = lax.psum(x, axis)  35 us
    unnamed x5, local copies, waits for them, and re-layouts  10.5 us
  transfers between devices with their start and end apart: 2, of which 2 were waited for; matrix products, arithmetic and copies ran while one was open for 0% of the time, Pallas kernels for 0%

commit v1 on v0

v1 whole, which is shorter than its diff:
```python
import jax
import jax.numpy as jnp
from jax import lax
from jax.experimental import pallas as pl
from jax.experimental.pallas import tpu as pltpu
from jax.sharding import Mesh
from jax.sharding import PartitionSpec as P

STEP = 10
ENDS_DP = ("ends", "dp_0", "dp_1")
TP = ("tp_0", "tp_1")
DP = ("dp_0", "dp_1")

SIZE = (32, 32, 32, 32)
START = (0, 32, 64, 96)
P1, P3, Z = "p1", "p3", "z"


def over(link, seg):
    de, dy, q = seg
    if link == P1:
        return (de, dy ^ 1, q)
    if link == P3:
        return (de, dy ^ 3, q)
    return (de ^ 1, dy, q)


REDUCE = (
    {
        Z: ((1, 2, 1), (1, 1, 1), (1, 2, 2), (1, 3, 2)),
        P1: ((1, 2, 0), (0, 2, 0), (1, 1, 0), (0, 1, 0)),
        P3: ((1, 2, 3), (0, 2, 3), (1, 3, 3), (0, 3, 3)),
    },
    {
        Z: ((1, 0, 1), (1, 0, 2), (1, 3, 1), (1, 1, 2)),
        P1: ((1, 1, 3), (0, 1, 3), (0, 2, 1), (0, 1, 1)),
        P3: ((1, 3, 0), (0, 3, 0), (0, 2, 2), (0, 3, 2)),
    },
    {
        Z: ((1, 0, 0), (1, 0, 3)),
        P1: ((0, 1, 2),),
        P3: ((0, 3, 1),),
    },
)
OWN = tuple((0, 0, q) for q in range(4))
GATHER = (
    {
        Z: ((0, 3, 1), (0, 1, 1), (0, 1, 2), (0, 3, 2)),
        P1: ((1, 0, 0), (0, 3, 0), (1, 0, 3), (0, 3, 1)),
        P3: ((1, 0, 3), (0, 1, 3), (1, 0, 0), (0, 1, 2)),
    },
    {
        Z: ((0, 2, 1), (0, 2, 2)),
        P1: ((1, 3, 0),),
        P3: ((1, 1, 3),),
    },
)


def send(link, x):
    if link == Z:
        return lax.ppermute(x, "ends", [(0, 1), (1, 0)])
    flip = 1 if link == P1 else 3
    return lax.ppermute(x, "dp_0", [(i, i ^ flip) for i in range(4)])


def to_other_core(x):
    return lax.ppermute(x, "dp_1", [(0, 1), (1, 0)])


def rows_of(segs):
    return sum(SIZE[q] for _, _, q in segs)


def layout(segs):
    at, row = {}, 0
    for seg in segs:
        at[seg] = row
        row += SIZE[seg[2]]
    return at


def slot(de, dy, other):
    return (de * 4 + dy) * 2 + other


def row_at(table, place):
    if isinstance(place, int):
        return place
    block, q = place
    return pl.multiple_of(table[block] * 128 + START[q], 8)


class Build:
    def __init__(self):
        self.arrays, self.outs, self.work = [], [], []

    def array(self, x):
        for i, have in enumerate(self.arrays):
            if have is x:
                return i
        self.arrays.append(x)
        return len(self.arrays) - 1

    def out(self, rows, dtype=jnp.bfloat16):
        self.outs.append((rows, dtype))
        return len(self.outs) - 1

    def piece(self, out, place, rows, sources):
        self.work.append((out, place, rows, [(self.array(x), at) for x, at in sources]))

    def run(self, table, into=None, squares=False):
        width = self.arrays[0].shape[-1]
        work, n_in, n_out = self.work, len(self.arrays), len(self.outs)
        loads = []
        for out, place, rows, sources in work:
            if len(sources) > 1 or squares:
                loads.extend((x, at, rows) for x, at in sources)
        sums = [w for w in work if len(w[3]) > 1 or squares]
        deepest = max([w[2] for w in work])

        def kernel(table_ref, *refs):
            ins, refs = refs[:n_in], refs[n_in:]
            if into is not None:
                refs = refs[1:]
            outs, refs = refs[:n_out], refs[n_out:]
            if squares:
                square_ref, refs = refs[0], refs[1:]
            (in_buf, in_sem, out_sem), bufs = refs[:3], refs[3:]

            def load(k):
                x, at, rows = loads[k]
                return pltpu.make_async_copy(
                    ins[x].at[pl.ds(row_at(table_ref, at), rows)],
                    in_buf.at[k, pl.ds(0, rows)],
                    in_sem.at[k],
                )

            for k in range(len(loads)):
                load(k).start()
            started, k, s = [], 0, 0
            total = None
            for w, (out, place, rows, sources) in enumerate(work):
                target = outs[out].at[pl.ds(row_at(table_ref, place), rows)]
                if len(sources) == 1 and not squares:
                    x, at = sources[0]
                    copy = pltpu.make_async_copy(
                        ins[x].at[pl.ds(row_at(table_ref, at), rows)], target, out_sem.at[w]
                    )
                    copy.start()
                    started.append(copy)
            for w, (out, place, rows, sources) in enumerate(work):
                if len(sources) == 1 and not squares:
                    continue
                target = outs[out].at[pl.ds(row_at(table_ref, place), rows)]
                acc = None
                for _ in sources:
                    load(k).wait()
                    term = in_buf[k, pl.ds(0, rows)].astype(jnp.float32)
                    acc = term if acc is None else acc + term
                    k += 1
                if squares:
                    part = jnp.sum((acc * acc).reshape(rows // 8, 8, width // 128, 128), axis=(0, 2))
                    total = part if total is None else total + part
                bufs[0][s, pl.ds(0, rows)] = acc.astype(bufs[0].dtype)
                copy = pltpu.make_async_copy(bufs[0].at[s, pl.ds(0, rows)], target, out_sem.at[w])
                copy.start()
                started.append(copy)
                s += 1
            if squares:
                square_ref[...] = total
            for copy in started:
                copy.wait()

        out_dtype = self.outs[0][1]
        out_shape = [jax.ShapeDtypeStruct((rows, width), dtype) for rows, dtype in self.outs]
        out_specs = [pl.BlockSpec(memory_space=pl.ANY)] * n_out
        if squares:
            out_shape.append(jax.ShapeDtypeStruct((8, 128), jnp.float32))
            out_specs.append(pl.BlockSpec(memory_space=pltpu.VMEM))
        scratch = [
            pltpu.VMEM((max(len(loads), 1), deepest if loads else 8, width), jnp.bfloat16),
            pltpu.SemaphoreType.DMA((max(len(loads), 1),)),
            pltpu.SemaphoreType.DMA((len(work),)),
        ]
        if sums:
            scratch.append(pltpu.VMEM((len(sums), deepest, width), out_dtype))
        moved = sum((len(w[3]) + 1) * w[2] for w in work) * width * 2
        extra = [] if into is None else [into]
        return pl.pallas_call(
            kernel,
            out_shape=out_shape,
            in_specs=[pl.BlockSpec(memory_space=pltpu.SMEM)]
            + [pl.BlockSpec(memory_space=pl.ANY)] * (n_in + len(extra)),
            out_specs=out_specs,
            scratch_shapes=scratch,
            input_output_aliases={} if into is None else {1 + n_in: 0},
            compiler_params=pltpu.CompilerParams(vmem_limit_bytes=40 * 2**20),
            cost_estimate=pl.CostEstimate(flops=0, bytes_accessed=moved, transcendentals=0),
        )(table, *self.arrays, *extra)


def reduce_rows(grad, table):
    plans = [{link: segs for link, segs in r.items()} for r in REDUCE]
    groups = [[seg for segs in plan.values() for seg in segs] for plan in plans[:2]]
    groups.append([seg for segs in plans[2].values() for seg in segs] + list(OWN))

    held = {}
    for group in groups:
        at = layout(group)
        build = Build()
        out = build.out(rows_of(group))
        for de, dy, q in group:
            build.piece(out, at[de, dy, q], SIZE[q], [(grad, (slot(de, dy, 1), q))])
        got = to_other_core(build.run(table)[0])
        for de, dy, q in group:
            held[de, dy, q] = [(grad, (slot(de, dy, 0), q)), (got, at[de, dy, q])]

    for plan in plans:
        build = Build()
        for link, segs in plan.items():
            at = layout(segs)
            out = build.out(rows_of(segs))
            for seg in segs:
                build.piece(out, at[seg], SIZE[seg[2]], held[seg])
        for (link, segs), x in zip(plan.items(), build.run(table)):
            at = layout(segs)
            got = send(link, x)
            for seg in segs:
                held[over(link, seg)].append((got, at[seg]))

    build = Build()
    out = build.out(128, jnp.float32)
    for seg in OWN:
        build.piece(out, START[seg[2]], SIZE[seg[2]], held[seg])
    return build.run(table, squares=True)


def gather_rows(own, table):
    held = {seg: (own, START[seg[2]]) for seg in OWN}
    out = None
    fresh = [(own, START, OWN)]
    for plan in ({link: OWN for link in (Z, P1, P3)},) + GATHER:
        if plan.keys() and all(segs == OWN for segs in plan.values()):
            messages = [own] * len(plan)
        else:
            build = Build()
            for link, segs in plan.items():
                at = layout(segs)
                to = build.out(rows_of(segs))
                for seg in segs:
                    build.piece(to, at[seg], SIZE[seg[2]], [held[seg]])
            messages = build.run(table)
        for (link, segs), x in zip(plan.items(), messages):
            at = layout(segs)
            got = send(link, x)
            fresh.append((got, at, tuple(segs), link))
            for seg in segs:
                held[over(link, seg)] = (got, at[seg])
        build = Build()
        build.out(2048)
        for x, at, segs, *link in fresh:
            other = to_other_core(x)
            for seg in segs:
                row = at[seg[2]] if not link else at[seg]
                de, dy, q = over(link[0], seg) if link else seg
                build.piece(0, (slot(de, dy, 0), q), SIZE[q], [(x, row)])
                build.piece(0, (slot(de, dy, 1), q), SIZE[q], [(other, row)])
        out = build.run(table, into=out)[0]
        fresh = []
    return out


def total_over_all(x):
    x = x + lax.ppermute(x, "dp_1", [(0, 1), (1, 0)])
    for axes in ("dp_0", "tp_1", ("ends", "tp_0")):
        for flip in (1, 3):
            x = x + lax.ppermute(x, axes, [(i, i ^ flip) for i in range(4)])
    return jnp.sum(x)


def per_device(grad, master, moment, second):
    rows_tp = grad.shape[2]
    width = grad.shape[3]
    e, y, c = (lax.axis_index(a) for a in ENDS_DP)
    table = jnp.stack(
        [
            ((e ^ de) * 4 + (y ^ dy)) * 2 + (c ^ other)
            for de in range(2)
            for dy in range(4)
            for other in range(2)
        ]
    ).astype(jnp.int32)
    summed, parts = reduce_rows(grad.reshape(rows_tp, width), table)
    squares = total_over_all(parts)
    vocab_total = rows_tp * lax.axis_size(TP)
    factor = jnp.minimum(
        jnp.float32(1.0), jnp.sqrt(jnp.float32(vocab_total * width)) / (jnp.sqrt(squares) + 1e-06)
    )
    clipped = factor * summed
    moment_out = 0.9 * moment[0] + 0.1 * clipped
    second_out = 0.999 * second[0] + 0.001 * clipped * clipped
    update = moment_out / (1.0 - 0.9**STEP) / (jnp.sqrt(second_out / (1.0 - 0.999**STEP)) + 1e-08)
    master_out = master[0] - 0.01 * (update + 0.1 * master[0])
    weights = gather_rows(master_out.astype(jnp.bfloat16), table)
    return (weights, master_out[None], moment_out[None], second_out[None])


def solution(mesh):
    finer = Mesh(
        mesh.devices.reshape(mesh.shape["ends"], 4, 2, 2, 4),
        ("ends", "dp_0", "dp_1", "tp_0", "tp_1"),
    )
    return jax.shard_map(
        per_device,
        mesh=finer,
        in_specs=(
            P("ends", DP, TP, None),
            P(TP, ENDS_DP, None),
            P(TP, ENDS_DP, None),
            P(TP, ENDS_DP, None),
        ),
        out_specs=(P(TP, None), P(TP, ENDS_DP, None), P(TP, ENDS_DP, None), P(TP, ENDS_DP, None)),
        check_vma=False,
    )
```

time: 288 us -> 190 us (0.66)
  waiting for transfers between devices: 219 us -> 62 us
  starting transfers between devices: 0.08 us -> 64.6 us
  Pallas kernels: 0 us -> 50.9 us
  blocking collectives: 35 us -> 0 us
  between operations: 14.8 us -> 1.76 us
  local copies, waits for them, and re-layouts: 10.5 us -> 4.67 us
    reduce_scatter x1 -> x0, waiting for transfers between devices: 129 us -> none  [per_device(): lax.psum_scatter(local.astype(jnp.bfloat16), ENDS_DP, scatter_dimension=0...]
    all_gather x1 -> x0, waiting for transfers between devices: 89.3 us -> none  [per_device(): weights = lax.all_gather(rounded, ENDS_DP, axis=0, tiled=True)]
    ppermute x0 -> x38, starting transfers between devices: none -> 64.6 us  [the longest x13 27.6 us: to_other_core(): return lax.ppermute(x, 'dp_1', [(0, 1), (1, 0)])]
    ppermute x0 -> x38, waiting for transfers between devices: none -> 62 us  [the longest x12 31.3 us: send(): return lax.ppermute(x, 'dp_0', [(i, i ^ flip) for i in range(4)])]
    pallas_call x0 -> x12, Pallas kernels: none -> 50.9 us  [run(): pl.pallas_call(kernel, out_shape=out_shape, in_specs=[pl.BlockSpec(memory...]
    psum x5 -> x0, blocking collectives: 35 us -> none  [one_axis_at_a_time(): x = lax.psum(x, axis)]
    unnamed x5 -> x4, local copies, waits for them, and re-layouts: 10.5 us -> 4.58 us
  transfers between devices with their start and end apart: 2 -> 38, of which waited for: 2 -> 20; matrix products, arithmetic and copies ran while one was open for 0% -> 0% of each run, Pallas kernels for 0% -> 16%
where the time goes in v1:
time: 190 us; the launch traced here: 189 us
  starting transfers between devices  64.6 us (34%)
  waiting for transfers between devices  62 us (33%)
  Pallas kernels  50.9 us (27%)
  other arithmetic  5.54 us (3%)
  local copies, waits for them, and re-layouts  4.67 us (2%)
    pallas_call x12, Pallas kernels, run(): pl.pallas_call(kernel, out_shape=out_shape, in_specs=[pl.BlockSpec(memory...  50.9 us
    ppermute x12, waiting for transfers between devices, send(): return lax.ppermute(x, 'dp_0', [(i, i ^ flip) for i in range(4)])  31.3 us
    ppermute x13, starting transfers between devices, to_other_core(): return lax.ppermute(x, 'dp_1', [(0, 1), (1, 0)])  27.6 us
    ppermute x6, waiting for transfers between devices, send(): return lax.ppermute(x, 'ends', [(0, 1), (1, 0)])  18.4 us
    ppermute x6, starting transfers between devices, send(): return lax.ppermute(x, 'ends', [(0, 1), (1, 0)])  12.4 us
    ppermute x12, starting transfers between devices, send(): return lax.ppermute(x, 'dp_0', [(i, i ^ flip) for i in range(4)])  11.7 us
    ppermute x6, waiting for transfers between devices, total_over_all(): x = x + lax.ppermute(x, axes, [(i, i ^ flip) for i in range(4)])  9.73 us
    ppermute x6, starting transfers between devices, total_over_all(): x = x + lax.ppermute(x, axes, [(i, i ^ flip) for i in range(4)])  8.65 us
  transfers between devices with their start and end apart: 38, of which 20 were waited for; matrix products, arithmetic and copies ran while one was open for 0% of the time, Pallas kernels for 16%

profile of v1, /device:TPU:1, one launch (start us, length us, event | category | flops | bytes accessed | tf_op | source)
XLA Modules:
  0.0 189.4 jit_solution(9440448828579301511)
XLA Ops:
  0.8 2.4 %shard_map.76 = bf16[384,3072]{1,0:T(8,128)(2,1)S(1)} custom-call(s32[16]{0:T(128)S(1)} %stack.67.table_ref, bf16[2048,3072]{1,0:T(8,128)(2,1)} %bitcast.46), custom_call_target="tpu_custom_call" | custom-call | bytes 4718592 | tf_op jit(solution)/shard_map/pallas_call | solution.py:190
  4.6 2.4 %shard_map.78 = bf16[384,3072]{1,0:T(8,128)(2,1)S(1)} custom-call(s32[16]{0:T(128)S(1)} %stack.67.table_ref, bf16[2048,3072]{1,0:T(8,128)(2,1)} %bitcast.47), custom_call_target="tpu_custom_call" | custom-call | bytes 4718592 | tf_op jit(solution)/shard_map/pallas_call | solution.py:190
  8.8 7.7 %shard_map.77 = (bf16[128,3072]{1,0:T(8,128)(2,1)S(1)}, bf16[128,3072]{1,0:T(8,128)(2,1)S(1)}, bf16[128,3072]{1,0:T(8,128)(2,1)S(1)}) custom-call(s32[16]{0:T(128)S(1)} %stack.67.table_ref, bf16[2048,3072]{1,0:T(8,128)(2,1)} %bitcast.48, bf16[384,3072]{1,0:T(8,128)(2,1)S(1)} %collective-permute-done.1.refs_1_), custom_call_target="tpu_custom_call" | custom-call | bytes 7077888 | tf_op jit(solution)/shard_map/pallas_call | solution.py:190
  17.9 1.9 %collective-permute-start.4 = (bf16[128,3072]{1,0:T(8,128)(2,1)S(1)}, bf16[128,3072]{1,0:T(8,128)(2,1)S(1)}, u32[]{:S(2)}, u32[]{:S(2)}) collective-permute-start(bf16[128,3072]{1,0:T(8,128)(2,1)S(1)} %get-tuple-element.22), channel_id=1, source_target_pairs={{0,48},{16,32},{32,16},{48,0},{1,49},{17,33},{33,17},{49,1},{2,50}... | collective-permute-start | bytes 2359304 | tf_op jit(solution)/shard_map/ppermute | solution.py:64
  19.8 3.6 %collective-permute-start.5 = (bf16[128,3072]{1,0:T(8,128)(2,1)S(1)}, bf16[128,3072]{1,0:T(8,128)(2,1)S(1)}, u32[]{:S(2)}, u32[]{:S(2)}) collective-permute-start(bf16[128,3072]{1,0:T(8,128)(2,1)S(1)} %get-tuple-element.23), channel_id=1, source_target_pairs={{0,64},{64,0},{1,65},{65,1},{2,66},{66,2},{3,67},{67,3},{4,68},{68... | collective-permute-start | bytes 2359304 | tf_op jit(solution)/shard_map/ppermute | solution.py:62
  23.4 4.6 %copy-done = bf16[1,1,2048,3072]{3,2,1,0:T(8,128)(2,1)S(1)} copy-done((bf16[1,1,2048,3072]{3,2,1,0:T(8,128)(2,1)S(1)}, bf16[1,1,2048,3072]{3,2,1,0:T(8,128)(2,1)}, u32[]{:S(2)}) %copy-start) | copy-done | bytes 12582936
  28.0 2.7 %shard_map.75 = bf16[256,3072]{1,0:T(8,128)(2,1)S(1)} custom-call(s32[16]{0:T(128)S(1)} %stack.67.table_ref, bf16[2048,3072]{1,0:T(8,128)(2,1)S(1)} %bitcast.52), custom_call_target="tpu_custom_call" | custom-call | bytes 3145728 | tf_op jit(solution)/shard_map/pallas_call | solution.py:190
  32.0 3.3 %collective-permute-done.2.refs_4_.refs_2_ = bf16[128,3072]{1,0:T(8,128)(2,1)S(1)} collective-permute-done((bf16[128,3072]{1,0:T(8,128)(2,1)S(1)}, bf16[128,3072]{1,0:T(8,128)(2,1)S(1)}, u32[]{:S(2)}, u32[]{:S(2)}) %collective-permute-start.2) | collective-permute-done | bytes 786464 | tf_op jit(solution)/shard_map/ppermute | solution.py:64
  35.3 2.3 %collective-permute-done.4.refs_2_.refs_4_.refs_9_ = bf16[128,3072]{1,0:T(8,128)(2,1)S(1)} collective-permute-done((bf16[128,3072]{1,0:T(8,128)(2,1)S(1)}, bf16[128,3072]{1,0:T(8,128)(2,1)S(1)}, u32[]{:S(2)}, u32[]{:S(2)}) %collective-permute-start.4) | collective-permute-done | bytes 786464 | tf_op jit(solution)/shard_map/ppermute | solution.py:64
  37.6 2.8 %collective-permute-done.5.refs_3_ = bf16[128,3072]{1,0:T(8,128)(2,1)S(1)} collective-permute-done((bf16[128,3072]{1,0:T(8,128)(2,1)S(1)}, bf16[128,3072]{1,0:T(8,128)(2,1)S(1)}, u32[]{:S(2)}, u32[]{:S(2)}) %collective-permute-start.5) | collective-permute-done | bytes 786464 | tf_op jit(solution)/shard_map/ppermute | solution.py:62
  40.4 10.2 %shard_map.79 = (bf16[128,3072]{1,0:T(8,128)(2,1)S(1)}, bf16[128,3072]{1,0:T(8,128)(2,1)S(1)}, bf16[128,3072]{1,0:T(8,128)(2,1)S(1)}) custom-call(s32[16]{0:T(128)S(1)} %stack.67.table_ref, bf16[2048,3072]{1,0:T(8,128)(2,1)} %bitcast.49, bf16[384,3072]{1,0:T(8,128)(2,1)S(1)} %collective-permute-done.3.refs_1_, ...), custom_call_target="tpu_custom_call" | custom-call | bytes 8650752 | tf_op jit(solution)/shard_map/pallas_call | solution.py:190
  51.5 2.6 %collective-permute-start.8 = (bf16[128,3072]{1,0:T(8,128)(2,1)S(1)}, bf16[128,3072]{1,0:T(8,128)(2,1)S(1)}, u32[]{:S(2)}, u32[]{:S(2)}) collective-permute-start(bf16[128,3072]{1,0:T(8,128)(2,1)S(1)} %get-tuple-element.26), channel_id=1, source_target_pairs={{0,64},{64,0},{1,65},{65,1},{2,66},{66,2},{3,67},{67,3},{4,68},{68... | collective-permute-start | bytes 2359304 | tf_op jit(solution)/shard_map/ppermute | solution.py:62
  54.1 15.3 %collective-permute-done.6.refs_3_ = bf16[128,3072]{1,0:T(8,128)(2,1)S(1)} collective-permute-done((bf16[128,3072]{1,0:T(8,128)(2,1)S(1)}, bf16[128,3072]{1,0:T(8,128)(2,1)S(1)}, u32[]{:S(2)}, u32[]{:S(2)}) %collective-permute-start.6) | collective-permute-done | bytes 786464 | tf_op jit(solution)/shard_map/ppermute | solution.py:64
  70.2 5.4 %shard_map.80 = (bf16[64,3072]{1,0:T(8,128)(2,1)S(1)}, bf16[32,3072]{1,0:T(8,128)(2,1)S(1)}, bf16[32,3072]{1,0:T(8,128)(2,1)S(1)}) custom-call(s32[16]{0:T(128)S(1)} %stack.67.table_ref, bf16[2048,3072]{1,0:T(8,128)(2,1)} %bitcast.50, bf16[256,3072]{1,0:T(8,128)(2,1)S(1)} %collective-permute-done.refs_1_, ...), custom_call_target="tpu_custom_call" | custom-call | bytes 3932160 | tf_op jit(solution)/shard_map/pallas_call | solution.py:190
  75.6 2.4 %collective-permute-start.9 = (bf16[64,3072]{1,0:T(8,128)(2,1)S(1)}, bf16[64,3072]{1,0:T(8,128)(2,1)S(1)}, u32[]{:S(2)}, u32[]{:S(2)}) collective-permute-start(bf16[64,3072]{1,0:T(8,128)(2,1)S(1)} %get-tuple-element.27), channel_id=1, source_target_pairs={{0,64},{64,0},{1,65},{65,1},{2,66},{66,2},{3,67},{67,3},{4,68},{68... | collective-permute-start | bytes 1179656 | tf_op jit(solution)/shard_map/ppermute | solution.py:62
  80.5 3.5 %collective-permute-done.10.refs_7_ = bf16[32,3072]{1,0:T(8,128)(2,1)S(1)} collective-permute-done((bf16[32,3072]{1,0:T(8,128)(2,1)S(1)}, bf16[32,3072]{1,0:T(8,128)(2,1)S(1)}, u32[]{:S(2)}, u32[]{:S(2)}) %collective-permute-start.10) | collective-permute-done | bytes 196640 | tf_op jit(solution)/shard_map/ppermute | solution.py:64
  85.1 6.8 %shard_map.81 = (f32[128,3072]{1,0:T(8,128)S(1)}, f32[8,128]{1,0:T(8,128)S(1)}) custom-call(s32[16]{0:T(128)S(1)} %stack.67.table_ref, bf16[2048,3072]{1,0:T(8,128)(2,1)} %bitcast.51, bf16[256,3072]{1,0:T(8,128)(2,1)S(1)} %collective-permute-done.refs_1_, bf16[128,3072]{1,0:T(8,128)(2,1)S(1)} %collective-permute-done.2.refs_4_.refs_2_, ...), custom_call_target="tpu_custom_call" | custom-call | bytes 4718592 | tf_op jit(solution)/shard_map/pallas_call | solution.py:190
  91.9 4.2 %collective-permute-start.12 = (f32[8,128]{1,0:T(8,128)S(1)}, f32[8,128]{1,0:T(8,128)S(1)}, u32[]{:S(2)}, u32[]{:S(2)}) collective-permute-start(f32[8,128]{1,0:T(8,128)S(1)} %get-tuple-element.30), channel_id=1, source_target_pairs={{0,8},{8,0},{1,9},{9,1},{2,10},{10,2},{3,11},{11,3},{4,12},{12,4},... | collective-permute-start | bytes 12296 | tf_op jit(solution)/shard_map/ppermute | solution.py:275
  100.7 2.3 %collective-permute-done.14 = f32[8,128]{1,0:T(8,128)S(1)} collective-permute-done((f32[8,128]{1,0:T(8,128)S(1)}, f32[8,128]{1,0:T(8,128)S(1)}, u32[]{:S(2)}, u32[]{:S(2)}) %collective-permute-start.14) | collective-permute-done | bytes 4128 | tf_op jit(solution)/shard_map/ppermute | solution.py:278
  105.5 2.5 %collective-permute-start.16 = (f32[8,128]{1,0:T(8,128)S(1)}, f32[8,128]{1,0:T(8,128)S(1)}, u32[]{:S(2)}, u32[]{:S(2)}) collective-permute-start(f32[8,128]{1,0:T(8,128)S(1)} %add.146), channel_id=1, source_target_pairs={{0,3},{1,2},{2,1},{3,0},{4,7},{5,6},{6,5},{7,4},{8,11},{9,10},{10,... | collective-permute-start | bytes 12296 | tf_op jit(solution)/shard_map/ppermute | solution.py:278
  111.6 2.0 %collective-permute-start.18 = (f32[8,128]{1,0:T(8,128)S(1)}, f32[8,128]{1,0:T(8,128)S(1)}, u32[]{:S(2)}, u32[]{:S(2)}) collective-permute-start(f32[8,128]{1,0:T(8,128)S(1)} %add.148), channel_id=1, source_target_pairs={{0,68},{4,64},{64,4},{68,0},{1,69},{5,65},{65,5},{69,1},{2,70},{6,... | collective-permute-start | bytes 12296 | tf_op jit(solution)/shard_map/ppermute | solution.py:278
  116.6 4.9 %fusion.5 = (bf16[128,3072]{1,0:T(8,128)(2,1)S(1)}, f32[128,3072]{1,0:T(8,128)}, f32[1,128,3072]{2,1,0:T(8,128)}, f32[1,128,3072]{2,1,0:T(8,128)}) fusion(f32[1,128,3072]{2,1,0:T(8,128)S(1)} %copy-done.1, f32[128,3072]{1,0:T(8,128)S(1)} %get-tuple-element.31, f32[]{:T(128)S(6)} %min_shard_map.3, f32[1,128,3072]{2,1,0:T(8,128)} %param.6, f32[1,128,3072]{2,1,0:T(8,128)} %param.5), kind=kLoop, calls=%fused_computation.10 | loop fusion | flops 6684672 | bytes 11796484 | tf_op jit(solution)/shard_map/convert_element_type | solution.py:305
  124.1 10.8 %collective-permute-done.21.refs_2_ = bf16[128,3072]{1,0:T(8,128)(2,1)S(1)} collective-permute-done((bf16[128,3072]{1,0:T(8,128)(2,1)S(1)}, bf16[128,3072]{1,0:T(8,128)(2,1)S(1)}, u32[]{:S(2)}, u32[]{:S(2)}) %collective-permute-start.21) | collective-permute-done | bytes 786464 | tf_op jit(solution)/shard_map/ppermute | solution.py:62
  134.9 3.7 %shard_map.82 = (bf16[128,3072]{1,0:T(8,128)(2,1)S(1)}, bf16[128,3072]{1,0:T(8,128)(2,1)S(1)}, bf16[128,3072]{1,0:T(8,128)(2,1)S(1)}) custom-call(s32[16]{0:T(128)S(1)} %stack.67.table_ref, bf16[128,3072]{1,0:T(8,128)(2,1)S(1)} %collective-permute-done.19.refs_0_.refs_6_, bf16[128,3072]{1,0:T(8,128)(2,1)S(1)} %collective-permute-done.20.refs_1_.refs_4_, ...), custom_call_target="tpu_custom_call" | custom-call | bytes 4718592 | tf_op jit(solution)/shard_map/pallas_call | solution.py:190
  138.6 2.5 %collective-permute-start.30 = (bf16[128,3072]{1,0:T(8,128)(2,1)S(1)}, bf16[128,3072]{1,0:T(8,128)(2,1)S(1)}, u32[]{:S(2)}, u32[]{:S(2)}) collective-permute-start(bf16[128,3072]{1,0:T(8,128)(2,1)S(1)} %get-tuple-element.37), channel_id=1, source_target_pairs={{0,64},{64,0},{1,65},{65,1},{2,66},{66,2},{3,67},{67,3},{4,68},{68... | collective-permute-start | bytes 2359304 | tf_op jit(solution)/shard_map/ppermute | solution.py:62
  142.4 9.6 %collective-permute-start.34 = (bf16[128,3072]{1,0:T(8,128)(2,1)S(1)}, bf16[128,3072]{1,0:T(8,128)(2,1)S(1)}, u32[]{:S(2)}, u32[]{:S(2)}) collective-permute-start(bf16[128,3072]{1,0:T(8,128)(2,1)S(1)} %get-tuple-element.38.refs_0_), channel_id=1, source_target_pairs={{0,8},{8,0},{1,9},{9,1},{2,10},{10,2},{3,11},{11,3},{4,12},{12,4},... | collective-permute-start | bytes 2359304 | tf_op jit(solution)/shard_map/ppermute | solution.py:68
  152.0 8.7 %collective-permute-start.36 = (bf16[128,3072]{1,0:T(8,128)(2,1)S(1)}, bf16[128,3072]{1,0:T(8,128)(2,1)S(1)}, u32[]{:S(2)}, u32[]{:S(2)}) collective-permute-start(bf16[128,3072]{1,0:T(8,128)(2,1)S(1)} %collective-permute-done.20.refs_1_.refs_4_), channel_id=1, source_target_pairs={{0,8},{8,0},{1,9},{9,1},{2,10},{10,2},{3,11},{11,3},{4,12},{12,4},... | collective-permute-start | bytes 2359304 | tf_op jit(solution)/shard_map/ppermute | solution.py:68
  166.4 6.1 %collective-permute-done.26.refs_2_ = bf16[32,3072]{1,0:T(8,128)(2,1)S(1)} collective-permute-done((bf16[32,3072]{1,0:T(8,128)(2,1)S(1)}, bf16[32,3072]{1,0:T(8,128)(2,1)S(1)}, u32[]{:S(2)}, u32[]{:S(2)}) %collective-permute-start.26) | collective-permute-done | bytes 196640 | tf_op jit(solution)/shard_map/ppermute | solution.py:64
  174.4 3.6 %collective-permute-done.24.refs_0_ = bf16[64,3072]{1,0:T(8,128)(2,1)S(1)} collective-permute-done((bf16[64,3072]{1,0:T(8,128)(2,1)S(1)}, bf16[64,3072]{1,0:T(8,128)(2,1)S(1)}, u32[]{:S(2)}, u32[]{:S(2)}) %collective-permute-start.24) | collective-permute-done | bytes 393248 | tf_op jit(solution)/shard_map/ppermute | solution.py:62
  178.9 2.1 %collective-permute-start.27 = (bf16[32,3072]{1,0:T(8,128)(2,1)S(1)}, bf16[32,3072]{1,0:T(8,128)(2,1)S(1)}, u32[]{:S(2)}, u32[]{:S(2)}) collective-permute-start(bf16[32,3072]{1,0:T(8,128)(2,1)S(1)} %collective-permute-done.26.refs_2_), channel_id=1, source_target_pairs={{0,8},{8,0},{1,9},{9,1},{2,10},{10,2},{3,11},{11,3},{4,12},{12,4},... | collective-permute-start | bytes 589832 | tf_op jit(solution)/shard_map/ppermute | solution.py:68
  181.1 3.5 %shard_map.84.refs_6_ = bf16[2048,3072]{1,0:T(8,128)(2,1)} custom-call(s32[16]{0:T(128)S(1)} %stack.67.table_ref, bf16[128,3072]{1,0:T(8,128)(2,1)S(1)} %get-tuple-element.38.refs_0_, bf16[128,3072]{1,0:T(8,128)(2,1)S(1)} %collective-permute-done.34.refs_1_, bf16[128,3072]{1,0:T(8,128)(2,1)S(1)} %collective-permute-done.21.refs_2_, ...), custom_call_target="tpu_custom_call" | custom-call | bytes 12582912 | tf_op jit(solution)/shard_map/pallas_call | solution.py:190
  184.5 2.9 %shard_map.85.refs_6_ = bf16[2048,3072]{1,0:T(8,128)(2,1)} custom-call(s32[16]{0:T(128)S(1)} %stack.67.table_ref, bf16[128,3072]{1,0:T(8,128)(2,1)S(1)} %collective-permute-done.30.refs_0_, bf16[128,3072]{1,0:T(8,128)(2,1)S(1)} %collective-permute-done.31.refs_1_, ...), custom_call_target="tpu_custom_call", output_to_operand_aliasing={{}: (7, {})} | custom-call | bytes 9437184 | tf_op jit(solution)/shard_map/pallas_call | solution.py:190
  (69 shorter events, 38.5 us)
Async XLA Ops:
  3.1 5.7 %collective-permute-start.1 = (bf16[384,3072]{1,0:T(8,128)(2,1)S(1)}, bf16[384,3072]{1,0:T(8,128)(2,1)S(1)}, u32[]{:S(2)}, u32[]{:S(2)}) collective-permute-start(bf16[384,3072]{1,0:T(8,128)(2,1)S(1)} %shard_map.76), channel_id=1, source_target_pairs={{0,8},{8,0},{1,9},{9,1},{2,10},{10,2},{3,11},{11,3},{4,12},{12,4},... | collective-permute-start | bytes 7077896 | tf_op jit(solution)/shard_map/ppermute | solution.py:68
  7.0 25.0 %collective-permute-start.3 = (bf16[384,3072]{1,0:T(8,128)(2,1)S(1)}, bf16[384,3072]{1,0:T(8,128)(2,1)S(1)}, u32[]{:S(2)}, u32[]{:S(2)}) collective-permute-start(bf16[384,3072]{1,0:T(8,128)(2,1)S(1)} %shard_map.78), channel_id=1, source_target_pairs={{0,8},{8,0},{1,9},{9,1},{2,10},{10,2},{3,11},{11,3},{4,12},{12,4},... | collective-permute-start | bytes 7077896 | tf_op jit(solution)/shard_map/ppermute | solution.py:68
  16.5 18.8 %collective-permute-start.2 = (bf16[128,3072]{1,0:T(8,128)(2,1)S(1)}, bf16[128,3072]{1,0:T(8,128)(2,1)S(1)}, u32[]{:S(2)}, u32[]{:S(2)}) collective-permute-start(bf16[128,3072]{1,0:T(8,128)(2,1)S(1)} %get-tuple-element.21), channel_id=1, source_target_pairs={{0,16},{16,0},{32,48},{48,32},{1,17},{17,1},{33,49},{49,33},{2,18}... | collective-permute-start | bytes 2359304 | tf_op jit(solution)/shard_map/ppermute | solution.py:64
  17.9 19.6 %collective-permute-start.4 = (bf16[128,3072]{1,0:T(8,128)(2,1)S(1)}, bf16[128,3072]{1,0:T(8,128)(2,1)S(1)}, u32[]{:S(2)}, u32[]{:S(2)}) collective-permute-start(bf16[128,3072]{1,0:T(8,128)(2,1)S(1)} %get-tuple-element.22), channel_id=1, source_target_pairs={{0,48},{16,32},{32,16},{48,0},{1,49},{17,33},{33,17},{49,1},{2,50}... | collective-permute-start | bytes 2359304 | tf_op jit(solution)/shard_map/ppermute | solution.py:64
  19.8 20.6 %collective-permute-start.5 = (bf16[128,3072]{1,0:T(8,128)(2,1)S(1)}, bf16[128,3072]{1,0:T(8,128)(2,1)S(1)}, u32[]{:S(2)}, u32[]{:S(2)}) collective-permute-start(bf16[128,3072]{1,0:T(8,128)(2,1)S(1)} %get-tuple-element.23), channel_id=1, source_target_pairs={{0,64},{64,0},{1,65},{65,1},{2,66},{66,2},{3,67},{67,3},{4,68},{68... | collective-permute-start | bytes 2359304 | tf_op jit(solution)/shard_map/ppermute | solution.py:62
  30.7 23.4 %collective-permute-start = (bf16[256,3072]{1,0:T(8,128)(2,1)S(1)}, bf16[256,3072]{1,0:T(8,128)(2,1)S(1)}, u32[]{:S(2)}, u32[]{:S(2)}) collective-permute-start(bf16[256,3072]{1,0:T(8,128)(2,1)S(1)} %shard_map.75), channel_id=1, source_target_pairs={{0,8},{8,0},{1,9},{9,1},{2,10},{10,2},{3,11},{11,3},{4,12},{12,4},... | collective-permute-start | bytes 4718600 | tf_op jit(solution)/shard_map/ppermute | solution.py:68
  50.6 18.8 %collective-permute-start.6 = (bf16[128,3072]{1,0:T(8,128)(2,1)S(1)}, bf16[128,3072]{1,0:T(8,128)(2,1)S(1)}, u32[]{:S(2)}, u32[]{:S(2)}) collective-permute-start(bf16[128,3072]{1,0:T(8,128)(2,1)S(1)} %get-tuple-element.24), channel_id=1, source_target_pairs={{0,48},{16,32},{32,16},{48,0},{1,49},{17,33},{33,17},{49,1},{2,50}... | collective-permute-start | bytes 2359304 | tf_op jit(solution)/shard_map/ppermute | solution.py:64
  51.5 17.9 %collective-permute-start.7 = (bf16[128,3072]{1,0:T(8,128)(2,1)S(1)}, bf16[128,3072]{1,0:T(8,128)(2,1)S(1)}, u32[]{:S(2)}, u32[]{:S(2)}) collective-permute-start(bf16[128,3072]{1,0:T(8,128)(2,1)S(1)} %get-tuple-element.25), channel_id=1, source_target_pairs={{0,16},{16,0},{32,48},{48,32},{1,17},{17,1},{33,49},{49,33},{2,18}... | collective-permute-start | bytes 2359304 | tf_op jit(solution)/shard_map/ppermute | solution.py:64
  51.5 18.7 %collective-permute-start.8 = (bf16[128,3072]{1,0:T(8,128)(2,1)S(1)}, bf16[128,3072]{1,0:T(8,128)(2,1)S(1)}, u32[]{:S(2)}, u32[]{:S(2)}) collective-permute-start(bf16[128,3072]{1,0:T(8,128)(2,1)S(1)} %get-tuple-element.26), channel_id=1, source_target_pairs={{0,64},{64,0},{1,65},{65,1},{2,66},{66,2},{3,67},{67,3},{4,68},{68... | collective-permute-start | bytes 2359304 | tf_op jit(solution)/shard_map/ppermute | solution.py:62
  75.6 9.5 %collective-permute-start.9 = (bf16[64,3072]{1,0:T(8,128)(2,1)S(1)}, bf16[64,3072]{1,0:T(8,128)(2,1)S(1)}, u32[]{:S(2)}, u32[]{:S(2)}) collective-permute-start(bf16[64,3072]{1,0:T(8,128)(2,1)S(1)} %get-tuple-element.27), channel_id=1, source_target_pairs={{0,64},{64,0},{1,65},{65,1},{2,66},{66,2},{3,67},{67,3},{4,68},{68... | collective-permute-start | bytes 1179656 | tf_op jit(solution)/shard_map/ppermute | solution.py:62
  78.0 6.0 %collective-permute-start.10 = (bf16[32,3072]{1,0:T(8,128)(2,1)S(1)}, bf16[32,3072]{1,0:T(8,128)(2,1)S(1)}, u32[]{:S(2)}, u32[]{:S(2)}) collective-permute-start(bf16[32,3072]{1,0:T(8,128)(2,1)S(1)} %get-tuple-element.28), channel_id=1, source_target_pairs={{0,48},{16,32},{32,16},{48,0},{1,49},{17,33},{33,17},{49,1},{2,50}... | collective-permute-start | bytes 589832 | tf_op jit(solution)/shard_map/ppermute | solution.py:64
  79.9 4.8 %collective-permute-start.11 = (bf16[32,3072]{1,0:T(8,128)(2,1)S(1)}, bf16[32,3072]{1,0:T(8,128)(2,1)S(1)}, u32[]{:S(2)}, u32[]{:S(2)}) collective-permute-start(bf16[32,3072]{1,0:T(8,128)(2,1)S(1)} %get-tuple-element.29), channel_id=1, source_target_pairs={{0,16},{16,0},{32,48},{48,32},{1,17},{17,1},{33,49},{49,33},{2,18}... | collective-permute-start | bytes 589832 | tf_op jit(solution)/shard_map/ppermute | solution.py:64
  91.9 5.0 %collective-permute-start.12 = (f32[8,128]{1,0:T(8,128)S(1)}, f32[8,128]{1,0:T(8,128)S(1)}, u32[]{:S(2)}, u32[]{:S(2)}) collective-permute-start(f32[8,128]{1,0:T(8,128)S(1)} %get-tuple-element.30), channel_id=1, source_target_pairs={{0,8},{8,0},{1,9},{9,1},{2,10},{10,2},{3,11},{11,3},{4,12},{12,4},... | collective-permute-start | bytes 12296 | tf_op jit(solution)/shard_map/ppermute | solution.py:275
  121.6 13.3 %collective-permute-start.21 = (bf16[128,3072]{1,0:T(8,128)(2,1)S(1)}, bf16[128,3072]{1,0:T(8,128)(2,1)S(1)}, u32[]{:S(2)}, u32[]{:S(2)}) collective-permute-start(bf16[128,3072]{1,0:T(8,128)(2,1)S(1)} %get-tuple-element.38.refs_0_), channel_id=1, source_target_pairs={{0,64},{64,0},{1,65},{65,1},{2,66},{66,2},{3,67},{67,3},{4,68},{68... | collective-permute-start | bytes 2359304 | tf_op jit(solution)/shard_map/ppermute | solution.py:62
  122.2 12.7 %collective-permute-start.20 = (bf16[128,3072]{1,0:T(8,128)(2,1)S(1)}, bf16[128,3072]{1,0:T(8,128)(2,1)S(1)}, u32[]{:S(2)}, u32[]{:S(2)}) collective-permute-start(bf16[128,3072]{1,0:T(8,128)(2,1)S(1)} %get-tuple-element.38.refs_0_), channel_id=1, source_target_pairs={{0,16},{16,0},{32,48},{48,32},{1,17},{17,1},{33,49},{49,33},{2,18}... | collective-permute-start | bytes 2359304 | tf_op jit(solution)/shard_map/ppermute | solution.py:64
  122.2 12.7 %collective-permute-start.19 = (bf16[128,3072]{1,0:T(8,128)(2,1)S(1)}, bf16[128,3072]{1,0:T(8,128)(2,1)S(1)}, u32[]{:S(2)}, u32[]{:S(2)}) collective-permute-start(bf16[128,3072]{1,0:T(8,128)(2,1)S(1)} %get-tuple-element.38.refs_0_), channel_id=1, source_target_pairs={{0,48},{16,32},{32,16},{48,0},{1,49},{17,33},{33,17},{49,1},{2,50}... | collective-permute-start | bytes 2359304 | tf_op jit(solution)/shard_map/ppermute | solution.py:64
  138.6 13.4 %collective-permute-start.30 = (bf16[128,3072]{1,0:T(8,128)(2,1)S(1)}, bf16[128,3072]{1,0:T(8,128)(2,1)S(1)}, u32[]{:S(2)}, u32[]{:S(2)}) collective-permute-start(bf16[128,3072]{1,0:T(8,128)(2,1)S(1)} %get-tuple-element.37), channel_id=1, source_target_pairs={{0,64},{64,0},{1,65},{65,1},{2,66},{66,2},{3,67},{67,3},{4,68},{68... | collective-permute-start | bytes 2359304 | tf_op jit(solution)/shard_map/ppermute | solution.py:62
  141.1 19.6 %collective-permute-start.22 = (bf16[128,3072]{1,0:T(8,128)(2,1)S(1)}, bf16[128,3072]{1,0:T(8,128)(2,1)S(1)}, u32[]{:S(2)}, u32[]{:S(2)}) collective-permute-start(bf16[128,3072]{1,0:T(8,128)(2,1)S(1)} %get-tuple-element.32), channel_id=1, source_target_pairs={{0,16},{16,0},{32,48},{48,32},{1,17},{17,1},{33,49},{49,33},{2,18}... | collective-permute-start | bytes 2359304 | tf_op jit(solution)/shard_map/ppermute | solution.py:64
  141.1 20.7 %collective-permute-start.23 = (bf16[128,3072]{1,0:T(8,128)(2,1)S(1)}, bf16[128,3072]{1,0:T(8,128)(2,1)S(1)}, u32[]{:S(2)}, u32[]{:S(2)}) collective-permute-start(bf16[128,3072]{1,0:T(8,128)(2,1)S(1)} %get-tuple-element.33), channel_id=1, source_target_pairs={{0,48},{16,32},{32,16},{48,0},{1,49},{17,33},{33,17},{49,1},{2,50}... | collective-permute-start | bytes 2359304 | tf_op jit(solution)/shard_map/ppermute | solution.py:64
  142.4 22.7 %collective-permute-start.34 = (bf16[128,3072]{1,0:T(8,128)(2,1)S(1)}, bf16[128,3072]{1,0:T(8,128)(2,1)S(1)}, u32[]{:S(2)}, u32[]{:S(2)}) collective-permute-start(bf16[128,3072]{1,0:T(8,128)(2,1)S(1)} %get-tuple-element.38.refs_0_), channel_id=1, source_target_pairs={{0,8},{8,0},{1,9},{9,1},{2,10},{10,2},{3,11},{11,3},{4,12},{12,4},... | collective-permute-start | bytes 2359304 | tf_op jit(solution)/shard_map/ppermute | solution.py:68
  152.0 13.3 %collective-permute-start.35 = (bf16[128,3072]{1,0:T(8,128)(2,1)S(1)}, bf16[128,3072]{1,0:T(8,128)(2,1)S(1)}, u32[]{:S(2)}, u32[]{:S(2)}) collective-permute-start(bf16[128,3072]{1,0:T(8,128)(2,1)S(1)} %collective-permute-done.21.refs_2_), channel_id=1, source_target_pairs={{0,8},{8,0},{1,9},{9,1},{2,10},{10,2},{3,11},{11,3},{4,12},{12,4},... | collective-permute-start | bytes 2359304 | tf_op jit(solution)/shard_map/ppermute | solution.py:68
  152.0 13.8 %collective-permute-start.36 = (bf16[128,3072]{1,0:T(8,128)(2,1)S(1)}, bf16[128,3072]{1,0:T(8,128)(2,1)S(1)}, u32[]{:S(2)}, u32[]{:S(2)}) collective-permute-start(bf16[128,3072]{1,0:T(8,128)(2,1)S(1)} %collective-permute-done.20.refs_1_.refs_4_), channel_id=1, source_target_pairs={{0,8},{8,0},{1,9},{9,1},{2,10},{10,2},{3,11},{11,3},{4,12},{12,4},... | collective-permute-start | bytes 2359304 | tf_op jit(solution)/shard_map/ppermute | solution.py:68
  160.7 5.7 %collective-permute-start.37 = (bf16[128,3072]{1,0:T(8,128)(2,1)S(1)}, bf16[128,3072]{1,0:T(8,128)(2,1)S(1)}, u32[]{:S(2)}, u32[]{:S(2)}) collective-permute-start(bf16[128,3072]{1,0:T(8,128)(2,1)S(1)} %collective-permute-done.19.refs_0_.refs_6_), channel_id=1, source_target_pairs={{0,8},{8,0},{1,9},{9,1},{2,10},{10,2},{3,11},{11,3},{4,12},{12,4},... | collective-permute-start | bytes 2359304 | tf_op jit(solution)/shard_map/ppermute | solution.py:68
  161.8 19.3 %collective-permute-start.31 = (bf16[128,3072]{1,0:T(8,128)(2,1)S(1)}, bf16[128,3072]{1,0:T(8,128)(2,1)S(1)}, u32[]{:S(2)}, u32[]{:S(2)}) collective-permute-start(bf16[128,3072]{1,0:T(8,128)(2,1)S(1)} %collective-permute-done.30.refs_0_), channel_id=1, source_target_pairs={{0,8},{8,0},{1,9},{9,1},{2,10},{10,2},{3,11},{11,3},{4,12},{12,4},... | collective-permute-start | bytes 2359304 | tf_op jit(solution)/shard_map/ppermute | solution.py:68
  165.1 19.4 %collective-permute-start.32 = (bf16[128,3072]{1,0:T(8,128)(2,1)S(1)}, bf16[128,3072]{1,0:T(8,128)(2,1)S(1)}, u32[]{:S(2)}, u32[]{:S(2)}) collective-permute-start(bf16[128,3072]{1,0:T(8,128)(2,1)S(1)} %collective-permute-done.22.refs_0_.refs_2_), channel_id=1, source_target_pairs={{0,8},{8,0},{1,9},{9,1},{2,10},{10,2},{3,11},{11,3},{4,12},{12,4},... | collective-permute-start | bytes 2359304 | tf_op jit(solution)/shard_map/ppermute | solution.py:68
  165.2 19.3 %collective-permute-start.33 = (bf16[128,3072]{1,0:T(8,128)(2,1)S(1)}, bf16[128,3072]{1,0:T(8,128)(2,1)S(1)}, u32[]{:S(2)}, u32[]{:S(2)}) collective-permute-start(bf16[128,3072]{1,0:T(8,128)(2,1)S(1)} %collective-permute-done.23.refs_1_.refs_4_), channel_id=1, source_target_pairs={{0,8},{8,0},{1,9},{9,1},{2,10},{10,2},{3,11},{11,3},{4,12},{12,4},... | collective-permute-start | bytes 2359304 | tf_op jit(solution)/shard_map/ppermute | solution.py:68
  165.7 12.2 %collective-permute-start.24 = (bf16[64,3072]{1,0:T(8,128)(2,1)S(1)}, bf16[64,3072]{1,0:T(8,128)(2,1)S(1)}, u32[]{:S(2)}, u32[]{:S(2)}) collective-permute-start(bf16[64,3072]{1,0:T(8,128)(2,1)S(1)} %get-tuple-element.34), channel_id=1, source_target_pairs={{0,64},{64,0},{1,65},{65,1},{2,66},{66,2},{3,67},{67,3},{4,68},{68... | collective-permute-start | bytes 1179656 | tf_op jit(solution)/shard_map/ppermute | solution.py:62
  166.4 6.1 %collective-permute-start.26 = (bf16[32,3072]{1,0:T(8,128)(2,1)S(1)}, bf16[32,3072]{1,0:T(8,128)(2,1)S(1)}, u32[]{:S(2)}, u32[]{:S(2)}) collective-permute-start(bf16[32,3072]{1,0:T(8,128)(2,1)S(1)} %get-tuple-element.35), channel_id=1, source_target_pairs={{0,16},{16,0},{32,48},{48,32},{1,17},{17,1},{33,49},{49,33},{2,18}... | collective-permute-start | bytes 589832 | tf_op jit(solution)/shard_map/ppermute | solution.py:64
  172.5 6.4 %collective-permute-start.28 = (bf16[32,3072]{1,0:T(8,128)(2,1)S(1)}, bf16[32,3072]{1,0:T(8,128)(2,1)S(1)}, u32[]{:S(2)}, u32[]{:S(2)}) collective-permute-start(bf16[32,3072]{1,0:T(8,128)(2,1)S(1)} %get-tuple-element.36), channel_id=1, source_target_pairs={{0,48},{16,32},{32,16},{48,0},{1,49},{17,33},{33,17},{49,1},{2,50}... | collective-permute-start | bytes 589832 | tf_op jit(solution)/shard_map/ppermute | solution.py:64
  177.9 9.6 %collective-permute-start.25 = (bf16[64,3072]{1,0:T(8,128)(2,1)S(1)}, bf16[64,3072]{1,0:T(8,128)(2,1)S(1)}, u32[]{:S(2)}, u32[]{:S(2)}) collective-permute-start(bf16[64,3072]{1,0:T(8,128)(2,1)S(1)} %collective-permute-done.24.refs_0_), channel_id=1, source_target_pairs={{0,8},{8,0},{1,9},{9,1},{2,10},{10,2},{3,11},{11,3},{4,12},{12,4},... | collective-permute-start | bytes 1179656 | tf_op jit(solution)/shard_map/ppermute | solution.py:68
  178.9 8.5 %collective-permute-start.27 = (bf16[32,3072]{1,0:T(8,128)(2,1)S(1)}, bf16[32,3072]{1,0:T(8,128)(2,1)S(1)}, u32[]{:S(2)}, u32[]{:S(2)}) collective-permute-start(bf16[32,3072]{1,0:T(8,128)(2,1)S(1)} %collective-permute-done.26.refs_2_), channel_id=1, source_target_pairs={{0,8},{8,0},{1,9},{9,1},{2,10},{10,2},{3,11},{11,3},{4,12},{12,4},... | collective-permute-start | bytes 589832 | tf_op jit(solution)/shard_map/ppermute | solution.py:68
  181.1 6.4 %collective-permute-start.29 = (bf16[32,3072]{1,0:T(8,128)(2,1)S(1)}, bf16[32,3072]{1,0:T(8,128)(2,1)S(1)}, u32[]{:S(2)}, u32[]{:S(2)}) collective-permute-start(bf16[32,3072]{1,0:T(8,128)(2,1)S(1)} %collective-permute-done.28.refs_4_), channel_id=1, source_target_pairs={{0,8},{8,0},{1,9},{9,1},{2,10},{10,2},{3,11},{11,3},{4,12},{12,4},... | collective-permute-start | bytes 589832 | tf_op jit(solution)/shard_map/ppermute | solution.py:68
  (8 other events, 59.7 us)

commit v2 on v0

v2 whole, which is shorter than its diff:
```python
import jax
import jax.numpy as jnp
from jax import lax
from jax.experimental import pallas as pl
from jax.experimental.pallas import tpu as pltpu
from jax.sharding import Mesh
from jax.sharding import PartitionSpec as P

STEP = 10
ENDS_DP = ("ends", "dp_0", "dp_1")
TP = ("tp_0", "tp_1")
DP = ("dp_0", "dp_1")

SIZE = (32, 32, 32, 32)
START = (0, 64, 96, 32)
STEP_COLUMNS = 512
P1, P3, Z = "p1", "p3", "z"


def over(link, seg):
    de, dy, q = seg
    if link == P1:
        return (de, dy ^ 1, q)
    if link == P3:
        return (de, dy ^ 3, q)
    return (de ^ 1, dy, q)


REDUCE = (
    {
        Z: ((1, 2, 1), (1, 1, 1), (1, 2, 2), (1, 3, 2)),
        P1: ((1, 2, 0), (0, 2, 0), (1, 1, 0), (0, 1, 0)),
        P3: ((1, 2, 3), (0, 2, 3), (1, 3, 3), (0, 3, 3)),
    },
    {
        Z: ((1, 0, 1), (1, 0, 2), (1, 3, 1), (1, 1, 2)),
        P1: ((1, 1, 3), (0, 1, 3), (0, 2, 1), (0, 1, 1)),
        P3: ((1, 3, 0), (0, 3, 0), (0, 2, 2), (0, 3, 2)),
    },
    {
        Z: ((1, 0, 0), (1, 0, 3)),
        P1: ((0, 1, 2),),
        P3: ((0, 3, 1),),
    },
)
CORE_PARTS = (
    (
        (
            (1, 2, 0, 128),
            (0, 2, 0, 64),
            (1, 1, 0, 32),
            (1, 1, 64, 32),
            (1, 3, 32, 32),
            (1, 3, 96, 32),
            (0, 1, 0, 32),
            (0, 3, 32, 32),
        ),
    ),
    (
        ((1, 1, 32, 32), (1, 1, 96, 32), (1, 3, 0, 32), (1, 3, 64, 32)),
        ((0, 1, 32, 64), (0, 2, 64, 64)),
        ((0, 3, 0, 32), (0, 3, 96, 32), (1, 0, 64, 64)),
        ((0, 1, 96, 32), (0, 3, 64, 32), (1, 0, 0, 64)),
        ((0, 0, 0, 128),),
    ),
)
OWN = ((0, 0, 0), (0, 0, 3), (0, 0, 1), (0, 0, 2))
GATHER = (
    {Z: OWN, P1: OWN, P3: OWN},
    {
        Z: ((0, 3, 1), (0, 1, 1), (0, 1, 2), (0, 3, 2)),
        P1: ((1, 0, 0), (1, 0, 3), (0, 3, 0), (0, 3, 1)),
        P3: ((1, 0, 0), (1, 0, 3), (0, 1, 3), (0, 1, 2)),
    },
    {
        Z: ((0, 2, 1), (0, 2, 2)),
        P1: ((1, 3, 0),),
        P3: ((1, 1, 3),),
    },
)


def send(link, x, name):
    with jax.named_scope(f"{name}_{link}"):
        return _send(link, x)


def _send(link, x):
    if link == Z:
        return lax.ppermute(x, "ends", [(0, 1), (1, 0)])
    flip = 1 if link == P1 else 3
    return lax.ppermute(x, "dp_0", [(i, i ^ flip) for i in range(4)])


def to_other_core(x, name):
    with jax.named_scope(f"{name}_core"):
        return lax.ppermute(x, "dp_1", [(0, 1), (1, 0)])


def rows_of(segs):
    return sum(SIZE[q] for _, _, q in segs)


def layout(segs):
    at, row = {}, 0
    for seg in segs:
        at[seg] = row
        row += SIZE[seg[2]]
    return at


def slot(de, dy, other):
    return (de * 4 + dy) * 2 + other


def block_row(table, block, row):
    return pl.multiple_of(table[block] * 128 + row, 8)


IN_VMEM = pl.BlockSpec(memory_space=pltpu.VMEM)
IN_HBM = pl.BlockSpec(memory_space=pltpu.HBM)
IN_SMEM = pl.BlockSpec(memory_space=pltpu.SMEM)


SMALL = pltpu.CompilerParams(vmem_limit_bytes=4 * 2**20)


def cost(rows, width):
    return pl.CostEstimate(flops=0, bytes_accessed=rows * width * 2, transcendentals=0)


def fetch(grad, table, parts, after, name):
    width = grad.shape[-1]
    sizes = [sum(n for _, _, _, n in part) for part in parts] * 2
    n_copies = 2 * sum(len(part) for part in parts)
    before = [] if after is None else [after]

    def kernel(table_ref, grad_ref, *refs):
        outs, sem = refs[len(before) : -1], refs[-1]
        copies = []
        for i, part in enumerate(parts * 2):
            other, row = int(i < len(parts)), 0
            for de, dy, first, n in part:
                copy = pltpu.make_async_copy(
                    grad_ref.at[pl.ds(block_row(table_ref, slot(de, dy, other), first), n)],
                    outs[i].at[pl.ds(row, n)],
                    sem.at[len(copies)],
                )
                copy.start()
                copies.append(copy)
                row += n
        for copy in copies:
            copy.wait()

    return pl.pallas_call(
        kernel,
        out_shape=[pltpu.VMEM((rows, width), jnp.bfloat16) for rows in sizes],
        in_specs=[IN_SMEM, IN_HBM] + [IN_VMEM] * len(before),
        out_specs=[IN_VMEM] * len(sizes),
        scratch_shapes=[pltpu.SemaphoreType.DMA((n_copies,))],
        compiler_params=SMALL,
        name=name,
        cost_estimate=cost(2 * sum(sizes), width),
    )(table, grad, *before)


def build(pieces, name, squares=False, after=()):
    arrays = list(after)
    for out in pieces:
        for _, sources in out:
            for x, _ in sources:
                if not any(x is have for have in arrays):
                    arrays.append(x)
    index = {id(x): i for i, x in enumerate(arrays)}
    plan = [[(n, [(index[id(x)], row) for x, row in sources]) for n, sources in out] for out in pieces]
    width = pieces[0][0][1][0][0].shape[-1]
    dtype = jnp.float32 if squares else jnp.bfloat16

    def kernel(*refs):
        ins, outs = refs[: len(arrays)], refs[len(arrays) :]
        total = None
        for out, out_ref in zip(plan, outs):
            at = 0
            for n, sources in out:
                for col in range(0, width, STEP_COLUMNS):
                    cols = pl.ds(col, STEP_COLUMNS)
                    terms = [ins[i][pl.ds(row, n), cols] for i, row in sources]
                    if len(terms) > 1:
                        acc = terms[0].astype(jnp.float32)
                        for term in terms[1:]:
                            acc += term.astype(jnp.float32)
                    else:
                        acc = terms[0]
                    out_ref[pl.ds(at, n), cols] = acc.astype(dtype)
                    if squares:
                        acc = acc * acc
                        for row in range(0, n, 8):
                            for lane in range(0, STEP_COLUMNS, 128):
                                part = acc[row : row + 8, lane : lane + 128]
                                total = part if total is None else total + part
                at += n
        if squares:
            outs[-1][...] = total

    shapes = [pltpu.VMEM((sum(n for n, _ in out), width), dtype) for out in plan]
    if squares:
        shapes.append(pltpu.VMEM((8, 128), jnp.float32))
    moved = sum(n * (1 + len(sources)) for out in plan for n, sources in out)
    return pl.pallas_call(
        kernel,
        out_shape=shapes,
        in_specs=[IN_VMEM] * len(arrays),
        out_specs=[IN_VMEM] * len(shapes),
        compiler_params=SMALL,
        name=name,
        cost_estimate=cost(moved, width),
    )(*arrays)


def place(out, table, pieces, name):
    arrays = []
    for x, *_ in pieces:
        if not any(x is have for have in arrays):
            arrays.append(x)
    index = {id(x): i for i, x in enumerate(arrays)}
    plan = [(index[id(x)], *rest) for x, *rest in pieces]
    width = arrays[0].shape[-1]
    old = [] if out is None else [out]

    def kernel(table_ref, *refs):
        ins, out_ref, token_ref, sem = refs[: len(arrays)], refs[-3], refs[-2], refs[-1]
        token_ref[...] = jnp.zeros_like(token_ref)
        copies = []
        for i, row, block, first, n in plan:
            copy = pltpu.make_async_copy(
                ins[i].at[pl.ds(row, n)],
                out_ref.at[pl.ds(block_row(table_ref, block, first), n)],
                sem.at[len(copies)],
            )
            copy.start()
            copies.append(copy)
        for copy in copies:
            copy.wait()

    return pl.pallas_call(
        kernel,
        out_shape=[
            jax.ShapeDtypeStruct((2048, width), jnp.bfloat16),
            pltpu.VMEM((8, 128), jnp.bfloat16),
        ],
        in_specs=[IN_SMEM] + [IN_VMEM] * len(arrays) + [IN_HBM] * len(old),
        out_specs=[IN_HBM, IN_VMEM],
        scratch_shapes=[pltpu.SemaphoreType.DMA((len(plan),))],
        input_output_aliases={1 + len(arrays): 0} if old else {},
        compiler_params=SMALL,
        name=name,
        cost_estimate=cost(2 * sum(p[-1] for p in plan), width),
    )(table, *arrays, *old)


def reduce_rows(grad, table):
    held = {}
    grad = pltpu.with_memory_space_constraint(grad, pltpu.HBM)

    def cross(parts, after, name):
        arrays = fetch(grad, table, parts, after, name)
        for k, part in enumerate(parts):
            got = to_other_core(arrays[k], f"{name}_{k}")
            row = 0
            for de, dy, first, n in part:
                for q in range(4):
                    if first <= START[q] < first + n:
                        at = row + START[q] - first
                        held[de, dy, q] = [(arrays[len(parts) + k], at), (got, at)]
                row += n

    cross(CORE_PARTS[0], None, "fetch0")
    for k, plan in enumerate(REDUCE):
        messages = build([[(SIZE[seg[2]], held[seg]) for seg in segs] for segs in plan.values()], f"sum{k}")
        if k == 0:
            cross(CORE_PARTS[1], messages[0], "fetch1")
        for (link, segs), x in zip(plan.items(), messages):
            at = layout(segs)
            got = send(link, x, f"reduce{k}")
            for seg in segs:
                held[over(link, seg)].append((got, at[seg]))

    return build([[(SIZE[seg[2]], held[seg]) for seg in OWN]], "own_sum", squares=True)


def runs_of(x, other, segs):
    runs = []
    for (de, dy, q), row in segs:
        last = runs[-1] if runs else None
        if last and last[1] == (de, dy) and last[2] + last[3] == START[q] and last[0] + last[3] == row:
            last[3] += SIZE[q]
        else:
            runs.append([row, (de, dy), START[q], SIZE[q]])
    pieces = []
    for row, (de, dy), first, n in runs:
        pieces.append((x, row, slot(de, dy, 0), first, n))
        pieces.append((other, row, slot(de, dy, 1), first, n))
    return pieces


def gather_rows(own, table):
    at = layout(OWN)
    held = {seg: (own, at[seg]) for seg in OWN}
    news, out, token = [(own, [(seg, at[seg]) for seg in OWN])], None, ()
    for k, plan in enumerate(GATHER):
        if k == 0:
            messages = [own] * len(plan)
        else:
            lists = plan.values()
            messages = build([[(SIZE[s[2]], [held[s]]) for s in segs] for segs in lists], f"copy{k}", after=token)
        came = []
        for (link, segs), x in zip(plan.items(), messages):
            at = layout(segs)
            got = send(link, x, f"gather{k}")
            came.append((got, [(over(link, seg), at[seg]) for seg in segs]))
        if k > 0:
            pieces = []
            for i, (x, segs) in enumerate(news):
                pieces.extend(runs_of(x, to_other_core(x, f"gather{k}_{i}"), segs))
            out, mark = place(out, table, pieces, f"place{k}")
            token = (mark,)
        for x, segs in came:
            held.update({seg: (x, row) for seg, row in segs})
        news = came if k > 0 else news + came
    last = sorted((seg for _, segs in news for seg, _ in segs), key=lambda seg: START[seg[2]])
    (x,) = build([[(SIZE[s[2]], [held[s]]) for s in last]], "copy3", after=token)
    at = layout(last)
    return place(out, table, runs_of(x, to_other_core(x, "last"), [(seg, at[seg]) for seg in last]), "place3")[0]


def total_over_all(x):
    x = jnp.sum(x, axis=0, keepdims=True)
    x = x + lax.ppermute(x, "dp_1", [(0, 1), (1, 0)])
    axes = ("ends", "dp_0", "tp_0", "tp_1")
    n = lax.axis_size(axes)
    return jnp.sum(lax.all_to_all(jnp.broadcast_to(x, (n, *x.shape)), axes, 0, 0))


def per_device(grad, master, moment, second):
    rows_tp = grad.shape[2]
    width = grad.shape[3]
    e, y, c = (lax.axis_index(a) for a in ENDS_DP)
    table = jnp.stack(
        [
            ((e ^ de) * 4 + (y ^ dy)) * 2 + (c ^ other)
            for de in range(2)
            for dy in range(4)
            for other in range(2)
        ]
    ).astype(jnp.int32)
    summed, parts = reduce_rows(grad.reshape(rows_tp, width), table)
    squares = total_over_all(parts)
    vocab_total = rows_tp * lax.axis_size(TP)
    factor = jnp.minimum(
        jnp.float32(1.0), jnp.sqrt(jnp.float32(vocab_total * width)) / (jnp.sqrt(squares) + 1e-06)
    )
    clipped = factor * summed
    moment_out = 0.9 * moment[0] + 0.1 * clipped
    second_out = 0.999 * second[0] + 0.001 * clipped * clipped
    update = moment_out / (1.0 - 0.9**STEP) / (jnp.sqrt(second_out / (1.0 - 0.999**STEP)) + 1e-08)
    master_out = master[0] - 0.01 * (update + 0.1 * master[0])
    weights = gather_rows(master_out.astype(jnp.bfloat16), table)
    return (weights, master_out[None], moment_out[None], second_out[None])


def solution(mesh):
    finer = Mesh(
        mesh.devices.reshape(mesh.shape["ends"], 4, 2, 2, 4),
        ("ends", "dp_0", "dp_1", "tp_0", "tp_1"),
    )
    return jax.shard_map(
        per_device,
        mesh=finer,
        in_specs=(
            P("ends", DP, TP, None),
            P(TP, ENDS_DP, None),
            P(TP, ENDS_DP, None),
            P(TP, ENDS_DP, None),
        ),
        out_specs=(P(TP, None), P(TP, ENDS_DP, None), P(TP, ENDS_DP, None), P(TP, ENDS_DP, None)),
        check_vma=False,
    )
```

time: 288 us -> 165 us (0.57)
  waiting for transfers between devices: 219 us -> 87 us
  starting transfers between devices: 0.08 us -> 37.6 us
  blocking collectives: 35 us -> 15.1 us
  Pallas kernels: 0 us -> 18 us
  between operations: 14.8 us -> 1.69 us
  local copies, waits for them, and re-layouts: 10.5 us -> 0.12 us
    reduce_scatter x1 -> x0, waiting for transfers between devices: 129 us -> none  [per_device(): lax.psum_scatter(local.astype(jnp.bfloat16), ENDS_DP, scatter_dimension=0...]
    all_gather x1 -> x0, waiting for transfers between devices: 89.3 us -> none  [per_device(): weights = lax.all_gather(rounded, ENDS_DP, axis=0, tiled=True)]
    ppermute x0 -> x33, waiting for transfers between devices: none -> 87 us  [the longest x12 41.8 us: _send(): return lax.ppermute(x, 'dp_0', [(i, i ^ flip) for i in range(4)])]
    ppermute x0 -> x33, starting transfers between devices: none -> 37.6 us  [the longest x14 18 us: to_other_core(): return lax.ppermute(x, 'dp_1', [(0, 1), (1, 0)])]
    psum x5 -> x0, blocking collectives: 35 us -> none  [one_axis_at_a_time(): x = lax.psum(x, axis)]
    pallas_call x0 -> x12, Pallas kernels: none -> 18 us  [the longest x3 8.42 us: place(): pl.pallas_call(kernel, out_shape=[jax.ShapeDtypeStruct((2048, width), jnp...]
    all_to_all x0 -> x1, blocking collectives: none -> 15.1 us  [total_over_all(): lax.all_to_all(jnp.broadcast_to(x, (n, *x.shape)), axes, 0, 0)]
    unnamed x5 -> x2, local copies, waits for them, and re-layouts: 10.5 us -> 0.01 us
  transfers between devices with their start and end apart: 2 -> 33, of which waited for: 2 -> 15; matrix products, arithmetic and copies ran while one was open for 0% -> 0% of each run, Pallas kernels for 0% -> 7%
where the time goes in v2:
time: 165 us
  waiting for transfers between devices  87 us (53%)
  starting transfers between devices  37.6 us (23%)
  Pallas kernels  18 us (11%)
  blocking collectives  15.1 us (9%)
  other arithmetic  5.55 us (3%)
  between operations  1.69 us (1%)
    ppermute x12, waiting for transfers between devices, _send(): return lax.ppermute(x, 'dp_0', [(i, i ^ flip) for i in range(4)])  41.8 us
    ppermute x6, waiting for transfers between devices, _send(): return lax.ppermute(x, 'ends', [(0, 1), (1, 0)])  38.3 us
    ppermute x14, starting transfers between devices, to_other_core(): return lax.ppermute(x, 'dp_1', [(0, 1), (1, 0)])  18 us
    all_to_all x1, blocking collectives, total_over_all(): lax.all_to_all(jnp.broadcast_to(x, (n, *x.shape)), axes, 0, 0)  15.1 us
    ppermute x12, starting transfers between devices, _send(): return lax.ppermute(x, 'dp_0', [(i, i ^ flip) for i in range(4)])  9.7 us
    pallas_call x3, Pallas kernels, place(): pl.pallas_call(kernel, out_shape=[jax.ShapeDtypeStruct((2048, width), jnp...  8.42 us
    ppermute x6, starting transfers between devices, _send(): return lax.ppermute(x, 'ends', [(0, 1), (1, 0)])  7.84 us
    pallas_call x2, Pallas kernels, fetch(): pl.pallas_call(kernel, out_shape=[pltpu.VMEM((rows, width), jnp.bfloat16)...  7.12 us
  transfers between devices with their start and end apart: 33, of which 15 were waited for; matrix products, arithmetic and copies ran while one was open for 0% of the time, Pallas kernels for 7%

profile of v2, /device:TPU:1, one launch (start us, length us, event | category | flops | bytes accessed | tf_op | source)
XLA Modules:
  0.0 165.1 jit_solution(4295778381779600341)
XLA Ops:
  0.8 3.0 %fetch0.1 = (bf16[384,3072]{1,0:T(8,128)(2,1)S(1)}, bf16[384,3072]{1,0:T(8,128)(2,1)S(1)}) custom-call(s32[16]{0:T(128)S(1)} %stack.67.table_ref, bf16[2048,3072]{1,0:T(8,128)(2,1)} %bitcast.51), custom_call_target="tpu_custom_call" | custom-call | bytes 9437184 | tf_op jit(solution)/shard_map/fetch0/pallas_call | solution.py:155
  3.7 1.5 collective-permute-start
  5.2 4.2 %collective-permute-done.refs_1_ = bf16[384,3072]{1,0:T(8,128)(2,1)S(1)} collective-permute-done((bf16[384,3072]{1,0:T(8,128)(2,1)S(1)}, bf16[384,3072]{1,0:T(8,128)(2,1)S(1)}, u32[]{:S(2)}, u32[]{:S(2)}) %collective-permute-start) | collective-permute-done | bytes 2359328 | tf_op jit(solution)/shard_map/fetch0_0_core/ppermute | solution.py:97
  9.9 1.5 collective-permute-start.2
  11.4 3.6 %collective-permute-start.7 = (bf16[128,3072]{1,0:T(8,128)(2,1)S(1)}, bf16[128,3072]{1,0:T(8,128)(2,1)S(1)}, u32[]{:S(2)}, u32[]{:S(2)}) collective-permute-start(bf16[128,3072]{1,0:T(8,128)(2,1)S(1)} %get-tuple-element.40.refs_0_), channel_id=1, source_target_pairs={{0,64},{64,0},{1,65},{65,1},{2,66},{66,2},{3,67},{67,3},{4,68},{68... | collective-permute-start | bytes 2359304 | tf_op jit(solution)/shard_map/reduce0_z/ppermute | solution.py:90
  15.0 4.1 %fetch1.1 = (bf16[128,3072]{1,0:T(8,128)(2,1)S(1)}, bf16[128,3072]{1,0:T(8,128)(2,1)S(1)}, bf16[128,3072]{1,0:T(8,128)(2,1)S(1)}, bf16[128,3072]{1,0:T(8,128)(2,...) custom-call(s32[16]{0:T(128)S(1)} %stack.67.table_ref, ...), custom_call_target="tpu_custom_call" | custom-call | bytes 15728640 | tf_op jit(solution)/shard_map/fetch1/pallas_call | solution.py:155
  19.1 2.0 %collective-permute-start.5 = (bf16[128,3072]{1,0:T(8,128)(2,1)S(1)}, bf16[128,3072]{1,0:T(8,128)(2,1)S(1)}, u32[]{:S(2)}, u32[]{:S(2)}) collective-permute-start(bf16[128,3072]{1,0:T(8,128)(2,1)S(1)} %get-tuple-element.48), channel_id=1, source_target_pairs={{0,48},{16,32},{32,16},{48,0},{1,49},{17,33},{33,17},{49,1},{2,50}... | collective-permute-start | bytes 2359304 | tf_op jit(solution)/shard_map/reduce0_p3/ppermute | solution.py:92
  21.1 1.2 collective-permute-start.3
  22.3 6.4 %collective-permute-done.2.refs_8_.refs_2_ = bf16[128,3072]{1,0:T(8,128)(2,1)S(1)} collective-permute-done((bf16[128,3072]{1,0:T(8,128)(2,1)S(1)}, bf16[128,3072]{1,0:T(8,128)(2,1)S(1)}, u32[]{:S(2)}, u32[]{:S(2)}) %collective-permute-start.2) | collective-permute-done | bytes 786464 | tf_op jit(solution)/shard_map/reduce0_p1/ppermute | solution.py:92
  30.0 8.6 %collective-permute-done.5.refs_4_.refs_5_ = bf16[128,3072]{1,0:T(8,128)(2,1)S(1)} collective-permute-done((bf16[128,3072]{1,0:T(8,128)(2,1)S(1)}, bf16[128,3072]{1,0:T(8,128)(2,1)S(1)}, u32[]{:S(2)}, u32[]{:S(2)}) %collective-permute-start.5) | collective-permute-done | bytes 786464 | tf_op jit(solution)/shard_map/reduce0_p3/ppermute | solution.py:92
  38.5 1.8 %collective-permute-start.9 = (bf16[128,3072]{1,0:T(8,128)(2,1)S(1)}, bf16[128,3072]{1,0:T(8,128)(2,1)S(1)}, u32[]{:S(2)}, u32[]{:S(2)}) collective-permute-start(bf16[128,3072]{1,0:T(8,128)(2,1)S(1)} %get-tuple-element.53), channel_id=1, source_target_pairs={{0,8},{8,0},{1,9},{9,1},{2,10},{10,2},{3,11},{11,3},{4,12},{12,4},... | collective-permute-start | bytes 2359304 | tf_op jit(solution)/shard_map/fetch1_3_core/ppermute | solution.py:97
  41.2 2.0 %collective-permute-start.8 = (bf16[128,3072]{1,0:T(8,128)(2,1)S(1)}, bf16[128,3072]{1,0:T(8,128)(2,1)S(1)}, u32[]{:S(2)}, u32[]{:S(2)}) collective-permute-start(bf16[128,3072]{1,0:T(8,128)(2,1)S(1)} %get-tuple-element.51), channel_id=1, source_target_pairs={{0,48},{16,32},{32,16},{48,0},{1,49},{17,33},{33,17},{49,1},{2,50}... | collective-permute-start | bytes 2359304 | tf_op jit(solution)/shard_map/reduce1_p3/ppermute | solution.py:92
  43.7 17.9 %collective-permute-done.8.refs_3_ = bf16[128,3072]{1,0:T(8,128)(2,1)S(1)} collective-permute-done((bf16[128,3072]{1,0:T(8,128)(2,1)S(1)}, bf16[128,3072]{1,0:T(8,128)(2,1)S(1)}, u32[]{:S(2)}, u32[]{:S(2)}) %collective-permute-start.8) | collective-permute-done | bytes 786464 | tf_op jit(solution)/shard_map/reduce1_p3/ppermute | solution.py:92
  62.0 1.5 collective-permute-done.11.refs_6_.refs_7_
  65.4 5.0 %collective-permute-done.13.refs_8_ = bf16[32,3072]{1,0:T(8,128)(2,1)S(1)} collective-permute-done((bf16[32,3072]{1,0:T(8,128)(2,1)S(1)}, bf16[32,3072]{1,0:T(8,128)(2,1)S(1)}, u32[]{:S(2)}, u32[]{:S(2)}) %collective-permute-start.13) | collective-permute-done | bytes 196640 | tf_op jit(solution)/shard_map/reduce2_p3/ppermute | solution.py:92
  70.4 4.6 %collective-permute-done.12.refs_4_ = bf16[64,3072]{1,0:T(8,128)(2,1)S(1)} collective-permute-done((bf16[64,3072]{1,0:T(8,128)(2,1)S(1)}, bf16[64,3072]{1,0:T(8,128)(2,1)S(1)}, u32[]{:S(2)}, u32[]{:S(2)}) %collective-permute-start.12) | collective-permute-done | bytes 393248 | tf_op jit(solution)/shard_map/reduce2_z/ppermute | solution.py:90
  75.6 2.1 %collective-permute-start.15 = (f32[1,128]{1,0:T(1,128)S(1)}, f32[1,128]{1,0:T(1,128)S(1)}, u32[]{:S(2)}, u32[]{:S(2)}) collective-permute-start(f32[1,128]{1,0:T(1,128)S(1)} %bitcast.55), channel_id=1, source_target_pairs={{0,8},{8,0},{1,9},{9,1},{2,10},{10,2},{3,11},{11,3},{4,12},{12,4},... | collective-permute-start | bytes 1544 | tf_op jit(solution)/shard_map/ppermute | solution.py:338
  78.5 15.1 %all_to_all.5 = f32[64,1,128]{2,1,0:T(1,128)S(1)} all-to-all(f32[64,1,128]{2,1,0:T(1,128)S(1)} %broadcast_in_dim.16), channel_id=1, replica_groups=mesh['ends'=2,'dp_0'=4,'dp_1'=2,'tp_0'=2,'tp_1'=4] {'ends','dp_0','tp_0'..., dimensions={0} | all-to-all | bytes 65536 | tf_op jit(solution)/shard_map/all_to_all | solution.py:341
  95.0 4.9 %fusion.5 = (bf16[128,3072]{1,0:T(8,128)(2,1)S(1)}, f32[128,3072]{1,0:T(8,128)}, f32[1,128,3072]{2,1,0:T(8,128)}, f32[1,128,3072]{2,1,0:T(8,128)}) fusion(f32[1,128,3072]{2,1,0:T(8,128)S(1)} %copy-done, f32[128,3072]{1,0:T(8,128)S(1)} %get-tuple-element.60, f32[]{:T(128)S(6)} %min_shard_map.3, f32[1,128,3072]{2,1,0:T(8,128)} %param.6, f32[1,128,3072]{2,1,0:T(8,128)} %param.5), kind=kLoop, calls=%fused_computation.10 | loop fusion | flops 6684672 | bytes 11796484 | tf_op jit(solution)/shard_map/convert_element_type | solution.py:367
  102.0 2.6 %collective-permute-start.25 = (bf16[128,3072]{1,0:T(8,128)(2,1)S(1)}, bf16[128,3072]{1,0:T(8,128)(2,1)S(1)}, u32[]{:S(2)}, u32[]{:S(2)}) collective-permute-start(bf16[128,3072]{1,0:T(8,128)(2,1)S(1)} %get-tuple-element.72.refs_0_), channel_id=1, source_target_pairs={{0,8},{8,0},{1,9},{9,1},{2,10},{10,2},{3,11},{11,3},{4,12},{12,4},... | collective-permute-start | bytes 2359304 | tf_op jit(solution)/shard_map/gather1_0_core/ppermute | solution.py:97
  104.5 14.2 %collective-permute-done.18.refs_2_ = bf16[128,3072]{1,0:T(8,128)(2,1)S(1)} collective-permute-done((bf16[128,3072]{1,0:T(8,128)(2,1)S(1)}, bf16[128,3072]{1,0:T(8,128)(2,1)S(1)}, u32[]{:S(2)}, u32[]{:S(2)}) %collective-permute-start.18) | collective-permute-done | bytes 786464 | tf_op jit(solution)/shard_map/gather0_z/ppermute | solution.py:90
  118.7 2.7 %collective-permute-start.26 = (bf16[128,3072]{1,0:T(8,128)(2,1)S(1)}, bf16[128,3072]{1,0:T(8,128)(2,1)S(1)}, u32[]{:S(2)}, u32[]{:S(2)}) collective-permute-start(bf16[128,3072]{1,0:T(8,128)(2,1)S(1)} %collective-permute-done.18.refs_2_), channel_id=1, source_target_pairs={{0,8},{8,0},{1,9},{9,1},{2,10},{10,2},{3,11},{11,3},{4,12},{12,4},... | collective-permute-start | bytes 2359304 | tf_op jit(solution)/shard_map/gather1_1_core/ppermute | solution.py:97
  123.7 2.4 %collective-permute-start.27 = (bf16[128,3072]{1,0:T(8,128)(2,1)S(1)}, bf16[128,3072]{1,0:T(8,128)(2,1)S(1)}, u32[]{:S(2)}, u32[]{:S(2)}) collective-permute-start(bf16[128,3072]{1,0:T(8,128)(2,1)S(1)} %collective-permute-done.17.refs_1_.refs_4_), channel_id=1, source_target_pairs={{0,8},{8,0},{1,9},{9,1},{2,10},{10,2},{3,11},{11,3},{4,12},{12,4},... | collective-permute-start | bytes 2359304 | tf_op jit(solution)/shard_map/gather1_2_core/ppermute | solution.py:97
  126.2 14.9 %collective-permute-done.19.refs_0_ = bf16[128,3072]{1,0:T(8,128)(2,1)S(1)} collective-permute-done((bf16[128,3072]{1,0:T(8,128)(2,1)S(1)}, bf16[128,3072]{1,0:T(8,128)(2,1)S(1)}, u32[]{:S(2)}, u32[]{:S(2)}) %collective-permute-start.19) | collective-permute-done | bytes 786464 | tf_op jit(solution)/shard_map/gather1_z/ppermute | solution.py:90
  141.1 2.0 %collective-permute-start.20 = (bf16[128,3072]{1,0:T(8,128)(2,1)S(1)}, bf16[128,3072]{1,0:T(8,128)(2,1)S(1)}, u32[]{:S(2)}, u32[]{:S(2)}) collective-permute-start(bf16[128,3072]{1,0:T(8,128)(2,1)S(1)} %collective-permute-done.19.refs_0_), channel_id=1, source_target_pairs={{0,8},{8,0},{1,9},{9,1},{2,10},{10,2},{3,11},{11,3},{4,12},{12,4},... | collective-permute-start | bytes 2359304 | tf_op jit(solution)/shard_map/gather2_0_core/ppermute | solution.py:97
  144.1 3.3 %place1.1 = (bf16[2048,3072]{1,0:T(8,128)(2,1)}, bf16[8,128]{1,0:T(8,128)(2,1)S(1)}) custom-call(s32[16]{0:T(128)S(1)} %stack.67.table_ref, bf16[128,3072]{1,0:T(8,128)(2,1)S(1)} %get-tuple-element.72.refs_0_, bf16[128,3072]{1,0:T(8,128)(2,1)S(1)} %collective-permute-done.25.refs_1_, bf16[128,3072]{1,0:T(8,128)(2,1)S(1)} %collective-permute-done.18.refs_2_, ...), custom_call_target="tpu_custom_call" | custom-call | bytes 12582912 | tf_op jit(solution)/shard_map/place1/pallas_call | solution.py:245
  147.5 2.0 %collective-permute-start.31 = (bf16[64,3072]{1,0:T(8,128)(2,1)S(1)}, bf16[64,3072]{1,0:T(8,128)(2,1)S(1)}, u32[]{:S(2)}, u32[]{:S(2)}) collective-permute-start(bf16[64,3072]{1,0:T(8,128)(2,1)S(1)} %get-tuple-element.69), channel_id=1, source_target_pairs={{0,64},{64,0},{1,65},{65,1},{2,66},{66,2},{3,67},{67,3},{4,68},{68... | collective-permute-start | bytes 1179656 | tf_op jit(solution)/shard_map/gather2_z/ppermute | solution.py:90
  150.3 2.9 %place2.1 = (bf16[2048,3072]{1,0:T(8,128)(2,1)}, bf16[8,128]{1,0:T(8,128)(2,1)S(1)}) custom-call(s32[16]{0:T(128)S(1)} %stack.67.table_ref, bf16[128,3072]{1,0:T(8,128)(2,1)S(1)} %collective-permute-done.19.refs_0_, bf16[128,3072]{1,0:T(8,128)(2,1)S(1)} %collective-permute-done.20.refs_1_, ...), custom_call_target="tpu_custom_call", output_to_operand_aliasing={{0}: (7, {})} | custom-call | bytes 9437184 | tf_op jit(solution)/shard_map/place2/pallas_call | solution.py:245
  153.2 2.5 %collective-permute-done.29.refs_1_ = bf16[32,3072]{1,0:T(8,128)(2,1)S(1)} collective-permute-done((bf16[32,3072]{1,0:T(8,128)(2,1)S(1)}, bf16[32,3072]{1,0:T(8,128)(2,1)S(1)}, u32[]{:S(2)}, u32[]{:S(2)}) %collective-permute-start.29) | collective-permute-done | bytes 196640 | tf_op jit(solution)/shard_map/gather2_p1/ppermute | solution.py:92
  156.7 3.1 %collective-permute-done.31.refs_3_ = bf16[64,3072]{1,0:T(8,128)(2,1)S(1)} collective-permute-done((bf16[64,3072]{1,0:T(8,128)(2,1)S(1)}, bf16[64,3072]{1,0:T(8,128)(2,1)S(1)}, u32[]{:S(2)}, u32[]{:S(2)}) %collective-permute-start.31) | collective-permute-done | bytes 393248 | tf_op jit(solution)/shard_map/gather2_z/ppermute | solution.py:90
  160.7 1.9 %collective-permute-done.32.refs_1_ = bf16[128,3072]{1,0:T(8,128)(2,1)S(1)} collective-permute-done((bf16[128,3072]{1,0:T(8,128)(2,1)S(1)}, bf16[128,3072]{1,0:T(8,128)(2,1)S(1)}, u32[]{:S(2)}, u32[]{:S(2)}) %collective-permute-start.32) | collective-permute-done | bytes 786464 | tf_op jit(solution)/shard_map/last_core/ppermute | solution.py:97
  162.7 2.3 %place3.1 = (bf16[2048,3072]{1,0:T(8,128)(2,1)}, bf16[8,128]{1,0:T(8,128)(2,1)}) custom-call(s32[16]{0:T(128)S(1)} %stack.67.table_ref, bf16[128,3072]{1,0:T(8,128)(2,1)S(1)} %copy3.1.refs_0_, bf16[128,3072]{1,0:T(8,128)(2,1)S(1)} %collective-permute-done.32.refs_1_, bf16[2048,3072]{1,0:T(8,128)(2,1)} %get-tuple-element.70.refs_2_), custom_call_target="tpu_custom_call", output_to_operand_aliasing={{0}: (3, {})} | custom-call | bytes 3145728 | tf_op jit(solution)/shard_map/place3/pallas_call | solution.py:245
  (55 shorter events, 15.8 us)
Async XLA Ops:
  3.7 5.7 %collective-permute-start = (bf16[384,3072]{1,0:T(8,128)(2,1)S(1)}, bf16[384,3072]{1,0:T(8,128)(2,1)S(1)}, u32[]{:S(2)}, u32[]{:S(2)}) collective-permute-start(bf16[384,3072]{1,0:T(8,128)(2,1)S(1)} %get-tuple-element.39), channel_id=1, source_target_pairs={{0,8},{8,0},{1,9},{9,1},{2,10},{10,2},{3,11},{11,3},{4,12},{12,4},... | collective-permute-start | bytes 7077896 | tf_op jit(solution)/shard_map/fetch0_0_core/ppermute | solution.py:97
  9.9 18.8 %collective-permute-start.2 = (bf16[128,3072]{1,0:T(8,128)(2,1)S(1)}, bf16[128,3072]{1,0:T(8,128)(2,1)S(1)}, u32[]{:S(2)}, u32[]{:S(2)}) collective-permute-start(bf16[128,3072]{1,0:T(8,128)(2,1)S(1)} %get-tuple-element.43), channel_id=1, source_target_pairs={{0,16},{16,0},{32,48},{48,32},{1,17},{17,1},{33,49},{49,33},{2,18}... | collective-permute-start | bytes 2359304 | tf_op jit(solution)/shard_map/reduce0_p1/ppermute | solution.py:92
  11.4 29.0 %collective-permute-start.7 = (bf16[128,3072]{1,0:T(8,128)(2,1)S(1)}, bf16[128,3072]{1,0:T(8,128)(2,1)S(1)}, u32[]{:S(2)}, u32[]{:S(2)}) collective-permute-start(bf16[128,3072]{1,0:T(8,128)(2,1)S(1)} %get-tuple-element.40.refs_0_), channel_id=1, source_target_pairs={{0,64},{64,0},{1,65},{65,1},{2,66},{66,2},{3,67},{67,3},{4,68},{68... | collective-permute-start | bytes 2359304 | tf_op jit(solution)/shard_map/reduce0_z/ppermute | solution.py:90
  19.1 19.4 %collective-permute-start.5 = (bf16[128,3072]{1,0:T(8,128)(2,1)S(1)}, bf16[128,3072]{1,0:T(8,128)(2,1)S(1)}, u32[]{:S(2)}, u32[]{:S(2)}) collective-permute-start(bf16[128,3072]{1,0:T(8,128)(2,1)S(1)} %get-tuple-element.48), channel_id=1, source_target_pairs={{0,48},{16,32},{32,16},{48,0},{1,49},{17,33},{33,17},{49,1},{2,50}... | collective-permute-start | bytes 2359304 | tf_op jit(solution)/shard_map/reduce0_p3/ppermute | solution.py:92
  21.1 19.3 %collective-permute-start.3 = (bf16[128,3072]{1,0:T(8,128)(2,1)S(1)}, bf16[128,3072]{1,0:T(8,128)(2,1)S(1)}, u32[]{:S(2)}, u32[]{:S(2)}) collective-permute-start(bf16[128,3072]{1,0:T(8,128)(2,1)S(1)} %get-tuple-element.45), channel_id=1, source_target_pairs={{0,8},{8,0},{1,9},{9,1},{2,10},{10,2},{3,11},{11,3},{4,12},{12,4},... | collective-permute-start | bytes 2359304 | tf_op jit(solution)/shard_map/fetch1_2_core/ppermute | solution.py:97
  22.3 18.1 %collective-permute-start.4 = (bf16[128,3072]{1,0:T(8,128)(2,1)S(1)}, bf16[128,3072]{1,0:T(8,128)(2,1)S(1)}, u32[]{:S(2)}, u32[]{:S(2)}) collective-permute-start(bf16[128,3072]{1,0:T(8,128)(2,1)S(1)} %get-tuple-element.47), channel_id=1, source_target_pairs={{0,8},{8,0},{1,9},{9,1},{2,10},{10,2},{3,11},{11,3},{4,12},{12,4},... | collective-permute-start | bytes 2359304 | tf_op jit(solution)/shard_map/fetch1_0_core/ppermute | solution.py:97
  28.8 11.6 %collective-permute-start.6 = (bf16[128,3072]{1,0:T(8,128)(2,1)S(1)}, bf16[128,3072]{1,0:T(8,128)(2,1)S(1)}, u32[]{:S(2)}, u32[]{:S(2)}) collective-permute-start(bf16[128,3072]{1,0:T(8,128)(2,1)S(1)} %get-tuple-element.50), channel_id=1, source_target_pairs={{0,8},{8,0},{1,9},{9,1},{2,10},{10,2},{3,11},{11,3},{4,12},{12,4},... | collective-permute-start | bytes 2359304 | tf_op jit(solution)/shard_map/fetch1_1_core/ppermute | solution.py:97
  38.5 5.2 %collective-permute-start.9 = (bf16[128,3072]{1,0:T(8,128)(2,1)S(1)}, bf16[128,3072]{1,0:T(8,128)(2,1)S(1)}, u32[]{:S(2)}, u32[]{:S(2)}) collective-permute-start(bf16[128,3072]{1,0:T(8,128)(2,1)S(1)} %get-tuple-element.53), channel_id=1, source_target_pairs={{0,8},{8,0},{1,9},{9,1},{2,10},{10,2},{3,11},{11,3},{4,12},{12,4},... | collective-permute-start | bytes 2359304 | tf_op jit(solution)/shard_map/fetch1_3_core/ppermute | solution.py:97
  41.2 20.5 %collective-permute-start.8 = (bf16[128,3072]{1,0:T(8,128)(2,1)S(1)}, bf16[128,3072]{1,0:T(8,128)(2,1)S(1)}, u32[]{:S(2)}, u32[]{:S(2)}) collective-permute-start(bf16[128,3072]{1,0:T(8,128)(2,1)S(1)} %get-tuple-element.51), channel_id=1, source_target_pairs={{0,48},{16,32},{32,16},{48,0},{1,49},{17,33},{33,17},{49,1},{2,50}... | collective-permute-start | bytes 2359304 | tf_op jit(solution)/shard_map/reduce1_p3/ppermute | solution.py:92
  43.1 18.8 %collective-permute-start.10 = (bf16[128,3072]{1,0:T(8,128)(2,1)S(1)}, bf16[128,3072]{1,0:T(8,128)(2,1)S(1)}, u32[]{:S(2)}, u32[]{:S(2)}) collective-permute-start(bf16[128,3072]{1,0:T(8,128)(2,1)S(1)} %get-tuple-element.54), channel_id=1, source_target_pairs={{0,16},{16,0},{32,48},{48,32},{1,17},{17,1},{33,49},{49,33},{2,18}... | collective-permute-start | bytes 2359304 | tf_op jit(solution)/shard_map/reduce1_p1/ppermute | solution.py:92
  43.1 20.4 %collective-permute-start.11 = (bf16[128,3072]{1,0:T(8,128)(2,1)S(1)}, bf16[128,3072]{1,0:T(8,128)(2,1)S(1)}, u32[]{:S(2)}, u32[]{:S(2)}) collective-permute-start(bf16[128,3072]{1,0:T(8,128)(2,1)S(1)} %get-tuple-element.55), channel_id=1, source_target_pairs={{0,64},{64,0},{1,65},{65,1},{2,66},{66,2},{3,67},{67,3},{4,68},{68... | collective-permute-start | bytes 2359304 | tf_op jit(solution)/shard_map/reduce1_z/ppermute | solution.py:90
  43.2 22.2 %collective-permute-start.1 = (bf16[128,3072]{1,0:T(8,128)(2,1)S(1)}, bf16[128,3072]{1,0:T(8,128)(2,1)S(1)}, u32[]{:S(2)}, u32[]{:S(2)}) collective-permute-start(bf16[128,3072]{1,0:T(8,128)(2,1)S(1)} %get-tuple-element.42), channel_id=1, source_target_pairs={{0,8},{8,0},{1,9},{9,1},{2,10},{10,2},{3,11},{11,3},{4,12},{12,4},... | collective-permute-start | bytes 2359304 | tf_op jit(solution)/shard_map/fetch1_4_core/ppermute | solution.py:97
  63.9 11.1 %collective-permute-start.12 = (bf16[64,3072]{1,0:T(8,128)(2,1)S(1)}, bf16[64,3072]{1,0:T(8,128)(2,1)S(1)}, u32[]{:S(2)}, u32[]{:S(2)}) collective-permute-start(bf16[64,3072]{1,0:T(8,128)(2,1)S(1)} %get-tuple-element.56), channel_id=1, source_target_pairs={{0,64},{64,0},{1,65},{65,1},{2,66},{66,2},{3,67},{67,3},{4,68},{68... | collective-permute-start | bytes 1179656 | tf_op jit(solution)/shard_map/reduce2_z/ppermute | solution.py:90
  64.0 6.4 %collective-permute-start.13 = (bf16[32,3072]{1,0:T(8,128)(2,1)S(1)}, bf16[32,3072]{1,0:T(8,128)(2,1)S(1)}, u32[]{:S(2)}, u32[]{:S(2)}) collective-permute-start(bf16[32,3072]{1,0:T(8,128)(2,1)S(1)} %get-tuple-element.57), channel_id=1, source_target_pairs={{0,48},{16,32},{32,16},{48,0},{1,49},{17,33},{33,17},{49,1},{2,50}... | collective-permute-start | bytes 589832 | tf_op jit(solution)/shard_map/reduce2_p3/ppermute | solution.py:92
  64.8 5.5 %collective-permute-start.14 = (bf16[32,3072]{1,0:T(8,128)(2,1)S(1)}, bf16[32,3072]{1,0:T(8,128)(2,1)S(1)}, u32[]{:S(2)}, u32[]{:S(2)}) collective-permute-start(bf16[32,3072]{1,0:T(8,128)(2,1)S(1)} %get-tuple-element.58), channel_id=1, source_target_pairs={{0,16},{16,0},{32,48},{48,32},{1,17},{17,1},{33,49},{49,33},{2,18}... | collective-permute-start | bytes 589832 | tf_op jit(solution)/shard_map/reduce2_p1/ppermute | solution.py:92
  75.6 2.9 %collective-permute-start.15 = (f32[1,128]{1,0:T(1,128)S(1)}, f32[1,128]{1,0:T(1,128)S(1)}, u32[]{:S(2)}, u32[]{:S(2)}) collective-permute-start(f32[1,128]{1,0:T(1,128)S(1)} %bitcast.55), channel_id=1, source_target_pairs={{0,8},{8,0},{1,9},{9,1},{2,10},{10,2},{3,11},{11,3},{4,12},{12,4},... | collective-permute-start | bytes 1544 | tf_op jit(solution)/shard_map/ppermute | solution.py:338
  99.9 18.8 %collective-permute-start.18 = (bf16[128,3072]{1,0:T(8,128)(2,1)S(1)}, bf16[128,3072]{1,0:T(8,128)(2,1)S(1)}, u32[]{:S(2)}, u32[]{:S(2)}) collective-permute-start(bf16[128,3072]{1,0:T(8,128)(2,1)S(1)} %get-tuple-element.72.refs_0_), channel_id=1, source_target_pairs={{0,64},{64,0},{1,65},{65,1},{2,66},{66,2},{3,67},{67,3},{4,68},{68... | collective-permute-start | bytes 2359304 | tf_op jit(solution)/shard_map/gather0_z/ppermute | solution.py:90
  100.9 20.4 %collective-permute-start.17 = (bf16[128,3072]{1,0:T(8,128)(2,1)S(1)}, bf16[128,3072]{1,0:T(8,128)(2,1)S(1)}, u32[]{:S(2)}, u32[]{:S(2)}) collective-permute-start(bf16[128,3072]{1,0:T(8,128)(2,1)S(1)} %get-tuple-element.72.refs_0_), channel_id=1, source_target_pairs={{0,16},{16,0},{32,48},{48,32},{1,17},{17,1},{33,49},{49,33},{2,18}... | collective-permute-start | bytes 2359304 | tf_op jit(solution)/shard_map/gather0_p1/ppermute | solution.py:92
  101.3 20.1 %collective-permute-start.16 = (bf16[128,3072]{1,0:T(8,128)(2,1)S(1)}, bf16[128,3072]{1,0:T(8,128)(2,1)S(1)}, u32[]{:S(2)}, u32[]{:S(2)}) collective-permute-start(bf16[128,3072]{1,0:T(8,128)(2,1)S(1)} %get-tuple-element.72.refs_0_), channel_id=1, source_target_pairs={{0,48},{16,32},{32,16},{48,0},{1,49},{17,33},{33,17},{49,1},{2,50}... | collective-permute-start | bytes 2359304 | tf_op jit(solution)/shard_map/gather0_p3/ppermute | solution.py:92
  102.0 21.7 %collective-permute-start.25 = (bf16[128,3072]{1,0:T(8,128)(2,1)S(1)}, bf16[128,3072]{1,0:T(8,128)(2,1)S(1)}, u32[]{:S(2)}, u32[]{:S(2)}) collective-permute-start(bf16[128,3072]{1,0:T(8,128)(2,1)S(1)} %get-tuple-element.72.refs_0_), channel_id=1, source_target_pairs={{0,8},{8,0},{1,9},{9,1},{2,10},{10,2},{3,11},{11,3},{4,12},{12,4},... | collective-permute-start | bytes 2359304 | tf_op jit(solution)/shard_map/gather1_0_core/ppermute | solution.py:97
  118.7 7.4 %collective-permute-start.26 = (bf16[128,3072]{1,0:T(8,128)(2,1)S(1)}, bf16[128,3072]{1,0:T(8,128)(2,1)S(1)}, u32[]{:S(2)}, u32[]{:S(2)}) collective-permute-start(bf16[128,3072]{1,0:T(8,128)(2,1)S(1)} %collective-permute-done.18.refs_2_), channel_id=1, source_target_pairs={{0,8},{8,0},{1,9},{9,1},{2,10},{10,2},{3,11},{11,3},{4,12},{12,4},... | collective-permute-start | bytes 2359304 | tf_op jit(solution)/shard_map/gather1_1_core/ppermute | solution.py:97
  121.5 19.6 %collective-permute-start.19 = (bf16[128,3072]{1,0:T(8,128)(2,1)S(1)}, bf16[128,3072]{1,0:T(8,128)(2,1)S(1)}, u32[]{:S(2)}, u32[]{:S(2)}) collective-permute-start(bf16[128,3072]{1,0:T(8,128)(2,1)S(1)} %get-tuple-element.61), channel_id=1, source_target_pairs={{0,64},{64,0},{1,65},{65,1},{2,66},{66,2},{3,67},{67,3},{4,68},{68... | collective-permute-start | bytes 2359304 | tf_op jit(solution)/shard_map/gather1_z/ppermute | solution.py:90
  122.6 20.4 %collective-permute-start.21 = (bf16[128,3072]{1,0:T(8,128)(2,1)S(1)}, bf16[128,3072]{1,0:T(8,128)(2,1)S(1)}, u32[]{:S(2)}, u32[]{:S(2)}) collective-permute-start(bf16[128,3072]{1,0:T(8,128)(2,1)S(1)} %get-tuple-element.62), channel_id=1, source_target_pairs={{0,16},{16,0},{32,48},{48,32},{1,17},{17,1},{33,49},{49,33},{2,18}... | collective-permute-start | bytes 2359304 | tf_op jit(solution)/shard_map/gather1_p1/ppermute | solution.py:92
  123.0 20.1 %collective-permute-start.23 = (bf16[128,3072]{1,0:T(8,128)(2,1)S(1)}, bf16[128,3072]{1,0:T(8,128)(2,1)S(1)}, u32[]{:S(2)}, u32[]{:S(2)}) collective-permute-start(bf16[128,3072]{1,0:T(8,128)(2,1)S(1)} %get-tuple-element.63), channel_id=1, source_target_pairs={{0,48},{16,32},{32,16},{48,0},{1,49},{17,33},{33,17},{49,1},{2,50}... | collective-permute-start | bytes 2359304 | tf_op jit(solution)/shard_map/gather1_p3/ppermute | solution.py:92
  123.7 20.5 %collective-permute-start.27 = (bf16[128,3072]{1,0:T(8,128)(2,1)S(1)}, bf16[128,3072]{1,0:T(8,128)(2,1)S(1)}, u32[]{:S(2)}, u32[]{:S(2)}) collective-permute-start(bf16[128,3072]{1,0:T(8,128)(2,1)S(1)} %collective-permute-done.17.refs_1_.refs_4_), channel_id=1, source_target_pairs={{0,8},{8,0},{1,9},{9,1},{2,10},{10,2},{3,11},{11,3},{4,12},{12,4},... | collective-permute-start | bytes 2359304 | tf_op jit(solution)/shard_map/gather1_2_core/ppermute | solution.py:97
  126.1 18.1 %collective-permute-start.28 = (bf16[128,3072]{1,0:T(8,128)(2,1)S(1)}, bf16[128,3072]{1,0:T(8,128)(2,1)S(1)}, u32[]{:S(2)}, u32[]{:S(2)}) collective-permute-start(bf16[128,3072]{1,0:T(8,128)(2,1)S(1)} %collective-permute-done.16.refs_0_.refs_6_), channel_id=1, source_target_pairs={{0,8},{8,0},{1,9},{9,1},{2,10},{10,2},{3,11},{11,3},{4,12},{12,4},... | collective-permute-start | bytes 2359304 | tf_op jit(solution)/shard_map/gather1_3_core/ppermute | solution.py:97
  141.1 8.4 %collective-permute-start.20 = (bf16[128,3072]{1,0:T(8,128)(2,1)S(1)}, bf16[128,3072]{1,0:T(8,128)(2,1)S(1)}, u32[]{:S(2)}, u32[]{:S(2)}) collective-permute-start(bf16[128,3072]{1,0:T(8,128)(2,1)S(1)} %collective-permute-done.19.refs_0_), channel_id=1, source_target_pairs={{0,8},{8,0},{1,9},{9,1},{2,10},{10,2},{3,11},{11,3},{4,12},{12,4},... | collective-permute-start | bytes 2359304 | tf_op jit(solution)/shard_map/gather2_0_core/ppermute | solution.py:97
  143.1 7.2 %collective-permute-start.22 = (bf16[128,3072]{1,0:T(8,128)(2,1)S(1)}, bf16[128,3072]{1,0:T(8,128)(2,1)S(1)}, u32[]{:S(2)}, u32[]{:S(2)}) collective-permute-start(bf16[128,3072]{1,0:T(8,128)(2,1)S(1)} %collective-permute-done.21.refs_2_.refs_1_), channel_id=1, source_target_pairs={{0,8},{8,0},{1,9},{9,1},{2,10},{10,2},{3,11},{11,3},{4,12},{12,4},... | collective-permute-start | bytes 2359304 | tf_op jit(solution)/shard_map/gather2_1_core/ppermute | solution.py:97
  143.1 7.2 %collective-permute-start.24 = (bf16[128,3072]{1,0:T(8,128)(2,1)S(1)}, bf16[128,3072]{1,0:T(8,128)(2,1)S(1)}, u32[]{:S(2)}, u32[]{:S(2)}) collective-permute-start(bf16[128,3072]{1,0:T(8,128)(2,1)S(1)} %collective-permute-done.23.refs_4_.refs_2_), channel_id=1, source_target_pairs={{0,8},{8,0},{1,9},{9,1},{2,10},{10,2},{3,11},{11,3},{4,12},{12,4},... | collective-permute-start | bytes 2359304 | tf_op jit(solution)/shard_map/gather2_2_core/ppermute | solution.py:97
  147.5 12.3 %collective-permute-start.31 = (bf16[64,3072]{1,0:T(8,128)(2,1)S(1)}, bf16[64,3072]{1,0:T(8,128)(2,1)S(1)}, u32[]{:S(2)}, u32[]{:S(2)}) collective-permute-start(bf16[64,3072]{1,0:T(8,128)(2,1)S(1)} %get-tuple-element.69), channel_id=1, source_target_pairs={{0,64},{64,0},{1,65},{65,1},{2,66},{66,2},{3,67},{67,3},{4,68},{68... | collective-permute-start | bytes 1179656 | tf_op jit(solution)/shard_map/gather2_z/ppermute | solution.py:90
  149.5 6.2 %collective-permute-start.29 = (bf16[32,3072]{1,0:T(8,128)(2,1)S(1)}, bf16[32,3072]{1,0:T(8,128)(2,1)S(1)}, u32[]{:S(2)}, u32[]{:S(2)}) collective-permute-start(bf16[32,3072]{1,0:T(8,128)(2,1)S(1)} %get-tuple-element.67), channel_id=1, source_target_pairs={{0,16},{16,0},{32,48},{48,32},{1,17},{17,1},{33,49},{49,33},{2,18}... | collective-permute-start | bytes 589832 | tf_op jit(solution)/shard_map/gather2_p1/ppermute | solution.py:92
  149.5 7.2 %collective-permute-start.30 = (bf16[32,3072]{1,0:T(8,128)(2,1)S(1)}, bf16[32,3072]{1,0:T(8,128)(2,1)S(1)}, u32[]{:S(2)}, u32[]{:S(2)}) collective-permute-start(bf16[32,3072]{1,0:T(8,128)(2,1)S(1)} %get-tuple-element.68), channel_id=1, source_target_pairs={{0,48},{16,32},{32,16},{48,0},{1,49},{17,33},{33,17},{49,1},{2,50}... | collective-permute-start | bytes 589832 | tf_op jit(solution)/shard_map/gather2_p3/ppermute | solution.py:92
  (2 other events, 22.8 us)

commit v3 on v2

--- a/solution.py
+++ b/solution.py
@@ -28,14 +28,24 @@
 
 REDUCE = (
     {
-        Z: ((1, 2, 1), (1, 1, 1), (1, 2, 2), (1, 3, 2)),
-        P1: ((1, 2, 0), (0, 2, 0), (1, 1, 0), (0, 1, 0)),
-        P3: ((1, 2, 3), (0, 2, 3), (1, 3, 3), (0, 3, 3)),
-    },
-    {
-        Z: ((1, 0, 1), (1, 0, 2), (1, 3, 1), (1, 1, 2)),
-        P1: ((1, 1, 3), (0, 1, 3), (0, 2, 1), (0, 1, 1)),
-        P3: ((1, 3, 0), (0, 3, 0), (0, 2, 2), (0, 3, 2)),
+        Z: ((1, 2, 1), (1, 2, 2)),
+        P1: ((1, 2, 0), (0, 2, 0)),
+        P3: ((1, 2, 3), (0, 2, 3)),
+    },
+    {
+        Z: ((1, 1, 1), (1, 3, 2)),
+        P1: ((1, 1, 0), (0, 1, 0)),
+        P3: ((1, 3, 3), (0, 3, 3)),
+    },
+    {
+        Z: ((1, 3, 1), (1, 1, 2)),
+        P1: ((0, 2, 1), (1, 1, 3)),
+        P3: ((0, 2, 2), (1, 3, 0)),
+    },
+    {
+        Z: ((1, 0, 1), (1, 0, 2)),
+        P1: ((0, 1, 3), (0, 1, 1)),
+        P3: ((0, 3, 0), (0, 3, 2)),
     },
     {
         Z: ((1, 0, 0), (1, 0, 3)),
@@ -43,6 +53,7 @@
         P3: ((0, 3, 1),),
     },
 )
+BUILT_TOGETHER = ((0, 1), (2,), (3,), (4,))
 CORE_PARTS = (
     (
         (
@@ -57,10 +68,8 @@
         ),
     ),
     (
-        ((1, 1, 32, 32), (1, 1, 96, 32), (1, 3, 0, 32), (1, 3, 64, 32)),
-        ((0, 1, 32, 64), (0, 2, 64, 64)),
-        ((0, 3, 0, 32), (0, 3, 96, 32), (1, 0, 64, 64)),
-        ((0, 1, 96, 32), (0, 3, 64, 32), (1, 0, 0, 64)),
+        ((1, 1, 32, 32), (1, 1, 96, 32), (1, 3, 0, 32), (1, 3, 64, 32), (0, 2, 64, 64)),
+        ((1, 0, 0, 128), (0, 1, 32, 96), (0, 3, 0, 32), (0, 3, 64, 64)),
         ((0, 0, 0, 128),),
     ),
 )
@@ -129,21 +138,21 @@
     return pl.CostEstimate(flops=0, bytes_accessed=rows * width * 2, transcendentals=0)
 
 
-def fetch(grad, table, parts, after, name):
+def fetch(grad, table, parts, other, after, name):
     width = grad.shape[-1]
-    sizes = [sum(n for _, _, _, n in part) for part in parts] * 2
-    n_copies = 2 * sum(len(part) for part in parts)
+    sizes = [sum(n for _, _, _, n in part) for part in parts]
+    n_copies = sum(len(part) for part in parts)
     before = [] if after is None else [after]
 
     def kernel(table_ref, grad_ref, *refs):
         outs, sem = refs[len(before) : -1], refs[-1]
         copies = []
-        for i, part in enumerate(parts * 2):
-            other, row = int(i < len(parts)), 0
+        for out, part in zip(outs, parts):
+            row = 0
             for de, dy, first, n in part:
                 copy = pltpu.make_async_copy(
                     grad_ref.at[pl.ds(block_row(table_ref, slot(de, dy, other), first), n)],
-                    outs[i].at[pl.ds(row, n)],
+                    out.at[pl.ds(row, n)],
                     sem.at[len(copies)],
                 )
                 copy.start()
@@ -262,26 +271,32 @@
     held = {}
     grad = pltpu.with_memory_space_constraint(grad, pltpu.HBM)
 
-    def cross(parts, after, name):
-        arrays = fetch(grad, table, parts, after, name)
-        for k, part in enumerate(parts):
-            got = to_other_core(arrays[k], f"{name}_{k}")
+    def cross(parts, others, owns, name):
+        for k, (part, other, own) in enumerate(zip(parts, others, owns)):
+            got = to_other_core(other, f"{name}_{k}")
             row = 0
             for de, dy, first, n in part:
                 for q in range(4):
                     if first <= START[q] < first + n:
                         at = row + START[q] - first
-                        held[de, dy, q] = [(arrays[len(parts) + k], at), (got, at)]
+                        held[de, dy, q] = [(own, at), (got, at)]
                 row += n
 
-    cross(CORE_PARTS[0], None, "fetch0")
-    for k, plan in enumerate(REDUCE):
-        messages = build([[(SIZE[seg[2]], held[seg]) for seg in segs] for segs in plan.values()], f"sum{k}")
-        if k == 0:
-            cross(CORE_PARTS[1], messages[0], "fetch1")
-        for (link, segs), x in zip(plan.items(), messages):
+    first, second = CORE_PARTS
+    others = fetch(grad, table, first, 1, None, "fetch0")
+    owns = fetch(grad, table, first, 0, others[0], "fetch1")
+    cross(first, others, owns, "first")
+    others = fetch(grad, table, second, 1, owns[0], "fetch2")
+    for rounds in BUILT_TOGETHER:
+        plan = [item for k in rounds for item in REDUCE[k].items()]
+        lists = [[(SIZE[seg[2]], held[seg]) for seg in segs] for _, segs in plan]
+        messages = build(lists, f"sum{rounds[0]}")
+        if rounds[0] == 0:
+            owns = fetch(grad, table, second, 0, messages[0], "fetch3")
+            cross(second, others, owns, "second")
+        for k, ((link, segs), x) in enumerate(zip(plan, messages)):
             at = layout(segs)
-            got = send(link, x, f"reduce{k}")
+            got = send(link, x, f"reduce{rounds[k // 3]}")
             for seg in segs:
                 held[over(link, seg)].append((got, at[seg]))
 
@@ -312,7 +327,7 @@
             messages = [own] * len(plan)
         else:
             lists = plan.values()
-            messages = build([[(SIZE[s[2]], [held[s]]) for s in segs] for segs in lists], f"copy{k}", after=token)
+            messages = build([[(SIZE[s[2]], [held[s]]) for s in segs] for segs in lists], f"copy{k}", after=[x for x, _ in news])
         came = []
         for (link, segs), x in zip(plan.items(), messages):
             at = layout(segs)
@@ -323,7 +338,7 @@
             for i, (x, segs) in enumerate(news):
                 pieces.extend(runs_of(x, to_other_core(x, f"gather{k}_{i}"), segs))
             out, mark = place(out, table, pieces, f"place{k}")
-            token = (mark,)
+            token = token or (mark,)
         for x, segs in came:
             held.update({seg: (x, row) for seg, row in segs})
         news = came if k > 0 else news + came

time: 165 us -> 151 us (0.915)
  waiting for transfers between devices: 87 us -> 57 us
  starting transfers between devices: 37.6 us -> 47.5 us
  Pallas kernels: 18 us -> 21.5 us
  blocking collectives: 15.1 us -> 17.8 us
    ppermute x12 -> x16, waiting for transfers between devices: 41.8 us -> 25.4 us  [_send(): return lax.ppermute(x, 'dp_0', [(i, i ^ flip) for i in range(4)])]
    ppermute x6 -> x8, waiting for transfers between devices: 38.3 us -> 30.7 us  [_send(): return lax.ppermute(x, 'ends', [(0, 1), (1, 0)])]
    ppermute x6 -> x8, starting transfers between devices: 7.84 us -> 14.9 us  [_send(): return lax.ppermute(x, 'ends', [(0, 1), (1, 0)])]
    ppermute x14 -> x12, waiting for transfers between devices: 6.11 us -> 0.03 us  [to_other_core(): return lax.ppermute(x, 'dp_1', [(0, 1), (1, 0)])]
    ppermute x12 -> x16, starting transfers between devices: 9.7 us -> 13.4 us  [_send(): return lax.ppermute(x, 'dp_0', [(i, i ^ flip) for i in range(4)])]
    pallas_call x2 -> x4, Pallas kernels: 7.12 us -> 10.1 us  [fetch(): pl.pallas_call(kernel, out_shape=[pltpu.VMEM((rows, width), jnp.bfloat16)...]
    all_to_all x1, blocking collectives: 15.1 us -> 17.8 us  [total_over_all(): lax.all_to_all(jnp.broadcast_to(x, (n, *x.shape)), axes, 0, 0)]
    ppermute x14 -> x12, starting transfers between devices: 18 us -> 17.4 us  [to_other_core(): return lax.ppermute(x, 'dp_1', [(0, 1), (1, 0)])]
  transfers between devices with their start and end apart: 33 -> 37, of which waited for: 15 -> 13; matrix products, arithmetic and copies ran while one was open for 0% -> 0% of each run, Pallas kernels for 7% -> 11%
where the time goes in v3:
time: 151 us
  waiting for transfers between devices  57 us (38%)
  starting transfers between devices  47.5 us (31%)
  Pallas kernels  21.5 us (14%)
  blocking collectives  17.8 us (12%)
  other arithmetic  5.55 us (4%)
  between operations  1.74 us (1%)
    ppermute x8, waiting for transfers between devices, _send(): return lax.ppermute(x, 'ends', [(0, 1), (1, 0)])  30.7 us
    ppermute x16, waiting for transfers between devices, _send(): return lax.ppermute(x, 'dp_0', [(i, i ^ flip) for i in range(4)])  25.4 us
    all_to_all x1, blocking collectives, total_over_all(): lax.all_to_all(jnp.broadcast_to(x, (n, *x.shape)), axes, 0, 0)  17.8 us
    ppermute x12, starting transfers between devices, to_other_core(): return lax.ppermute(x, 'dp_1', [(0, 1), (1, 0)])  17.4 us
    ppermute x8, starting transfers between devices, _send(): return lax.ppermute(x, 'ends', [(0, 1), (1, 0)])  14.9 us
    ppermute x16, starting transfers between devices, _send(): return lax.ppermute(x, 'dp_0', [(i, i ^ flip) for i in range(4)])  13.4 us
    pallas_call x4, Pallas kernels, fetch(): pl.pallas_call(kernel, out_shape=[pltpu.VMEM((rows, width), jnp.bfloat16)...  10.1 us
    pallas_call x3, Pallas kernels, place(): pl.pallas_call(kernel, out_shape=[jax.ShapeDtypeStruct((2048, width), jnp...  8.99 us
  transfers between devices with their start and end apart: 37, of which 13 were waited for; matrix products, arithmetic and copies ran while one was open for 0% of the time, Pallas kernels for 11%

profile of v3, /device:TPU:1, one launch (start us, length us, event | category | flops | bytes accessed | tf_op | source)
XLA Modules:
  0.0 151.2 jit_solution(3790612348009853935)
XLA Ops:
  0.8 2.2 %fetch0.1.refs_0_ = bf16[384,3072]{1,0:T(8,128)(2,1)S(1)} custom-call(s32[16]{0:T(128)S(1)} %stack.67.table_ref, bf16[2048,3072]{1,0:T(8,128)(2,1)} %bitcast.51), custom_call_target="tpu_custom_call" | custom-call | bytes 4718592 | tf_op jit(solution)/shard_map/fetch0/pallas_call | solution.py:164
  4.5 2.2 %fetch1.1.refs_0_ = bf16[384,3072]{1,0:T(8,128)(2,1)S(1)} custom-call(s32[16]{0:T(128)S(1)} %stack.67.table_ref, bf16[2048,3072]{1,0:T(8,128)(2,1)} %bitcast.52, bf16[384,3072]{1,0:T(8,128)(2,1)S(1)} %fetch0.1.refs_0_), custom_call_target="tpu_custom_call" | custom-call | bytes 4718592 | tf_op jit(solution)/shard_map/fetch1/pallas_call | solution.py:164
  6.7 2.8 %fetch2.1 = (bf16[192,3072]{1,0:T(8,128)(2,1)S(1)}, bf16[320,3072]{1,0:T(8,128)(2,1)S(1)}, bf16[128,3072]{1,0:T(8,128)(2,1)S(1)}) custom-call(s32[16]{0:T(128)S(1)} %stack.67.table_ref, bf16[2048,3072]{1,0:T(8,128)(2,1)} %bitcast.53, bf16[384,3072]{1,0:T(8,128)(2,1)S(1)} %fetch1.1.refs_0_), custom_call_target="tpu_custom_call" | custom-call | bytes 7864320 | tf_op jit(solution)/shard_map/fetch2/pallas_call | solution.py:164
  10.6 2.9 %collective-permute-start.4 = (bf16[64,3072]{1,0:T(8,128)(2,1)S(1)}, bf16[64,3072]{1,0:T(8,128)(2,1)S(1)}, u32[]{:S(2)}, u32[]{:S(2)}) collective-permute-start(bf16[64,3072]{1,0:T(8,128)(2,1)S(1)} %get-tuple-element.43), channel_id=1, source_target_pairs={{0,48},{16,32},{32,16},{48,0},{1,49},{17,33},{33,17},{49,1},{2,50}... | collective-permute-start | bytes 1179656 | tf_op jit(solution)/shard_map/reduce0_p3/ppermute | solution.py:101
  13.6 3.6 %collective-permute-start.9 = (bf16[64,3072]{1,0:T(8,128)(2,1)S(1)}, bf16[64,3072]{1,0:T(8,128)(2,1)S(1)}, u32[]{:S(2)}, u32[]{:S(2)}) collective-permute-start(bf16[64,3072]{1,0:T(8,128)(2,1)S(1)} %get-tuple-element.37.refs_0_), channel_id=1, source_target_pairs={{0,64},{64,0},{1,65},{65,1},{2,66},{66,2},{3,67},{67,3},{4,68},{68... | collective-permute-start | bytes 1179656 | tf_op jit(solution)/shard_map/reduce0_z/ppermute | solution.py:99
  18.1 4.8 %collective-permute-done.4.refs_2_.refs_3_ = bf16[64,3072]{1,0:T(8,128)(2,1)S(1)} collective-permute-done((bf16[64,3072]{1,0:T(8,128)(2,1)S(1)}, bf16[64,3072]{1,0:T(8,128)(2,1)S(1)}, u32[]{:S(2)}, u32[]{:S(2)}) %collective-permute-start.4) | collective-permute-done | bytes 393248 | tf_op jit(solution)/shard_map/reduce0_p3/ppermute | solution.py:101
  22.9 3.5 %collective-permute-start.5 = (bf16[64,3072]{1,0:T(8,128)(2,1)S(1)}, bf16[64,3072]{1,0:T(8,128)(2,1)S(1)}, u32[]{:S(2)}, u32[]{:S(2)}) collective-permute-start(bf16[64,3072]{1,0:T(8,128)(2,1)S(1)} %get-tuple-element.44), channel_id=1, source_target_pairs={{0,64},{64,0},{1,65},{65,1},{2,66},{66,2},{3,67},{67,3},{4,68},{68... | collective-permute-start | bytes 1179656 | tf_op jit(solution)/shard_map/reduce1_z/ppermute | solution.py:99
  26.4 1.5 %collective-permute-start.1 = (bf16[128,3072]{1,0:T(8,128)(2,1)S(1)}, bf16[128,3072]{1,0:T(8,128)(2,1)S(1)}, u32[]{:S(2)}, u32[]{:S(2)}) collective-permute-start(bf16[128,3072]{1,0:T(8,128)(2,1)S(1)} %get-tuple-element.39), channel_id=1, source_target_pairs={{0,8},{8,0},{1,9},{9,1},{2,10},{10,2},{3,11},{11,3},{4,12},{12,4},... | collective-permute-start | bytes 2359304 | tf_op jit(solution)/shard_map/second_2_core/ppermute | solution.py:106
  28.0 2.8 %fetch3.1 = (bf16[192,3072]{1,0:T(8,128)(2,1)S(1)}, bf16[320,3072]{1,0:T(8,128)(2,1)S(1)}, bf16[128,3072]{1,0:T(8,128)(2,1)S(1)}) custom-call(s32[16]{0:T(128)S(1)} %stack.67.table_ref, bf16[2048,3072]{1,0:T(8,128)(2,1)} %bitcast.54, bf16[64,3072]{1,0:T(8,128)(2,1)S(1)} %get-tuple-element.37.refs_0_), custom_call_target="tpu_custom_call" | custom-call | bytes 7864320 | tf_op jit(solution)/shard_map/fetch3/pallas_call | solution.py:164
  31.2 2.7 %collective-permute-start.10 = (bf16[64,3072]{1,0:T(8,128)(2,1)S(1)}, bf16[64,3072]{1,0:T(8,128)(2,1)S(1)}, u32[]{:S(2)}, u32[]{:S(2)}) collective-permute-start(bf16[64,3072]{1,0:T(8,128)(2,1)S(1)} %get-tuple-element.49), channel_id=1, source_target_pairs={{0,48},{16,32},{32,16},{48,0},{1,49},{17,33},{33,17},{49,1},{2,50}... | collective-permute-start | bytes 1179656 | tf_op jit(solution)/shard_map/reduce2_p3/ppermute | solution.py:101
  34.8 2.4 %collective-permute-start.13 = (bf16[64,3072]{1,0:T(8,128)(2,1)S(1)}, bf16[64,3072]{1,0:T(8,128)(2,1)S(1)}, u32[]{:S(2)}, u32[]{:S(2)}) collective-permute-start(bf16[64,3072]{1,0:T(8,128)(2,1)S(1)} %get-tuple-element.52), channel_id=1, source_target_pairs={{0,64},{64,0},{1,65},{65,1},{2,66},{66,2},{3,67},{67,3},{4,68},{68... | collective-permute-start | bytes 1179656 | tf_op jit(solution)/shard_map/reduce2_z/ppermute | solution.py:99
  38.9 3.5 %collective-permute-done.10.refs_3_ = bf16[64,3072]{1,0:T(8,128)(2,1)S(1)} collective-permute-done((bf16[64,3072]{1,0:T(8,128)(2,1)S(1)}, bf16[64,3072]{1,0:T(8,128)(2,1)S(1)}, u32[]{:S(2)}, u32[]{:S(2)}) %collective-permute-start.10) | collective-permute-done | bytes 393248 | tf_op jit(solution)/shard_map/reduce2_p3/ppermute | solution.py:101
  42.9 4.1 %collective-permute-done.12.refs_5_ = bf16[64,3072]{1,0:T(8,128)(2,1)S(1)} collective-permute-done((bf16[64,3072]{1,0:T(8,128)(2,1)S(1)}, bf16[64,3072]{1,0:T(8,128)(2,1)S(1)}, u32[]{:S(2)}, u32[]{:S(2)}) %collective-permute-start.12) | collective-permute-done | bytes 393248 | tf_op jit(solution)/shard_map/reduce2_p1/ppermute | solution.py:101
  47.0 2.7 %collective-permute-start.7 = (bf16[64,3072]{1,0:T(8,128)(2,1)S(1)}, bf16[64,3072]{1,0:T(8,128)(2,1)S(1)}, u32[]{:S(2)}, u32[]{:S(2)}) collective-permute-start(bf16[64,3072]{1,0:T(8,128)(2,1)S(1)} %get-tuple-element.46), channel_id=1, source_target_pairs={{0,48},{16,32},{32,16},{48,0},{1,49},{17,33},{33,17},{49,1},{2,50}... | collective-permute-start | bytes 1179656 | tf_op jit(solution)/shard_map/reduce3_p3/ppermute | solution.py:101
  50.3 5.1 %collective-permute-done.15.refs_6_ = bf16[64,3072]{1,0:T(8,128)(2,1)S(1)} collective-permute-done((bf16[64,3072]{1,0:T(8,128)(2,1)S(1)}, bf16[64,3072]{1,0:T(8,128)(2,1)S(1)}, u32[]{:S(2)}, u32[]{:S(2)}) %collective-permute-start.15) | collective-permute-done | bytes 393248 | tf_op jit(solution)/shard_map/reduce3_p1/ppermute | solution.py:101
  55.4 2.2 %collective-permute-done.7.refs_3_ = bf16[64,3072]{1,0:T(8,128)(2,1)S(1)} collective-permute-done((bf16[64,3072]{1,0:T(8,128)(2,1)S(1)}, bf16[64,3072]{1,0:T(8,128)(2,1)S(1)}, u32[]{:S(2)}, u32[]{:S(2)}) %collective-permute-start.7) | collective-permute-done | bytes 393248 | tf_op jit(solution)/shard_map/reduce3_p3/ppermute | solution.py:101
  57.6 4.2 %collective-permute-done.17.refs_8_ = bf16[32,3072]{1,0:T(8,128)(2,1)S(1)} collective-permute-done((bf16[32,3072]{1,0:T(8,128)(2,1)S(1)}, bf16[32,3072]{1,0:T(8,128)(2,1)S(1)}, u32[]{:S(2)}, u32[]{:S(2)}) %collective-permute-start.17) | collective-permute-done | bytes 196640 | tf_op jit(solution)/shard_map/reduce4_p3/ppermute | solution.py:101
  63.6 1.8 %collective-permute-start.19 = (f32[1,128]{1,0:T(1,128)S(1)}, f32[1,128]{1,0:T(1,128)S(1)}, u32[]{:S(2)}, u32[]{:S(2)}) collective-permute-start(f32[1,128]{1,0:T(1,128)S(1)} %bitcast.57), channel_id=1, source_target_pairs={{0,8},{8,0},{1,9},{9,1},{2,10},{10,2},{3,11},{11,3},{4,12},{12,4},... | collective-permute-start | bytes 1544 | tf_op jit(solution)/shard_map/ppermute | solution.py:353
  66.2 17.8 %all_to_all.5 = f32[64,1,128]{2,1,0:T(1,128)S(1)} all-to-all(f32[64,1,128]{2,1,0:T(1,128)S(1)} %broadcast_in_dim.16), channel_id=1, replica_groups=mesh['ends'=2,'dp_0'=4,'dp_1'=2,'tp_0'=2,'tp_1'=4] {'ends','dp_0','tp_0'..., dimensions={0} | all-to-all | bytes 65536 | tf_op jit(solution)/shard_map/all_to_all | solution.py:356
  85.4 4.9 %fusion.5 = (bf16[128,3072]{1,0:T(8,128)(2,1)S(1)}, f32[128,3072]{1,0:T(8,128)}, f32[1,128,3072]{2,1,0:T(8,128)}, f32[1,128,3072]{2,1,0:T(8,128)}) fusion(f32[1,128,3072]{2,1,0:T(8,128)S(1)} %copy-done, f32[128,3072]{1,0:T(8,128)S(1)} %get-tuple-element.59, f32[]{:T(128)S(6)} %min_shard_map.3, f32[1,128,3072]{2,1,0:T(8,128)} %param.6, f32[1,128,3072]{2,1,0:T(8,128)} %param.5), kind=kLoop, calls=%fused_computation.10 | loop fusion | flops 6684672 | bytes 11796484 | tf_op jit(solution)/shard_map/convert_element_type | solution.py:382
  92.4 16.7 %collective-permute-done.21.refs_2_.refs_1_ = bf16[128,3072]{1,0:T(8,128)(2,1)S(1)} collective-permute-done((bf16[128,3072]{1,0:T(8,128)(2,1)S(1)}, bf16[128,3072]{1,0:T(8,128)(2,1)S(1)}, u32[]{:S(2)}, u32[]{:S(2)}) %collective-permute-start.21) | collective-permute-done | bytes 786464 | tf_op jit(solution)/shard_map/gather0_z/ppermute | solution.py:99
  109.8 2.2 %collective-permute-start.27 = (bf16[128,3072]{1,0:T(8,128)(2,1)S(1)}, bf16[128,3072]{1,0:T(8,128)(2,1)S(1)}, u32[]{:S(2)}, u32[]{:S(2)}) collective-permute-start(bf16[128,3072]{1,0:T(8,128)(2,1)S(1)} %get-tuple-element.61), channel_id=1, source_target_pairs={{0,64},{64,0},{1,65},{65,1},{2,66},{66,2},{3,67},{67,3},{4,68},{68... | collective-permute-start | bytes 2359304 | tf_op jit(solution)/shard_map/gather1_z/ppermute | solution.py:99
  112.8 3.9 %collective-permute-start.20 = (bf16[128,3072]{1,0:T(8,128)(2,1)S(1)}, bf16[128,3072]{1,0:T(8,128)(2,1)S(1)}, u32[]{:S(2)}, u32[]{:S(2)}) collective-permute-start(bf16[128,3072]{1,0:T(8,128)(2,1)S(1)} %get-tuple-element.70.refs_0_), channel_id=1, source_target_pairs={{0,8},{8,0},{1,9},{9,1},{2,10},{10,2},{3,11},{11,3},{4,12},{12,4},... | collective-permute-start | bytes 2359304 | tf_op jit(solution)/shard_map/gather1_0_core/ppermute | solution.py:106
  116.7 10.7 %collective-permute-done.27.refs_0_ = bf16[128,3072]{1,0:T(8,128)(2,1)S(1)} collective-permute-done((bf16[128,3072]{1,0:T(8,128)(2,1)S(1)}, bf16[128,3072]{1,0:T(8,128)(2,1)S(1)}, u32[]{:S(2)}, u32[]{:S(2)}) %collective-permute-start.27) | collective-permute-done | bytes 786464 | tf_op jit(solution)/shard_map/gather1_z/ppermute | solution.py:99
  127.4 4.1 %collective-permute-start.24 = (bf16[128,3072]{1,0:T(8,128)(2,1)S(1)}, bf16[128,3072]{1,0:T(8,128)(2,1)S(1)}, u32[]{:S(2)}, u32[]{:S(2)}) collective-permute-start(bf16[128,3072]{1,0:T(8,128)(2,1)S(1)} %collective-permute-done.23.refs_4_.refs_2_), channel_id=1, source_target_pairs={{0,8},{8,0},{1,9},{9,1},{2,10},{10,2},{3,11},{11,3},{4,12},{12,4},... | collective-permute-start | bytes 2359304 | tf_op jit(solution)/shard_map/gather1_2_core/ppermute | solution.py:106
  132.0 1.6 %collective-permute-start.32 = (bf16[64,3072]{1,0:T(8,128)(2,1)S(1)}, bf16[64,3072]{1,0:T(8,128)(2,1)S(1)}, u32[]{:S(2)}, u32[]{:S(2)}) collective-permute-start(bf16[64,3072]{1,0:T(8,128)(2,1)S(1)} %get-tuple-element.66), channel_id=1, source_target_pairs={{0,64},{64,0},{1,65},{65,1},{2,66},{66,2},{3,67},{67,3},{4,68},{68... | collective-permute-start | bytes 1179656 | tf_op jit(solution)/shard_map/gather2_z/ppermute | solution.py:99
  134.5 1.6 %collective-permute-start.34 = (bf16[128,3072]{1,0:T(8,128)(2,1)S(1)}, bf16[128,3072]{1,0:T(8,128)(2,1)S(1)}, u32[]{:S(2)}, u32[]{:S(2)}) collective-permute-start(bf16[128,3072]{1,0:T(8,128)(2,1)S(1)} %collective-permute-done.27.refs_0_), channel_id=1, source_target_pairs={{0,8},{8,0},{1,9},{9,1},{2,10},{10,2},{3,11},{11,3},{4,12},{12,4},... | collective-permute-start | bytes 2359304 | tf_op jit(solution)/shard_map/gather2_0_core/ppermute | solution.py:106
  136.3 3.3 %place1.1 = (bf16[2048,3072]{1,0:T(8,128)(2,1)}, bf16[8,128]{1,0:T(8,128)(2,1)S(1)}) custom-call(s32[16]{0:T(128)S(1)} %stack.67.table_ref, bf16[128,3072]{1,0:T(8,128)(2,1)S(1)} %get-tuple-element.70.refs_0_, bf16[128,3072]{1,0:T(8,128)(2,1)S(1)} %collective-permute-done.20.refs_1_, bf16[128,3072]{1,0:T(8,128)(2,1)S(1)} %collective-permute-done.21.refs_2_.refs_1_, ...), custom_call_target="tpu_custom_call" | custom-call | bytes 12582912 | tf_op jit(solution)/shard_map/place1/pallas_call | solution.py:254
  141.0 2.1 %collective-permute-done.32.refs_3_ = bf16[64,3072]{1,0:T(8,128)(2,1)S(1)} collective-permute-done((bf16[64,3072]{1,0:T(8,128)(2,1)S(1)}, bf16[64,3072]{1,0:T(8,128)(2,1)S(1)}, u32[]{:S(2)}, u32[]{:S(2)}) %collective-permute-start.32) | collective-permute-done | bytes 393248 | tf_op jit(solution)/shard_map/gather2_z/ppermute | solution.py:99
  143.1 2.2 %collective-permute-start.33 = (bf16[128,3072]{1,0:T(8,128)(2,1)S(1)}, bf16[128,3072]{1,0:T(8,128)(2,1)S(1)}, u32[]{:S(2)}, u32[]{:S(2)}) collective-permute-start(bf16[128,3072]{1,0:T(8,128)(2,1)S(1)} %copy3.1.refs_0_), channel_id=1, source_target_pairs={{0,8},{8,0},{1,9},{9,1},{2,10},{10,2},{3,11},{11,3},{4,12},{12,4},... | collective-permute-start | bytes 2359304 | tf_op jit(solution)/shard_map/last_core/ppermute | solution.py:106
  145.3 3.4 %place2.1 = (bf16[2048,3072]{1,0:T(8,128)(2,1)}, bf16[8,128]{1,0:T(8,128)(2,1)}) custom-call(s32[16]{0:T(128)S(1)} %stack.67.table_ref, bf16[128,3072]{1,0:T(8,128)(2,1)S(1)} %collective-permute-done.27.refs_0_, bf16[128,3072]{1,0:T(8,128)(2,1)S(1)} %collective-permute-done.34.refs_1_, ...), custom_call_target="tpu_custom_call", output_to_operand_aliasing={{0}: (7, {})} | custom-call | bytes 9437184 | tf_op jit(solution)/shard_map/place2/pallas_call | solution.py:254
  148.8 2.3 %place3.1 = (bf16[2048,3072]{1,0:T(8,128)(2,1)}, bf16[8,128]{1,0:T(8,128)(2,1)}) custom-call(s32[16]{0:T(128)S(1)} %stack.67.table_ref, bf16[128,3072]{1,0:T(8,128)(2,1)S(1)} %copy3.1.refs_0_, bf16[128,3072]{1,0:T(8,128)(2,1)S(1)} %collective-permute-done.33.refs_1_, bf16[2048,3072]{1,0:T(8,128)(2,1)} %get-tuple-element.68.refs_2_), custom_call_target="tpu_custom_call", output_to_operand_aliasing={{0}: (3, {})} | custom-call | bytes 3145728 | tf_op jit(solution)/shard_map/place3/pallas_call | solution.py:254
  (66 shorter events, 17.3 us)
Async XLA Ops:
  3.0 7.1 %collective-permute-start = (bf16[384,3072]{1,0:T(8,128)(2,1)S(1)}, bf16[384,3072]{1,0:T(8,128)(2,1)S(1)}, u32[]{:S(2)}, u32[]{:S(2)}) collective-permute-start(bf16[384,3072]{1,0:T(8,128)(2,1)S(1)} %fetch0.1.refs_0_), channel_id=1, source_target_pairs={{0,8},{8,0},{1,9},{9,1},{2,10},{10,2},{3,11},{11,3},{4,12},{12,4},... | collective-permute-start | bytes 7077896 | tf_op jit(solution)/shard_map/first_0_core/ppermute | solution.py:106
  9.5 21.7 %collective-permute-start.3 = (bf16[320,3072]{1,0:T(8,128)(2,1)S(1)}, bf16[320,3072]{1,0:T(8,128)(2,1)S(1)}, u32[]{:S(2)}, u32[]{:S(2)}) collective-permute-start(bf16[320,3072]{1,0:T(8,128)(2,1)S(1)} %get-tuple-element.42), channel_id=1, source_target_pairs={{0,8},{8,0},{1,9},{9,1},{2,10},{10,2},{3,11},{11,3},{4,12},{12,4},... | collective-permute-start | bytes 5898248 | tf_op jit(solution)/shard_map/second_1_core/ppermute | solution.py:106
  9.6 7.6 %collective-permute-start.8 = (bf16[192,3072]{1,0:T(8,128)(2,1)S(1)}, bf16[192,3072]{1,0:T(8,128)(2,1)S(1)}, u32[]{:S(2)}, u32[]{:S(2)}) collective-permute-start(bf16[192,3072]{1,0:T(8,128)(2,1)S(1)} %get-tuple-element.48), channel_id=1, source_target_pairs={{0,8},{8,0},{1,9},{9,1},{2,10},{10,2},{3,11},{11,3},{4,12},{12,4},... | collective-permute-start | bytes 3538952 | tf_op jit(solution)/shard_map/second_0_core/ppermute | solution.py:106
  10.6 12.3 %collective-permute-start.4 = (bf16[64,3072]{1,0:T(8,128)(2,1)S(1)}, bf16[64,3072]{1,0:T(8,128)(2,1)S(1)}, u32[]{:S(2)}, u32[]{:S(2)}) collective-permute-start(bf16[64,3072]{1,0:T(8,128)(2,1)S(1)} %get-tuple-element.43), channel_id=1, source_target_pairs={{0,48},{16,32},{32,16},{48,0},{1,49},{17,33},{33,17},{49,1},{2,50}... | collective-permute-start | bytes 1179656 | tf_op jit(solution)/shard_map/reduce0_p3/ppermute | solution.py:101
  13.5 12.8 %collective-permute-start.6 = (bf16[64,3072]{1,0:T(8,128)(2,1)S(1)}, bf16[64,3072]{1,0:T(8,128)(2,1)S(1)}, u32[]{:S(2)}, u32[]{:S(2)}) collective-permute-start(bf16[64,3072]{1,0:T(8,128)(2,1)S(1)} %get-tuple-element.45), channel_id=1, source_target_pairs={{0,16},{16,0},{32,48},{48,32},{1,17},{17,1},{33,49},{49,33},{2,18}... | collective-permute-start | bytes 1179656 | tf_op jit(solution)/shard_map/reduce0_p1/ppermute | solution.py:101
  13.6 14.4 %collective-permute-start.9 = (bf16[64,3072]{1,0:T(8,128)(2,1)S(1)}, bf16[64,3072]{1,0:T(8,128)(2,1)S(1)}, u32[]{:S(2)}, u32[]{:S(2)}) collective-permute-start(bf16[64,3072]{1,0:T(8,128)(2,1)S(1)} %get-tuple-element.37.refs_0_), channel_id=1, source_target_pairs={{0,64},{64,0},{1,65},{65,1},{2,66},{66,2},{3,67},{67,3},{4,68},{68... | collective-permute-start | bytes 1179656 | tf_op jit(solution)/shard_map/reduce0_z/ppermute | solution.py:99
  17.2 16.8 %collective-permute-start.11 = (bf16[64,3072]{1,0:T(8,128)(2,1)S(1)}, bf16[64,3072]{1,0:T(8,128)(2,1)S(1)}, u32[]{:S(2)}, u32[]{:S(2)}) collective-permute-start(bf16[64,3072]{1,0:T(8,128)(2,1)S(1)} %get-tuple-element.50), channel_id=1, source_target_pairs={{0,48},{16,32},{32,16},{48,0},{1,49},{17,33},{33,17},{49,1},{2,50}... | collective-permute-start | bytes 1179656 | tf_op jit(solution)/shard_map/reduce1_p3/ppermute | solution.py:101
  22.9 12.0 %collective-permute-start.5 = (bf16[64,3072]{1,0:T(8,128)(2,1)S(1)}, bf16[64,3072]{1,0:T(8,128)(2,1)S(1)}, u32[]{:S(2)}, u32[]{:S(2)}) collective-permute-start(bf16[64,3072]{1,0:T(8,128)(2,1)S(1)} %get-tuple-element.44), channel_id=1, source_target_pairs={{0,64},{64,0},{1,65},{65,1},{2,66},{66,2},{3,67},{67,3},{4,68},{68... | collective-permute-start | bytes 1179656 | tf_op jit(solution)/shard_map/reduce1_z/ppermute | solution.py:99
  26.4 23.9 %collective-permute-start.1 = (bf16[128,3072]{1,0:T(8,128)(2,1)S(1)}, bf16[128,3072]{1,0:T(8,128)(2,1)S(1)}, u32[]{:S(2)}, u32[]{:S(2)}) collective-permute-start(bf16[128,3072]{1,0:T(8,128)(2,1)S(1)} %get-tuple-element.39), channel_id=1, source_target_pairs={{0,8},{8,0},{1,9},{9,1},{2,10},{10,2},{3,11},{11,3},{4,12},{12,4},... | collective-permute-start | bytes 2359304 | tf_op jit(solution)/shard_map/second_2_core/ppermute | solution.py:106
  27.9 10.7 %collective-permute-start.2 = (bf16[64,3072]{1,0:T(8,128)(2,1)S(1)}, bf16[64,3072]{1,0:T(8,128)(2,1)S(1)}, u32[]{:S(2)}, u32[]{:S(2)}) collective-permute-start(bf16[64,3072]{1,0:T(8,128)(2,1)S(1)} %get-tuple-element.40), channel_id=1, source_target_pairs={{0,16},{16,0},{32,48},{48,32},{1,17},{17,1},{33,49},{49,33},{2,18}... | collective-permute-start | bytes 1179656 | tf_op jit(solution)/shard_map/reduce1_p1/ppermute | solution.py:101
  31.2 11.2 %collective-permute-start.10 = (bf16[64,3072]{1,0:T(8,128)(2,1)S(1)}, bf16[64,3072]{1,0:T(8,128)(2,1)S(1)}, u32[]{:S(2)}, u32[]{:S(2)}) collective-permute-start(bf16[64,3072]{1,0:T(8,128)(2,1)S(1)} %get-tuple-element.49), channel_id=1, source_target_pairs={{0,48},{16,32},{32,16},{48,0},{1,49},{17,33},{33,17},{49,1},{2,50}... | collective-permute-start | bytes 1179656 | tf_op jit(solution)/shard_map/reduce2_p3/ppermute | solution.py:101
  34.0 13.0 %collective-permute-start.12 = (bf16[64,3072]{1,0:T(8,128)(2,1)S(1)}, bf16[64,3072]{1,0:T(8,128)(2,1)S(1)}, u32[]{:S(2)}, u32[]{:S(2)}) collective-permute-start(bf16[64,3072]{1,0:T(8,128)(2,1)S(1)} %get-tuple-element.51), channel_id=1, source_target_pairs={{0,16},{16,0},{32,48},{48,32},{1,17},{17,1},{33,49},{49,33},{2,18}... | collective-permute-start | bytes 1179656 | tf_op jit(solution)/shard_map/reduce2_p1/ppermute | solution.py:101
  34.8 14.9 %collective-permute-start.13 = (bf16[64,3072]{1,0:T(8,128)(2,1)S(1)}, bf16[64,3072]{1,0:T(8,128)(2,1)S(1)}, u32[]{:S(2)}, u32[]{:S(2)}) collective-permute-start(bf16[64,3072]{1,0:T(8,128)(2,1)S(1)} %get-tuple-element.52), channel_id=1, source_target_pairs={{0,64},{64,0},{1,65},{65,1},{2,66},{66,2},{3,67},{67,3},{4,68},{68... | collective-permute-start | bytes 1179656 | tf_op jit(solution)/shard_map/reduce2_z/ppermute | solution.py:99
  38.6 16.9 %collective-permute-start.15 = (bf16[64,3072]{1,0:T(8,128)(2,1)S(1)}, bf16[64,3072]{1,0:T(8,128)(2,1)S(1)}, u32[]{:S(2)}, u32[]{:S(2)}) collective-permute-start(bf16[64,3072]{1,0:T(8,128)(2,1)S(1)} %get-tuple-element.54), channel_id=1, source_target_pairs={{0,16},{16,0},{32,48},{48,32},{1,17},{17,1},{33,49},{49,33},{2,18}... | collective-permute-start | bytes 1179656 | tf_op jit(solution)/shard_map/reduce3_p1/ppermute | solution.py:101
  42.4 13.0 %collective-permute-start.16 = (bf16[64,3072]{1,0:T(8,128)(2,1)S(1)}, bf16[64,3072]{1,0:T(8,128)(2,1)S(1)}, u32[]{:S(2)}, u32[]{:S(2)}) collective-permute-start(bf16[64,3072]{1,0:T(8,128)(2,1)S(1)} %get-tuple-element.55), channel_id=1, source_target_pairs={{0,64},{64,0},{1,65},{65,1},{2,66},{66,2},{3,67},{67,3},{4,68},{68... | collective-permute-start | bytes 1179656 | tf_op jit(solution)/shard_map/reduce3_z/ppermute | solution.py:99
  47.0 10.6 %collective-permute-start.7 = (bf16[64,3072]{1,0:T(8,128)(2,1)S(1)}, bf16[64,3072]{1,0:T(8,128)(2,1)S(1)}, u32[]{:S(2)}, u32[]{:S(2)}) collective-permute-start(bf16[64,3072]{1,0:T(8,128)(2,1)S(1)} %get-tuple-element.46), channel_id=1, source_target_pairs={{0,48},{16,32},{32,16},{48,0},{1,49},{17,33},{33,17},{49,1},{2,50}... | collective-permute-start | bytes 1179656 | tf_op jit(solution)/shard_map/reduce3_p3/ppermute | solution.py:101
  50.1 12.9 %collective-permute-start.14 = (bf16[64,3072]{1,0:T(8,128)(2,1)S(1)}, bf16[64,3072]{1,0:T(8,128)(2,1)S(1)}, u32[]{:S(2)}, u32[]{:S(2)}) collective-permute-start(bf16[64,3072]{1,0:T(8,128)(2,1)S(1)} %get-tuple-element.53), channel_id=1, source_target_pairs={{0,64},{64,0},{1,65},{65,1},{2,66},{66,2},{3,67},{67,3},{4,68},{68... | collective-permute-start | bytes 1179656 | tf_op jit(solution)/shard_map/reduce4_z/ppermute | solution.py:99
  50.3 11.6 %collective-permute-start.17 = (bf16[32,3072]{1,0:T(8,128)(2,1)S(1)}, bf16[32,3072]{1,0:T(8,128)(2,1)S(1)}, u32[]{:S(2)}, u32[]{:S(2)}) collective-permute-start(bf16[32,3072]{1,0:T(8,128)(2,1)S(1)} %get-tuple-element.56), channel_id=1, source_target_pairs={{0,48},{16,32},{32,16},{48,0},{1,49},{17,33},{33,17},{49,1},{2,50}... | collective-permute-start | bytes 589832 | tf_op jit(solution)/shard_map/reduce4_p3/ppermute | solution.py:101
  55.4 6.4 %collective-permute-start.18 = (bf16[32,3072]{1,0:T(8,128)(2,1)S(1)}, bf16[32,3072]{1,0:T(8,128)(2,1)S(1)}, u32[]{:S(2)}, u32[]{:S(2)}) collective-permute-start(bf16[32,3072]{1,0:T(8,128)(2,1)S(1)} %get-tuple-element.57), channel_id=1, source_target_pairs={{0,16},{16,0},{32,48},{48,32},{1,17},{17,1},{33,49},{49,33},{2,18}... | collective-permute-start | bytes 589832 | tf_op jit(solution)/shard_map/reduce4_p1/ppermute | solution.py:101
  90.3 18.8 %collective-permute-start.21 = (bf16[128,3072]{1,0:T(8,128)(2,1)S(1)}, bf16[128,3072]{1,0:T(8,128)(2,1)S(1)}, u32[]{:S(2)}, u32[]{:S(2)}) collective-permute-start(bf16[128,3072]{1,0:T(8,128)(2,1)S(1)} %get-tuple-element.70.refs_0_), channel_id=1, source_target_pairs={{0,64},{64,0},{1,65},{65,1},{2,66},{66,2},{3,67},{67,3},{4,68},{68... | collective-permute-start | bytes 2359304 | tf_op jit(solution)/shard_map/gather0_z/ppermute | solution.py:99
  91.4 17.8 %collective-permute-start.23 = (bf16[128,3072]{1,0:T(8,128)(2,1)S(1)}, bf16[128,3072]{1,0:T(8,128)(2,1)S(1)}, u32[]{:S(2)}, u32[]{:S(2)}) collective-permute-start(bf16[128,3072]{1,0:T(8,128)(2,1)S(1)} %get-tuple-element.70.refs_0_), channel_id=1, source_target_pairs={{0,16},{16,0},{32,48},{48,32},{1,17},{17,1},{33,49},{49,33},{2,18}... | collective-permute-start | bytes 2359304 | tf_op jit(solution)/shard_map/gather0_p1/ppermute | solution.py:101
  91.7 18.0 %collective-permute-start.25 = (bf16[128,3072]{1,0:T(8,128)(2,1)S(1)}, bf16[128,3072]{1,0:T(8,128)(2,1)S(1)}, u32[]{:S(2)}, u32[]{:S(2)}) collective-permute-start(bf16[128,3072]{1,0:T(8,128)(2,1)S(1)} %get-tuple-element.70.refs_0_), channel_id=1, source_target_pairs={{0,48},{16,32},{32,16},{48,0},{1,49},{17,33},{33,17},{49,1},{2,50}... | collective-permute-start | bytes 2359304 | tf_op jit(solution)/shard_map/gather0_p3/ppermute | solution.py:101
  109.8 17.6 %collective-permute-start.27 = (bf16[128,3072]{1,0:T(8,128)(2,1)S(1)}, bf16[128,3072]{1,0:T(8,128)(2,1)S(1)}, u32[]{:S(2)}, u32[]{:S(2)}) collective-permute-start(bf16[128,3072]{1,0:T(8,128)(2,1)S(1)} %get-tuple-element.61), channel_id=1, source_target_pairs={{0,64},{64,0},{1,65},{65,1},{2,66},{66,2},{3,67},{67,3},{4,68},{68... | collective-permute-start | bytes 2359304 | tf_op jit(solution)/shard_map/gather1_z/ppermute | solution.py:99
  112.0 19.5 %collective-permute-start.28 = (bf16[128,3072]{1,0:T(8,128)(2,1)S(1)}, bf16[128,3072]{1,0:T(8,128)(2,1)S(1)}, u32[]{:S(2)}, u32[]{:S(2)}) collective-permute-start(bf16[128,3072]{1,0:T(8,128)(2,1)S(1)} %get-tuple-element.62), channel_id=1, source_target_pairs={{0,16},{16,0},{32,48},{48,32},{1,17},{17,1},{33,49},{49,33},{2,18}... | collective-permute-start | bytes 2359304 | tf_op jit(solution)/shard_map/gather1_p1/ppermute | solution.py:101
  112.0 20.0 %collective-permute-start.29 = (bf16[128,3072]{1,0:T(8,128)(2,1)S(1)}, bf16[128,3072]{1,0:T(8,128)(2,1)S(1)}, u32[]{:S(2)}, u32[]{:S(2)}) collective-permute-start(bf16[128,3072]{1,0:T(8,128)(2,1)S(1)} %get-tuple-element.63), channel_id=1, source_target_pairs={{0,48},{16,32},{32,16},{48,0},{1,49},{17,33},{33,17},{49,1},{2,50}... | collective-permute-start | bytes 2359304 | tf_op jit(solution)/shard_map/gather1_p3/ppermute | solution.py:101
  112.8 20.8 %collective-permute-start.20 = (bf16[128,3072]{1,0:T(8,128)(2,1)S(1)}, bf16[128,3072]{1,0:T(8,128)(2,1)S(1)}, u32[]{:S(2)}, u32[]{:S(2)}) collective-permute-start(bf16[128,3072]{1,0:T(8,128)(2,1)S(1)} %get-tuple-element.70.refs_0_), channel_id=1, source_target_pairs={{0,8},{8,0},{1,9},{9,1},{2,10},{10,2},{3,11},{11,3},{4,12},{12,4},... | collective-permute-start | bytes 2359304 | tf_op jit(solution)/shard_map/gather1_0_core/ppermute | solution.py:106
  116.7 16.9 %collective-permute-start.22 = (bf16[128,3072]{1,0:T(8,128)(2,1)S(1)}, bf16[128,3072]{1,0:T(8,128)(2,1)S(1)}, u32[]{:S(2)}, u32[]{:S(2)}) collective-permute-start(bf16[128,3072]{1,0:T(8,128)(2,1)S(1)} %collective-permute-done.21.refs_2_.refs_1_), channel_id=1, source_target_pairs={{0,8},{8,0},{1,9},{9,1},{2,10},{10,2},{3,11},{11,3},{4,12},{12,4},... | collective-permute-start | bytes 2359304 | tf_op jit(solution)/shard_map/gather1_1_core/ppermute | solution.py:106
  127.4 7.1 %collective-permute-start.24 = (bf16[128,3072]{1,0:T(8,128)(2,1)S(1)}, bf16[128,3072]{1,0:T(8,128)(2,1)S(1)}, u32[]{:S(2)}, u32[]{:S(2)}) collective-permute-start(bf16[128,3072]{1,0:T(8,128)(2,1)S(1)} %collective-permute-done.23.refs_4_.refs_2_), channel_id=1, source_target_pairs={{0,8},{8,0},{1,9},{9,1},{2,10},{10,2},{3,11},{11,3},{4,12},{12,4},... | collective-permute-start | bytes 2359304 | tf_op jit(solution)/shard_map/gather1_2_core/ppermute | solution.py:106
  132.0 11.0 %collective-permute-start.32 = (bf16[64,3072]{1,0:T(8,128)(2,1)S(1)}, bf16[64,3072]{1,0:T(8,128)(2,1)S(1)}, u32[]{:S(2)}, u32[]{:S(2)}) collective-permute-start(bf16[64,3072]{1,0:T(8,128)(2,1)S(1)} %get-tuple-element.66), channel_id=1, source_target_pairs={{0,64},{64,0},{1,65},{65,1},{2,66},{66,2},{3,67},{67,3},{4,68},{68... | collective-permute-start | bytes 1179656 | tf_op jit(solution)/shard_map/gather2_z/ppermute | solution.py:99
  133.6 7.3 %collective-permute-start.31 = (bf16[32,3072]{1,0:T(8,128)(2,1)S(1)}, bf16[32,3072]{1,0:T(8,128)(2,1)S(1)}, u32[]{:S(2)}, u32[]{:S(2)}) collective-permute-start(bf16[32,3072]{1,0:T(8,128)(2,1)S(1)} %get-tuple-element.65), channel_id=1, source_target_pairs={{0,48},{16,32},{32,16},{48,0},{1,49},{17,33},{33,17},{49,1},{2,50}... | collective-permute-start | bytes 589832 | tf_op jit(solution)/shard_map/gather2_p3/ppermute | solution.py:101
  134.5 10.8 %collective-permute-start.34 = (bf16[128,3072]{1,0:T(8,128)(2,1)S(1)}, bf16[128,3072]{1,0:T(8,128)(2,1)S(1)}, u32[]{:S(2)}, u32[]{:S(2)}) collective-permute-start(bf16[128,3072]{1,0:T(8,128)(2,1)S(1)} %collective-permute-done.27.refs_0_), channel_id=1, source_target_pairs={{0,8},{8,0},{1,9},{9,1},{2,10},{10,2},{3,11},{11,3},{4,12},{12,4},... | collective-permute-start | bytes 2359304 | tf_op jit(solution)/shard_map/gather2_0_core/ppermute | solution.py:106
  136.2 9.1 %collective-permute-start.35 = (bf16[128,3072]{1,0:T(8,128)(2,1)S(1)}, bf16[128,3072]{1,0:T(8,128)(2,1)S(1)}, u32[]{:S(2)}, u32[]{:S(2)}) collective-permute-start(bf16[128,3072]{1,0:T(8,128)(2,1)S(1)} %collective-permute-done.28.refs_1_.refs_2_), channel_id=1, source_target_pairs={{0,8},{8,0},{1,9},{9,1},{2,10},{10,2},{3,11},{11,3},{4,12},{12,4},... | collective-permute-start | bytes 2359304 | tf_op jit(solution)/shard_map/gather2_1_core/ppermute | solution.py:106
  (6 other events, 46.9 us)

commit v4 on v3

--- a/solution.py
+++ b/solution.py
@@ -187,7 +187,9 @@
 
     def kernel(*refs):
         ins, outs = refs[: len(arrays)], refs[len(arrays) :]
-        total = None
+        total, copies = None, []
+        if squares:
+            (sum_ref, square_ref, scratch, sem), outs = outs, outs[2:3]
         for out, out_ref in zip(plan, outs):
             at = 0
             for n, sources in out:
@@ -207,26 +209,36 @@
                             for lane in range(0, STEP_COLUMNS, 128):
                                 part = acc[row : row + 8, lane : lane + 128]
                                 total = part if total is None else total + part
+                if squares:
+                    some = pl.ds(at, n)
+                    copies.append(pltpu.make_async_copy(scratch.at[some], sum_ref.at[some], sem.at[len(copies)]))
+                    copies[-1].start()
                 at += n
         if squares:
-            outs[-1][...] = total
+            square_ref[...] = total
+        for copy in copies:
+            copy.wait()
 
     shapes = [pltpu.VMEM((sum(n for n, _ in out), width), dtype) for out in plan]
+    specs, scratch_shapes = [IN_VMEM] * len(shapes), []
     if squares:
-        shapes.append(pltpu.VMEM((8, 128), jnp.float32))
+        scratch_shapes = [shapes[0], pltpu.SemaphoreType.DMA((len(plan[0]),))]
+        shapes = [pltpu.HBM(shapes[0].shape, dtype), pltpu.VMEM((8, 128), jnp.float32)]
+        specs = [IN_HBM, IN_VMEM]
     moved = sum(n * (1 + len(sources)) for out in plan for n, sources in out)
     return pl.pallas_call(
         kernel,
         out_shape=shapes,
         in_specs=[IN_VMEM] * len(arrays),
-        out_specs=[IN_VMEM] * len(shapes),
+        out_specs=specs,
+        scratch_shapes=scratch_shapes,
         compiler_params=SMALL,
         name=name,
         cost_estimate=cost(moved, width),
     )(*arrays)
 
 
-def place(out, table, pieces, name):
+def place(out, table, pieces, name, stored=()):
     arrays = []
     for x, *_ in pieces:
         if not any(x is have for have in arrays):
@@ -237,9 +249,15 @@
     old = [] if out is None else [out]
 
     def kernel(table_ref, *refs):
-        ins, out_ref, token_ref, sem = refs[: len(arrays)], refs[-3], refs[-2], refs[-1]
+        ins, sem = refs[: len(arrays)], refs[-1]
+        stored_in = refs[len(arrays) : len(arrays) + len(stored)]
+        out_ref, token_ref, *stored_out = refs[-3 - len(stored) : -1]
         token_ref[...] = jnp.zeros_like(token_ref)
         copies = []
+        for x, to in zip(stored_in, stored_out):
+            copy = pltpu.make_async_copy(x, to, sem.at[len(copies)])
+            copy.start()
+            copies.append(copy)
         for i, row, block, first, n in plan:
             copy = pltpu.make_async_copy(
                 ins[i].at[pl.ds(row, n)],
@@ -256,15 +274,16 @@
         out_shape=[
             jax.ShapeDtypeStruct((2048, width), jnp.bfloat16),
             pltpu.VMEM((8, 128), jnp.bfloat16),
+            *(jax.ShapeDtypeStruct(x.shape, x.dtype) for x in stored),
         ],
-        in_specs=[IN_SMEM] + [IN_VMEM] * len(arrays) + [IN_HBM] * len(old),
-        out_specs=[IN_HBM, IN_VMEM],
-        scratch_shapes=[pltpu.SemaphoreType.DMA((len(plan),))],
-        input_output_aliases={1 + len(arrays): 0} if old else {},
+        in_specs=[IN_SMEM] + [IN_VMEM] * (len(arrays) + len(stored)) + [IN_HBM] * len(old),
+        out_specs=[IN_HBM, IN_VMEM] + [IN_HBM] * len(stored),
+        scratch_shapes=[pltpu.SemaphoreType.DMA((len(plan) + len(stored),))],
+        input_output_aliases={1 + len(arrays) + len(stored): 0} if old else {},
         compiler_params=SMALL,
         name=name,
         cost_estimate=cost(2 * sum(p[-1] for p in plan), width),
-    )(table, *arrays, *old)
+    )(table, *arrays, *stored, *old)
 
 
 def reduce_rows(grad, table):
@@ -318,10 +337,10 @@
     return pieces
 
 
-def gather_rows(own, table):
+def gather_rows(own, table, states):
     at = layout(OWN)
     held = {seg: (own, at[seg]) for seg in OWN}
-    news, out, token = [(own, [(seg, at[seg]) for seg in OWN])], None, ()
+    news, out, token, states_out = [(own, [(seg, at[seg]) for seg in OWN])], None, (), None
     for k, plan in enumerate(GATHER):
         if k == 0:
             messages = [own] * len(plan)
@@ -337,7 +356,8 @@
             pieces = []
             for i, (x, segs) in enumerate(news):
                 pieces.extend(runs_of(x, to_other_core(x, f"gather{k}_{i}"), segs))
-            out, mark = place(out, table, pieces, f"place{k}")
+            out, mark, *stored = place(out, table, pieces, f"place{k}", states)
+            states_out, states = states_out or stored, ()
             token = token or (mark,)
         for x, segs in came:
             held.update({seg: (x, row) for seg, row in segs})
@@ -345,15 +365,68 @@
     last = sorted((seg for _, segs in news for seg, _ in segs), key=lambda seg: START[seg[2]])
     (x,) = build([[(SIZE[s[2]], [held[s]]) for s in last]], "copy3", after=token)
     at = layout(last)
-    return place(out, table, runs_of(x, to_other_core(x, "last"), [(seg, at[seg]) for seg in last]), "place3")[0]
-
-
-def total_over_all(x):
+    out, _ = place(out, table, runs_of(x, to_other_core(x, "last"), [(seg, at[seg]) for seg in last]), "place3")
+    return out, states_out
+
+
+def parts_of_total(x):
     x = jnp.sum(x, axis=0, keepdims=True)
     x = x + lax.ppermute(x, "dp_1", [(0, 1), (1, 0)])
     axes = ("ends", "dp_0", "tp_0", "tp_1")
     n = lax.axis_size(axes)
-    return jnp.sum(lax.all_to_all(jnp.broadcast_to(x, (n, *x.shape)), axes, 0, 0))
+    return lax.all_to_all(jnp.broadcast_to(x, (n, *x.shape)), axes, 0, 0)
+
+
+def adamw(parts, summed, master, moment, second, size):
+    rows, width = summed.shape
+
+    def kernel(parts_ref, *refs):
+        from_hbm, (w_ref, master_out, moment_out, second_out) = refs[:4], refs[4:8]
+        (summed_ref, master_ref, moment_ref, second_ref), sem = refs[8:12], refs[12]
+
+        def load(k, i):
+            at = pl.ds(k * 32, 32)
+            return pltpu.make_async_copy(from_hbm[i].at[at], refs[8 + i].at[at], sem.at[k * 4 + i])
+
+        for k in range(rows // 32):
+            for i in range(4):
+                load(k, i).start()
+        squares = jnp.sum(jnp.sum(parts_ref[...], axis=0), axis=1, keepdims=True)
+        limit = jnp.sqrt(jnp.full_like(squares, size))
+        factor = jnp.minimum(1.0, limit / (jnp.sqrt(squares) + 1e-06))
+
+        def some_rows(i, carry):
+            at = pl.ds(pl.multiple_of(i * 16, 16), 16)
+            for col in range(0, width, STEP_COLUMNS):
+                cols = pl.ds(col, STEP_COLUMNS)
+                clipped = factor * summed_ref[at, cols]
+                m = 0.9 * moment_ref[at, cols] + 0.1 * clipped
+                v = 0.999 * second_ref[at, cols] + 0.001 * clipped * clipped
+                root = jnp.sqrt(v * (1.0 / (1.0 - 0.999**STEP))) + 1e-08
+                update = m * (1.0 / (1.0 - 0.9**STEP)) / root
+                old = master_ref[at, cols]
+                new = old - 0.01 * (update + 0.1 * old)
+                w_ref[at, cols] = new.astype(jnp.bfloat16)
+                master_out[at, cols] = new
+                moment_out[at, cols] = m
+                second_out[at, cols] = v
+            return carry
+
+        for k in range(rows // 32):
+            for i in range(4):
+                load(k, i).wait()
+            lax.fori_loop(2 * k, 2 * k + 2, some_rows, 0)
+
+    return pl.pallas_call(
+        kernel,
+        out_shape=[pltpu.VMEM((rows, width), jnp.bfloat16)] + [pltpu.VMEM((rows, width), jnp.float32)] * 3,
+        in_specs=[IN_VMEM] + [IN_HBM] * 4,
+        out_specs=[IN_VMEM] * 4,
+        scratch_shapes=[pltpu.VMEM((rows, width), jnp.float32)] * 4 + [pltpu.SemaphoreType.DMA((rows // 8,))],
+        compiler_params=pltpu.CompilerParams(vmem_limit_bytes=10 * 2**20),
+        name="adamw",
+        cost_estimate=cost(15 * rows, width),
+    )(parts, *(pltpu.with_memory_space_constraint(x, pltpu.HBM) for x in (summed, master, moment, second)))
 
 
 def per_device(grad, master, moment, second):
@@ -369,18 +442,12 @@
         ]
     ).astype(jnp.int32)
     summed, parts = reduce_rows(grad.reshape(rows_tp, width), table)
-    squares = total_over_all(parts)
-    vocab_total = rows_tp * lax.axis_size(TP)
-    factor = jnp.minimum(
-        jnp.float32(1.0), jnp.sqrt(jnp.float32(vocab_total * width)) / (jnp.sqrt(squares) + 1e-06)
+    size = rows_tp * lax.axis_size(TP) * width
+    rounded, *states = adamw(
+        parts_of_total(parts), summed, master[0], moment[0], second[0], float(size)
     )
-    clipped = factor * summed
-    moment_out = 0.9 * moment[0] + 0.1 * clipped
-    second_out = 0.999 * second[0] + 0.001 * clipped * clipped
-    update = moment_out / (1.0 - 0.9**STEP) / (jnp.sqrt(second_out / (1.0 - 0.999**STEP)) + 1e-08)
-    master_out = master[0] - 0.01 * (update + 0.1 * master[0])
-    weights = gather_rows(master_out.astype(jnp.bfloat16), table)
-    return (weights, master_out[None], moment_out[None], second_out[None])
+    weights, states = gather_rows(rounded, table, states)
+    return (weights, *(x[None] for x in states))
 
 
 def solution(mesh):

time: 151 us -> 149 us (0.987)
  Pallas kernels: 21.5 us -> 27.1 us
  other arithmetic: 5.55 us -> 0.02 us
    convert_element_type x1 -> x0, other arithmetic: 4.92 us -> none  [per_device(): weights = gather_rows(master_out.astype(jnp.bfloat16), table)]
    pallas_call x0 -> x1, Pallas kernels: none -> 3.26 us  [adamw(): pl.pallas_call(kernel, out_shape=[pltpu.VMEM((rows, width), jnp.bfloat16)...]
  transfers between devices with their start and end apart: 37 -> 37, of which waited for: 13 -> 13; matrix products, arithmetic and copies ran while one was open for 0% -> 0% of each run, Pallas kernels for 11% -> 12%
where the time goes in v4:
time: 149 us
  waiting for transfers between devices  56.4 us (38%)
  starting transfers between devices  46.5 us (31%)
  Pallas kernels  27.1 us (18%)
  blocking collectives  17.8 us (12%)
    ppermute x8, waiting for transfers between devices, _send(): return lax.ppermute(x, 'ends', [(0, 1), (1, 0)])  30.1 us
    ppermute x16, waiting for transfers between devices, _send(): return lax.ppermute(x, 'dp_0', [(i, i ^ flip) for i in range(4)])  25.4 us
    all_to_all x1, blocking collectives, parts_of_total(): return lax.all_to_all(jnp.broadcast_to(x, (n, *x.shape)), axes, 0, 0)  17.8 us
    ppermute x12, starting transfers between devices, to_other_core(): return lax.ppermute(x, 'dp_1', [(0, 1), (1, 0)])  16.5 us
    ppermute x8, starting transfers between devices, _send(): return lax.ppermute(x, 'ends', [(0, 1), (1, 0)])  14.8 us
    ppermute x16, starting transfers between devices, _send(): return lax.ppermute(x, 'dp_0', [(i, i ^ flip) for i in range(4)])  13.4 us
    pallas_call x3, Pallas kernels, place(): pl.pallas_call(kernel, out_shape=[jax.ShapeDtypeStruct((2048, width), jnp...  10.5 us
    pallas_call x4, Pallas kernels, fetch(): pl.pallas_call(kernel, out_shape=[pltpu.VMEM((rows, width), jnp.bfloat16)...  10.1 us
  transfers between devices with their start and end apart: 37, of which 13 were waited for; matrix products, arithmetic and copies ran while one was open for 0% of the time, Pallas kernels for 12%

profile of v4, /device:TPU:1, one launch (start us, length us, event | category | flops | bytes accessed | tf_op | source)
XLA Modules:
  0.0 148.9 jit_solution(15713288945972764308)
XLA Ops:
  0.8 2.2 %fetch0.1.refs_0_ = bf16[384,3072]{1,0:T(8,128)(2,1)S(1)} custom-call(s32[16]{0:T(128)S(1)} %stack.67.table_ref, bf16[2048,3072]{1,0:T(8,128)(2,1)} %bitcast.27), custom_call_target="tpu_custom_call" | custom-call | bytes 4718592 | tf_op jit(solution)/shard_map/fetch0/pallas_call | solution.py:164
  4.5 2.2 %fetch1.1.refs_0_ = bf16[384,3072]{1,0:T(8,128)(2,1)S(1)} custom-call(s32[16]{0:T(128)S(1)} %stack.67.table_ref, bf16[2048,3072]{1,0:T(8,128)(2,1)} %bitcast.28, bf16[384,3072]{1,0:T(8,128)(2,1)S(1)} %fetch0.1.refs_0_), custom_call_target="tpu_custom_call" | custom-call | bytes 4718592 | tf_op jit(solution)/shard_map/fetch1/pallas_call | solution.py:164
  6.7 2.8 %fetch2.1 = (bf16[192,3072]{1,0:T(8,128)(2,1)S(1)}, bf16[320,3072]{1,0:T(8,128)(2,1)S(1)}, bf16[128,3072]{1,0:T(8,128)(2,1)S(1)}) custom-call(s32[16]{0:T(128)S(1)} %stack.67.table_ref, bf16[2048,3072]{1,0:T(8,128)(2,1)} %bitcast.29, bf16[384,3072]{1,0:T(8,128)(2,1)S(1)} %fetch1.1.refs_0_), custom_call_target="tpu_custom_call" | custom-call | bytes 7864320 | tf_op jit(solution)/shard_map/fetch2/pallas_call | solution.py:164
  10.6 2.9 %collective-permute-start.4 = (bf16[64,3072]{1,0:T(8,128)(2,1)S(1)}, bf16[64,3072]{1,0:T(8,128)(2,1)S(1)}, u32[]{:S(2)}, u32[]{:S(2)}) collective-permute-start(bf16[64,3072]{1,0:T(8,128)(2,1)S(1)} %get-tuple-element.50), channel_id=1, source_target_pairs={{0,48},{16,32},{32,16},{48,0},{1,49},{17,33},{33,17},{49,1},{2,50}... | collective-permute-start | bytes 1179656 | tf_op jit(solution)/shard_map/reduce0_p3/ppermute | solution.py:101
  13.6 3.6 %collective-permute-start.9 = (bf16[64,3072]{1,0:T(8,128)(2,1)S(1)}, bf16[64,3072]{1,0:T(8,128)(2,1)S(1)}, u32[]{:S(2)}, u32[]{:S(2)}) collective-permute-start(bf16[64,3072]{1,0:T(8,128)(2,1)S(1)} %get-tuple-element.44.refs_0_), channel_id=1, source_target_pairs={{0,64},{64,0},{1,65},{65,1},{2,66},{66,2},{3,67},{67,3},{4,68},{68... | collective-permute-start | bytes 1179656 | tf_op jit(solution)/shard_map/reduce0_z/ppermute | solution.py:99
  18.1 4.8 %collective-permute-done.4.refs_2_.refs_3_ = bf16[64,3072]{1,0:T(8,128)(2,1)S(1)} collective-permute-done((bf16[64,3072]{1,0:T(8,128)(2,1)S(1)}, bf16[64,3072]{1,0:T(8,128)(2,1)S(1)}, u32[]{:S(2)}, u32[]{:S(2)}) %collective-permute-start.4) | collective-permute-done | bytes 393248 | tf_op jit(solution)/shard_map/reduce0_p3/ppermute | solution.py:101
  22.9 3.5 %collective-permute-start.5 = (bf16[64,3072]{1,0:T(8,128)(2,1)S(1)}, bf16[64,3072]{1,0:T(8,128)(2,1)S(1)}, u32[]{:S(2)}, u32[]{:S(2)}) collective-permute-start(bf16[64,3072]{1,0:T(8,128)(2,1)S(1)} %get-tuple-element.51), channel_id=1, source_target_pairs={{0,64},{64,0},{1,65},{65,1},{2,66},{66,2},{3,67},{67,3},{4,68},{68... | collective-permute-start | bytes 1179656 | tf_op jit(solution)/shard_map/reduce1_z/ppermute | solution.py:99
  26.4 1.5 %collective-permute-start.1 = (bf16[128,3072]{1,0:T(8,128)(2,1)S(1)}, bf16[128,3072]{1,0:T(8,128)(2,1)S(1)}, u32[]{:S(2)}, u32[]{:S(2)}) collective-permute-start(bf16[128,3072]{1,0:T(8,128)(2,1)S(1)} %get-tuple-element.46), channel_id=1, source_target_pairs={{0,8},{8,0},{1,9},{9,1},{2,10},{10,2},{3,11},{11,3},{4,12},{12,4},... | collective-permute-start | bytes 2359304 | tf_op jit(solution)/shard_map/second_2_core/ppermute | solution.py:106
  28.0 2.8 %fetch3.1 = (bf16[192,3072]{1,0:T(8,128)(2,1)S(1)}, bf16[320,3072]{1,0:T(8,128)(2,1)S(1)}, bf16[128,3072]{1,0:T(8,128)(2,1)S(1)}) custom-call(s32[16]{0:T(128)S(1)} %stack.67.table_ref, bf16[2048,3072]{1,0:T(8,128)(2,1)} %bitcast.30, bf16[64,3072]{1,0:T(8,128)(2,1)S(1)} %get-tuple-element.44.refs_0_), custom_call_target="tpu_custom_call" | custom-call | bytes 7864320 | tf_op jit(solution)/shard_map/fetch3/pallas_call | solution.py:164
  31.2 2.7 %collective-permute-start.10 = (bf16[64,3072]{1,0:T(8,128)(2,1)S(1)}, bf16[64,3072]{1,0:T(8,128)(2,1)S(1)}, u32[]{:S(2)}, u32[]{:S(2)}) collective-permute-start(bf16[64,3072]{1,0:T(8,128)(2,1)S(1)} %get-tuple-element.56), channel_id=1, source_target_pairs={{0,48},{16,32},{32,16},{48,0},{1,49},{17,33},{33,17},{49,1},{2,50}... | collective-permute-start | bytes 1179656 | tf_op jit(solution)/shard_map/reduce2_p3/ppermute | solution.py:101
  34.8 2.4 %collective-permute-start.13 = (bf16[64,3072]{1,0:T(8,128)(2,1)S(1)}, bf16[64,3072]{1,0:T(8,128)(2,1)S(1)}, u32[]{:S(2)}, u32[]{:S(2)}) collective-permute-start(bf16[64,3072]{1,0:T(8,128)(2,1)S(1)} %get-tuple-element.59), channel_id=1, source_target_pairs={{0,64},{64,0},{1,65},{65,1},{2,66},{66,2},{3,67},{67,3},{4,68},{68... | collective-permute-start | bytes 1179656 | tf_op jit(solution)/shard_map/reduce2_z/ppermute | solution.py:99
  39.0 3.5 %collective-permute-done.10.refs_3_ = bf16[64,3072]{1,0:T(8,128)(2,1)S(1)} collective-permute-done((bf16[64,3072]{1,0:T(8,128)(2,1)S(1)}, bf16[64,3072]{1,0:T(8,128)(2,1)S(1)}, u32[]{:S(2)}, u32[]{:S(2)}) %collective-permute-start.10) | collective-permute-done | bytes 393248 | tf_op jit(solution)/shard_map/reduce2_p3/ppermute | solution.py:101
  42.9 4.1 %collective-permute-done.12.refs_5_ = bf16[64,3072]{1,0:T(8,128)(2,1)S(1)} collective-permute-done((bf16[64,3072]{1,0:T(8,128)(2,1)S(1)}, bf16[64,3072]{1,0:T(8,128)(2,1)S(1)}, u32[]{:S(2)}, u32[]{:S(2)}) %collective-permute-start.12) | collective-permute-done | bytes 393248 | tf_op jit(solution)/shard_map/reduce2_p1/ppermute | solution.py:101
  47.0 2.7 %collective-permute-start.7 = (bf16[64,3072]{1,0:T(8,128)(2,1)S(1)}, bf16[64,3072]{1,0:T(8,128)(2,1)S(1)}, u32[]{:S(2)}, u32[]{:S(2)}) collective-permute-start(bf16[64,3072]{1,0:T(8,128)(2,1)S(1)} %get-tuple-element.53), channel_id=1, source_target_pairs={{0,48},{16,32},{32,16},{48,0},{1,49},{17,33},{33,17},{49,1},{2,50}... | collective-permute-start | bytes 1179656 | tf_op jit(solution)/shard_map/reduce3_p3/ppermute | solution.py:101
  50.3 5.1 %collective-permute-done.15.refs_6_ = bf16[64,3072]{1,0:T(8,128)(2,1)S(1)} collective-permute-done((bf16[64,3072]{1,0:T(8,128)(2,1)S(1)}, bf16[64,3072]{1,0:T(8,128)(2,1)S(1)}, u32[]{:S(2)}, u32[]{:S(2)}) %collective-permute-start.15) | collective-permute-done | bytes 393248 | tf_op jit(solution)/shard_map/reduce3_p1/ppermute | solution.py:101
  55.4 2.2 %collective-permute-done.7.refs_3_ = bf16[64,3072]{1,0:T(8,128)(2,1)S(1)} collective-permute-done((bf16[64,3072]{1,0:T(8,128)(2,1)S(1)}, bf16[64,3072]{1,0:T(8,128)(2,1)S(1)}, u32[]{:S(2)}, u32[]{:S(2)}) %collective-permute-start.7) | collective-permute-done | bytes 393248 | tf_op jit(solution)/shard_map/reduce3_p3/ppermute | solution.py:101
  57.6 4.2 %collective-permute-done.17.refs_8_ = bf16[32,3072]{1,0:T(8,128)(2,1)S(1)} collective-permute-done((bf16[32,3072]{1,0:T(8,128)(2,1)S(1)}, bf16[32,3072]{1,0:T(8,128)(2,1)S(1)}, u32[]{:S(2)}, u32[]{:S(2)}) %collective-permute-start.17) | collective-permute-done | bytes 196640 | tf_op jit(solution)/shard_map/reduce4_p3/ppermute | solution.py:101
  64.4 1.8 %collective-permute-start.19 = (f32[1,128]{1,0:T(1,128)S(1)}, f32[1,128]{1,0:T(1,128)S(1)}, u32[]{:S(2)}, u32[]{:S(2)}) collective-permute-start(f32[1,128]{1,0:T(1,128)S(1)} %bitcast.34), channel_id=1, source_target_pairs={{0,8},{8,0},{1,9},{9,1},{2,10},{10,2},{3,11},{11,3},{4,12},{12,4},... | collective-permute-start | bytes 1544 | tf_op jit(solution)/shard_map/ppermute | solution.py:374
  67.0 17.8 %all_to_all.5.parts_ref = f32[64,1,128]{2,1,0:T(1,128)S(1)} all-to-all(f32[64,1,128]{2,1,0:T(1,128)S(1)} %broadcast_in_dim.16), channel_id=1, replica_groups=mesh['ends'=2,'dp_0'=4,'dp_1'=2,'tp_0'=2,'tp_1'=4] {'ends','dp_0','tp_0'..., dimensions={0} | all-to-all | bytes 65536 | tf_op jit(solution)/shard_map/all_to_all | solution.py:377
  84.8 3.3 %adamw.1 = (bf16[128,3072]{1,0:T(8,128)(2,1)S(1)}, f32[128,3072]{1,0:T(8,128)S(1)}, f32[128,3072]{1,0:T(8,128)S(1)}, f32[128,3072]{1,0:T(8,128)S(1)}) custom-call(f32[64,1,128]{2,1,0:T(1,128)S(1)} %all_to_all.5.parts_ref, f32[128,3072]{1,0:T(8,128)} %get-tuple-element.66.refs_0_, f32[128,3072]{1,0:T(8,128)} %bitcast.31, f32[128,3072]{1,0:T(8,128)} %bitcast.32, ...), custom_call_target="tpu_custom_call" | custom-call | bytes 11796480 | tf_op jit(solution)/shard_map/adamw/pallas_call | solution.py:420
  90.3 16.7 %collective-permute-done.21.refs_2_.refs_1_ = bf16[128,3072]{1,0:T(8,128)(2,1)S(1)} collective-permute-done((bf16[128,3072]{1,0:T(8,128)(2,1)S(1)}, bf16[128,3072]{1,0:T(8,128)(2,1)S(1)}, u32[]{:S(2)}, u32[]{:S(2)}) %collective-permute-start.21) | collective-permute-done | bytes 786464 | tf_op jit(solution)/shard_map/gather0_z/ppermute | solution.py:99
  107.7 2.0 %collective-permute-start.27 = (bf16[128,3072]{1,0:T(8,128)(2,1)S(1)}, bf16[128,3072]{1,0:T(8,128)(2,1)S(1)}, u32[]{:S(2)}, u32[]{:S(2)}) collective-permute-start(bf16[128,3072]{1,0:T(8,128)(2,1)S(1)} %get-tuple-element.72), channel_id=1, source_target_pairs={{0,64},{64,0},{1,65},{65,1},{2,66},{66,2},{3,67},{67,3},{4,68},{68... | collective-permute-start | bytes 2359304 | tf_op jit(solution)/shard_map/gather1_z/ppermute | solution.py:99
  110.5 3.9 %collective-permute-start.20 = (bf16[128,3072]{1,0:T(8,128)(2,1)S(1)}, bf16[128,3072]{1,0:T(8,128)(2,1)S(1)}, u32[]{:S(2)}, u32[]{:S(2)}) collective-permute-start(bf16[128,3072]{1,0:T(8,128)(2,1)S(1)} %get-tuple-element.67.refs_0_), channel_id=1, source_target_pairs={{0,8},{8,0},{1,9},{9,1},{2,10},{10,2},{3,11},{11,3},{4,12},{12,4},... | collective-permute-start | bytes 2359304 | tf_op jit(solution)/shard_map/gather1_0_core/ppermute | solution.py:106
  114.4 10.7 %collective-permute-done.27.refs_0_ = bf16[128,3072]{1,0:T(8,128)(2,1)S(1)} collective-permute-done((bf16[128,3072]{1,0:T(8,128)(2,1)S(1)}, bf16[128,3072]{1,0:T(8,128)(2,1)S(1)}, u32[]{:S(2)}, u32[]{:S(2)}) %collective-permute-start.27) | collective-permute-done | bytes 786464 | tf_op jit(solution)/shard_map/gather1_z/ppermute | solution.py:99
  125.1 4.1 %collective-permute-start.24 = (bf16[128,3072]{1,0:T(8,128)(2,1)S(1)}, bf16[128,3072]{1,0:T(8,128)(2,1)S(1)}, u32[]{:S(2)}, u32[]{:S(2)}) collective-permute-start(bf16[128,3072]{1,0:T(8,128)(2,1)S(1)} %collective-permute-done.23.refs_4_.refs_2_), channel_id=1, source_target_pairs={{0,8},{8,0},{1,9},{9,1},{2,10},{10,2},{3,11},{11,3},{4,12},{12,4},... | collective-permute-start | bytes 2359304 | tf_op jit(solution)/shard_map/gather1_2_core/ppermute | solution.py:106
  129.7 1.6 %collective-permute-start.32 = (bf16[64,3072]{1,0:T(8,128)(2,1)S(1)}, bf16[64,3072]{1,0:T(8,128)(2,1)S(1)}, u32[]{:S(2)}, u32[]{:S(2)}) collective-permute-start(bf16[64,3072]{1,0:T(8,128)(2,1)S(1)} %get-tuple-element.77), channel_id=1, source_target_pairs={{0,64},{64,0},{1,65},{65,1},{2,66},{66,2},{3,67},{67,3},{4,68},{68... | collective-permute-start | bytes 1179656 | tf_op jit(solution)/shard_map/gather2_z/ppermute | solution.py:99
  132.2 1.6 %collective-permute-start.34 = (bf16[128,3072]{1,0:T(8,128)(2,1)S(1)}, bf16[128,3072]{1,0:T(8,128)(2,1)S(1)}, u32[]{:S(2)}, u32[]{:S(2)}) collective-permute-start(bf16[128,3072]{1,0:T(8,128)(2,1)S(1)} %collective-permute-done.27.refs_0_), channel_id=1, source_target_pairs={{0,8},{8,0},{1,9},{9,1},{2,10},{10,2},{3,11},{11,3},{4,12},{12,4},... | collective-permute-start | bytes 2359304 | tf_op jit(solution)/shard_map/gather2_0_core/ppermute | solution.py:106
  133.9 4.7 %place1.1 = (bf16[2048,3072]{1,0:T(8,128)(2,1)}, bf16[8,128]{1,0:T(8,128)(2,1)S(1)}, f32[128,3072]{1,0:T(8,128)}, f32[128,3072]{1,0:T(8,128)}, f32[128,3072]{1,0:T(8,128)}) custom-call(s32[16]{0:T(128)S(1)} %stack.67.table_ref, bf16[128,3072]{1,0:T(8,128)(2,1)S(1)} %get-tuple-element.67.refs_0_, bf16[128,3072]{1,0:T(8,128)(2,1)S(1)} %collective-permute-done.20.refs_1_, ...), custom_call_target="tpu_custom_call" | custom-call | bytes 12582912 | tf_op jit(solution)/shard_map/place1/pallas_call | solution.py:272
  139.2 1.5 %collective-permute-done.32.refs_3_ = bf16[64,3072]{1,0:T(8,128)(2,1)S(1)} collective-permute-done((bf16[64,3072]{1,0:T(8,128)(2,1)S(1)}, bf16[64,3072]{1,0:T(8,128)(2,1)S(1)}, u32[]{:S(2)}, u32[]{:S(2)}) %collective-permute-start.32) | collective-permute-done | bytes 393248 | tf_op jit(solution)/shard_map/gather2_z/ppermute | solution.py:99
  140.7 2.2 %collective-permute-start.33 = (bf16[128,3072]{1,0:T(8,128)(2,1)S(1)}, bf16[128,3072]{1,0:T(8,128)(2,1)S(1)}, u32[]{:S(2)}, u32[]{:S(2)}) collective-permute-start(bf16[128,3072]{1,0:T(8,128)(2,1)S(1)} %copy3.1.refs_0_), channel_id=1, source_target_pairs={{0,8},{8,0},{1,9},{9,1},{2,10},{10,2},{3,11},{11,3},{4,12},{12,4},... | collective-permute-start | bytes 2359304 | tf_op jit(solution)/shard_map/last_core/ppermute | solution.py:106
  143.0 3.5 %place2.1 = (bf16[2048,3072]{1,0:T(8,128)(2,1)}, bf16[8,128]{1,0:T(8,128)(2,1)}) custom-call(s32[16]{0:T(128)S(1)} %stack.67.table_ref, bf16[128,3072]{1,0:T(8,128)(2,1)S(1)} %collective-permute-done.27.refs_0_, bf16[128,3072]{1,0:T(8,128)(2,1)S(1)} %collective-permute-done.34.refs_1_, ...), custom_call_target="tpu_custom_call", output_to_operand_aliasing={{0}: (7, {})} | custom-call | bytes 9437184 | tf_op jit(solution)/shard_map/place2/pallas_call | solution.py:272
  146.4 2.3 %place3.1 = (bf16[2048,3072]{1,0:T(8,128)(2,1)}, bf16[8,128]{1,0:T(8,128)(2,1)}) custom-call(s32[16]{0:T(128)S(1)} %stack.67.table_ref, bf16[128,3072]{1,0:T(8,128)(2,1)S(1)} %copy3.1.refs_0_, bf16[128,3072]{1,0:T(8,128)(2,1)S(1)} %collective-permute-done.33.refs_1_, bf16[2048,3072]{1,0:T(8,128)(2,1)} %get-tuple-element.79.refs_2_), custom_call_target="tpu_custom_call", output_to_operand_aliasing={{0}: (3, {})} | custom-call | bytes 3145728 | tf_op jit(solution)/shard_map/place3/pallas_call | solution.py:272
  (63 shorter events, 16.7 us)
Async XLA Ops:
  3.0 7.1 %collective-permute-start = (bf16[384,3072]{1,0:T(8,128)(2,1)S(1)}, bf16[384,3072]{1,0:T(8,128)(2,1)S(1)}, u32[]{:S(2)}, u32[]{:S(2)}) collective-permute-start(bf16[384,3072]{1,0:T(8,128)(2,1)S(1)} %fetch0.1.refs_0_), channel_id=1, source_target_pairs={{0,8},{8,0},{1,9},{9,1},{2,10},{10,2},{3,11},{11,3},{4,12},{12,4},... | collective-permute-start | bytes 7077896 | tf_op jit(solution)/shard_map/first_0_core/ppermute | solution.py:106
  9.5 21.7 %collective-permute-start.3 = (bf16[320,3072]{1,0:T(8,128)(2,1)S(1)}, bf16[320,3072]{1,0:T(8,128)(2,1)S(1)}, u32[]{:S(2)}, u32[]{:S(2)}) collective-permute-start(bf16[320,3072]{1,0:T(8,128)(2,1)S(1)} %get-tuple-element.49), channel_id=1, source_target_pairs={{0,8},{8,0},{1,9},{9,1},{2,10},{10,2},{3,11},{11,3},{4,12},{12,4},... | collective-permute-start | bytes 5898248 | tf_op jit(solution)/shard_map/second_1_core/ppermute | solution.py:106
  9.6 7.6 %collective-permute-start.8 = (bf16[192,3072]{1,0:T(8,128)(2,1)S(1)}, bf16[192,3072]{1,0:T(8,128)(2,1)S(1)}, u32[]{:S(2)}, u32[]{:S(2)}) collective-permute-start(bf16[192,3072]{1,0:T(8,128)(2,1)S(1)} %get-tuple-element.55), channel_id=1, source_target_pairs={{0,8},{8,0},{1,9},{9,1},{2,10},{10,2},{3,11},{11,3},{4,12},{12,4},... | collective-permute-start | bytes 3538952 | tf_op jit(solution)/shard_map/second_0_core/ppermute | solution.py:106
  10.6 12.3 %collective-permute-start.4 = (bf16[64,3072]{1,0:T(8,128)(2,1)S(1)}, bf16[64,3072]{1,0:T(8,128)(2,1)S(1)}, u32[]{:S(2)}, u32[]{:S(2)}) collective-permute-start(bf16[64,3072]{1,0:T(8,128)(2,1)S(1)} %get-tuple-element.50), channel_id=1, source_target_pairs={{0,48},{16,32},{32,16},{48,0},{1,49},{17,33},{33,17},{49,1},{2,50}... | collective-permute-start | bytes 1179656 | tf_op jit(solution)/shard_map/reduce0_p3/ppermute | solution.py:101
  13.5 12.8 %collective-permute-start.6 = (bf16[64,3072]{1,0:T(8,128)(2,1)S(1)}, bf16[64,3072]{1,0:T(8,128)(2,1)S(1)}, u32[]{:S(2)}, u32[]{:S(2)}) collective-permute-start(bf16[64,3072]{1,0:T(8,128)(2,1)S(1)} %get-tuple-element.52), channel_id=1, source_target_pairs={{0,16},{16,0},{32,48},{48,32},{1,17},{17,1},{33,49},{49,33},{2,18}... | collective-permute-start | bytes 1179656 | tf_op jit(solution)/shard_map/reduce0_p1/ppermute | solution.py:101
  13.6 14.4 %collective-permute-start.9 = (bf16[64,3072]{1,0:T(8,128)(2,1)S(1)}, bf16[64,3072]{1,0:T(8,128)(2,1)S(1)}, u32[]{:S(2)}, u32[]{:S(2)}) collective-permute-start(bf16[64,3072]{1,0:T(8,128)(2,1)S(1)} %get-tuple-element.44.refs_0_), channel_id=1, source_target_pairs={{0,64},{64,0},{1,65},{65,1},{2,66},{66,2},{3,67},{67,3},{4,68},{68... | collective-permute-start | bytes 1179656 | tf_op jit(solution)/shard_map/reduce0_z/ppermute | solution.py:99
  17.2 16.8 %collective-permute-start.11 = (bf16[64,3072]{1,0:T(8,128)(2,1)S(1)}, bf16[64,3072]{1,0:T(8,128)(2,1)S(1)}, u32[]{:S(2)}, u32[]{:S(2)}) collective-permute-start(bf16[64,3072]{1,0:T(8,128)(2,1)S(1)} %get-tuple-element.57), channel_id=1, source_target_pairs={{0,48},{16,32},{32,16},{48,0},{1,49},{17,33},{33,17},{49,1},{2,50}... | collective-permute-start | bytes 1179656 | tf_op jit(solution)/shard_map/reduce1_p3/ppermute | solution.py:101
  22.9 12.0 %collective-permute-start.5 = (bf16[64,3072]{1,0:T(8,128)(2,1)S(1)}, bf16[64,3072]{1,0:T(8,128)(2,1)S(1)}, u32[]{:S(2)}, u32[]{:S(2)}) collective-permute-start(bf16[64,3072]{1,0:T(8,128)(2,1)S(1)} %get-tuple-element.51), channel_id=1, source_target_pairs={{0,64},{64,0},{1,65},{65,1},{2,66},{66,2},{3,67},{67,3},{4,68},{68... | collective-permute-start | bytes 1179656 | tf_op jit(solution)/shard_map/reduce1_z/ppermute | solution.py:99
  26.4 23.9 %collective-permute-start.1 = (bf16[128,3072]{1,0:T(8,128)(2,1)S(1)}, bf16[128,3072]{1,0:T(8,128)(2,1)S(1)}, u32[]{:S(2)}, u32[]{:S(2)}) collective-permute-start(bf16[128,3072]{1,0:T(8,128)(2,1)S(1)} %get-tuple-element.46), channel_id=1, source_target_pairs={{0,8},{8,0},{1,9},{9,1},{2,10},{10,2},{3,11},{11,3},{4,12},{12,4},... | collective-permute-start | bytes 2359304 | tf_op jit(solution)/shard_map/second_2_core/ppermute | solution.py:106
  27.9 10.7 %collective-permute-start.2 = (bf16[64,3072]{1,0:T(8,128)(2,1)S(1)}, bf16[64,3072]{1,0:T(8,128)(2,1)S(1)}, u32[]{:S(2)}, u32[]{:S(2)}) collective-permute-start(bf16[64,3072]{1,0:T(8,128)(2,1)S(1)} %get-tuple-element.47), channel_id=1, source_target_pairs={{0,16},{16,0},{32,48},{48,32},{1,17},{17,1},{33,49},{49,33},{2,18}... | collective-permute-start | bytes 1179656 | tf_op jit(solution)/shard_map/reduce1_p1/ppermute | solution.py:101
  31.2 11.2 %collective-permute-start.10 = (bf16[64,3072]{1,0:T(8,128)(2,1)S(1)}, bf16[64,3072]{1,0:T(8,128)(2,1)S(1)}, u32[]{:S(2)}, u32[]{:S(2)}) collective-permute-start(bf16[64,3072]{1,0:T(8,128)(2,1)S(1)} %get-tuple-element.56), channel_id=1, source_target_pairs={{0,48},{16,32},{32,16},{48,0},{1,49},{17,33},{33,17},{49,1},{2,50}... | collective-permute-start | bytes 1179656 | tf_op jit(solution)/shard_map/reduce2_p3/ppermute | solution.py:101
  34.0 13.0 %collective-permute-start.12 = (bf16[64,3072]{1,0:T(8,128)(2,1)S(1)}, bf16[64,3072]{1,0:T(8,128)(2,1)S(1)}, u32[]{:S(2)}, u32[]{:S(2)}) collective-permute-start(bf16[64,3072]{1,0:T(8,128)(2,1)S(1)} %get-tuple-element.58), channel_id=1, source_target_pairs={{0,16},{16,0},{32,48},{48,32},{1,17},{17,1},{33,49},{49,33},{2,18}... | collective-permute-start | bytes 1179656 | tf_op jit(solution)/shard_map/reduce2_p1/ppermute | solution.py:101
  34.8 14.9 %collective-permute-start.13 = (bf16[64,3072]{1,0:T(8,128)(2,1)S(1)}, bf16[64,3072]{1,0:T(8,128)(2,1)S(1)}, u32[]{:S(2)}, u32[]{:S(2)}) collective-permute-start(bf16[64,3072]{1,0:T(8,128)(2,1)S(1)} %get-tuple-element.59), channel_id=1, source_target_pairs={{0,64},{64,0},{1,65},{65,1},{2,66},{66,2},{3,67},{67,3},{4,68},{68... | collective-permute-start | bytes 1179656 | tf_op jit(solution)/shard_map/reduce2_z/ppermute | solution.py:99
  38.6 16.9 %collective-permute-start.15 = (bf16[64,3072]{1,0:T(8,128)(2,1)S(1)}, bf16[64,3072]{1,0:T(8,128)(2,1)S(1)}, u32[]{:S(2)}, u32[]{:S(2)}) collective-permute-start(bf16[64,3072]{1,0:T(8,128)(2,1)S(1)} %get-tuple-element.61), channel_id=1, source_target_pairs={{0,16},{16,0},{32,48},{48,32},{1,17},{17,1},{33,49},{49,33},{2,18}... | collective-permute-start | bytes 1179656 | tf_op jit(solution)/shard_map/reduce3_p1/ppermute | solution.py:101
  42.4 13.0 %collective-permute-start.16 = (bf16[64,3072]{1,0:T(8,128)(2,1)S(1)}, bf16[64,3072]{1,0:T(8,128)(2,1)S(1)}, u32[]{:S(2)}, u32[]{:S(2)}) collective-permute-start(bf16[64,3072]{1,0:T(8,128)(2,1)S(1)} %get-tuple-element.62), channel_id=1, source_target_pairs={{0,64},{64,0},{1,65},{65,1},{2,66},{66,2},{3,67},{67,3},{4,68},{68... | collective-permute-start | bytes 1179656 | tf_op jit(solution)/shard_map/reduce3_z/ppermute | solution.py:99
  47.0 10.6 %collective-permute-start.7 = (bf16[64,3072]{1,0:T(8,128)(2,1)S(1)}, bf16[64,3072]{1,0:T(8,128)(2,1)S(1)}, u32[]{:S(2)}, u32[]{:S(2)}) collective-permute-start(bf16[64,3072]{1,0:T(8,128)(2,1)S(1)} %get-tuple-element.53), channel_id=1, source_target_pairs={{0,48},{16,32},{32,16},{48,0},{1,49},{17,33},{33,17},{49,1},{2,50}... | collective-permute-start | bytes 1179656 | tf_op jit(solution)/shard_map/reduce3_p3/ppermute | solution.py:101
  50.1 12.9 %collective-permute-start.14 = (bf16[64,3072]{1,0:T(8,128)(2,1)S(1)}, bf16[64,3072]{1,0:T(8,128)(2,1)S(1)}, u32[]{:S(2)}, u32[]{:S(2)}) collective-permute-start(bf16[64,3072]{1,0:T(8,128)(2,1)S(1)} %get-tuple-element.60), channel_id=1, source_target_pairs={{0,64},{64,0},{1,65},{65,1},{2,66},{66,2},{3,67},{67,3},{4,68},{68... | collective-permute-start | bytes 1179656 | tf_op jit(solution)/shard_map/reduce4_z/ppermute | solution.py:99
  50.3 11.6 %collective-permute-start.17 = (bf16[32,3072]{1,0:T(8,128)(2,1)S(1)}, bf16[32,3072]{1,0:T(8,128)(2,1)S(1)}, u32[]{:S(2)}, u32[]{:S(2)}) collective-permute-start(bf16[32,3072]{1,0:T(8,128)(2,1)S(1)} %get-tuple-element.63), channel_id=1, source_target_pairs={{0,48},{16,32},{32,16},{48,0},{1,49},{17,33},{33,17},{49,1},{2,50}... | collective-permute-start | bytes 589832 | tf_op jit(solution)/shard_map/reduce4_p3/ppermute | solution.py:101
  88.1 18.9 %collective-permute-start.21 = (bf16[128,3072]{1,0:T(8,128)(2,1)S(1)}, bf16[128,3072]{1,0:T(8,128)(2,1)S(1)}, u32[]{:S(2)}, u32[]{:S(2)}) collective-permute-start(bf16[128,3072]{1,0:T(8,128)(2,1)S(1)} %get-tuple-element.67.refs_0_), channel_id=1, source_target_pairs={{0,64},{64,0},{1,65},{65,1},{2,66},{66,2},{3,67},{67,3},{4,68},{68... | collective-permute-start | bytes 2359304 | tf_op jit(solution)/shard_map/gather0_z/ppermute | solution.py:99
  89.2 17.8 %collective-permute-start.23 = (bf16[128,3072]{1,0:T(8,128)(2,1)S(1)}, bf16[128,3072]{1,0:T(8,128)(2,1)S(1)}, u32[]{:S(2)}, u32[]{:S(2)}) collective-permute-start(bf16[128,3072]{1,0:T(8,128)(2,1)S(1)} %get-tuple-element.67.refs_0_), channel_id=1, source_target_pairs={{0,16},{16,0},{32,48},{48,32},{1,17},{17,1},{33,49},{49,33},{2,18}... | collective-permute-start | bytes 2359304 | tf_op jit(solution)/shard_map/gather0_p1/ppermute | solution.py:101
  89.6 18.0 %collective-permute-start.25 = (bf16[128,3072]{1,0:T(8,128)(2,1)S(1)}, bf16[128,3072]{1,0:T(8,128)(2,1)S(1)}, u32[]{:S(2)}, u32[]{:S(2)}) collective-permute-start(bf16[128,3072]{1,0:T(8,128)(2,1)S(1)} %get-tuple-element.67.refs_0_), channel_id=1, source_target_pairs={{0,48},{16,32},{32,16},{48,0},{1,49},{17,33},{33,17},{49,1},{2,50}... | collective-permute-start | bytes 2359304 | tf_op jit(solution)/shard_map/gather0_p3/ppermute | solution.py:101
  107.7 17.4 %collective-permute-start.27 = (bf16[128,3072]{1,0:T(8,128)(2,1)S(1)}, bf16[128,3072]{1,0:T(8,128)(2,1)S(1)}, u32[]{:S(2)}, u32[]{:S(2)}) collective-permute-start(bf16[128,3072]{1,0:T(8,128)(2,1)S(1)} %get-tuple-element.72), channel_id=1, source_target_pairs={{0,64},{64,0},{1,65},{65,1},{2,66},{66,2},{3,67},{67,3},{4,68},{68... | collective-permute-start | bytes 2359304 | tf_op jit(solution)/shard_map/gather1_z/ppermute | solution.py:99
  109.7 19.5 %collective-permute-start.28 = (bf16[128,3072]{1,0:T(8,128)(2,1)S(1)}, bf16[128,3072]{1,0:T(8,128)(2,1)S(1)}, u32[]{:S(2)}, u32[]{:S(2)}) collective-permute-start(bf16[128,3072]{1,0:T(8,128)(2,1)S(1)} %get-tuple-element.73), channel_id=1, source_target_pairs={{0,16},{16,0},{32,48},{48,32},{1,17},{17,1},{33,49},{49,33},{2,18}... | collective-permute-start | bytes 2359304 | tf_op jit(solution)/shard_map/gather1_p1/ppermute | solution.py:101
  109.7 20.0 %collective-permute-start.29 = (bf16[128,3072]{1,0:T(8,128)(2,1)S(1)}, bf16[128,3072]{1,0:T(8,128)(2,1)S(1)}, u32[]{:S(2)}, u32[]{:S(2)}) collective-permute-start(bf16[128,3072]{1,0:T(8,128)(2,1)S(1)} %get-tuple-element.74), channel_id=1, source_target_pairs={{0,48},{16,32},{32,16},{48,0},{1,49},{17,33},{33,17},{49,1},{2,50}... | collective-permute-start | bytes 2359304 | tf_op jit(solution)/shard_map/gather1_p3/ppermute | solution.py:101
  110.5 20.8 %collective-permute-start.20 = (bf16[128,3072]{1,0:T(8,128)(2,1)S(1)}, bf16[128,3072]{1,0:T(8,128)(2,1)S(1)}, u32[]{:S(2)}, u32[]{:S(2)}) collective-permute-start(bf16[128,3072]{1,0:T(8,128)(2,1)S(1)} %get-tuple-element.67.refs_0_), channel_id=1, source_target_pairs={{0,8},{8,0},{1,9},{9,1},{2,10},{10,2},{3,11},{11,3},{4,12},{12,4},... | collective-permute-start | bytes 2359304 | tf_op jit(solution)/shard_map/gather1_0_core/ppermute | solution.py:106
  114.4 16.9 %collective-permute-start.22 = (bf16[128,3072]{1,0:T(8,128)(2,1)S(1)}, bf16[128,3072]{1,0:T(8,128)(2,1)S(1)}, u32[]{:S(2)}, u32[]{:S(2)}) collective-permute-start(bf16[128,3072]{1,0:T(8,128)(2,1)S(1)} %collective-permute-done.21.refs_2_.refs_1_), channel_id=1, source_target_pairs={{0,8},{8,0},{1,9},{9,1},{2,10},{10,2},{3,11},{11,3},{4,12},{12,4},... | collective-permute-start | bytes 2359304 | tf_op jit(solution)/shard_map/gather1_1_core/ppermute | solution.py:106
  125.1 7.1 %collective-permute-start.24 = (bf16[128,3072]{1,0:T(8,128)(2,1)S(1)}, bf16[128,3072]{1,0:T(8,128)(2,1)S(1)}, u32[]{:S(2)}, u32[]{:S(2)}) collective-permute-start(bf16[128,3072]{1,0:T(8,128)(2,1)S(1)} %collective-permute-done.23.refs_4_.refs_2_), channel_id=1, source_target_pairs={{0,8},{8,0},{1,9},{9,1},{2,10},{10,2},{3,11},{11,3},{4,12},{12,4},... | collective-permute-start | bytes 2359304 | tf_op jit(solution)/shard_map/gather1_2_core/ppermute | solution.py:106
  129.7 11.0 %collective-permute-start.32 = (bf16[64,3072]{1,0:T(8,128)(2,1)S(1)}, bf16[64,3072]{1,0:T(8,128)(2,1)S(1)}, u32[]{:S(2)}, u32[]{:S(2)}) collective-permute-start(bf16[64,3072]{1,0:T(8,128)(2,1)S(1)} %get-tuple-element.77), channel_id=1, source_target_pairs={{0,64},{64,0},{1,65},{65,1},{2,66},{66,2},{3,67},{67,3},{4,68},{68... | collective-permute-start | bytes 1179656 | tf_op jit(solution)/shard_map/gather2_z/ppermute | solution.py:99
  131.3 7.3 %collective-permute-start.30 = (bf16[32,3072]{1,0:T(8,128)(2,1)S(1)}, bf16[32,3072]{1,0:T(8,128)(2,1)S(1)}, u32[]{:S(2)}, u32[]{:S(2)}) collective-permute-start(bf16[32,3072]{1,0:T(8,128)(2,1)S(1)} %get-tuple-element.75), channel_id=1, source_target_pairs={{0,16},{16,0},{32,48},{48,32},{1,17},{17,1},{33,49},{49,33},{2,18}... | collective-permute-start | bytes 589832 | tf_op jit(solution)/shard_map/gather2_p1/ppermute | solution.py:101
  131.3 7.9 %collective-permute-start.31 = (bf16[32,3072]{1,0:T(8,128)(2,1)S(1)}, bf16[32,3072]{1,0:T(8,128)(2,1)S(1)}, u32[]{:S(2)}, u32[]{:S(2)}) collective-permute-start(bf16[32,3072]{1,0:T(8,128)(2,1)S(1)} %get-tuple-element.76), channel_id=1, source_target_pairs={{0,48},{16,32},{32,16},{48,0},{1,49},{17,33},{33,17},{49,1},{2,50}... | collective-permute-start | bytes 589832 | tf_op jit(solution)/shard_map/gather2_p3/ppermute | solution.py:101
  132.2 10.8 %collective-permute-start.34 = (bf16[128,3072]{1,0:T(8,128)(2,1)S(1)}, bf16[128,3072]{1,0:T(8,128)(2,1)S(1)}, u32[]{:S(2)}, u32[]{:S(2)}) collective-permute-start(bf16[128,3072]{1,0:T(8,128)(2,1)S(1)} %collective-permute-done.27.refs_0_), channel_id=1, source_target_pairs={{0,8},{8,0},{1,9},{9,1},{2,10},{10,2},{3,11},{11,3},{4,12},{12,4},... | collective-permute-start | bytes 2359304 | tf_op jit(solution)/shard_map/gather2_0_core/ppermute | solution.py:106
  133.8 9.1 %collective-permute-start.35 = (bf16[128,3072]{1,0:T(8,128)(2,1)S(1)}, bf16[128,3072]{1,0:T(8,128)(2,1)S(1)}, u32[]{:S(2)}, u32[]{:S(2)}) collective-permute-start(bf16[128,3072]{1,0:T(8,128)(2,1)S(1)} %collective-permute-done.28.refs_1_.refs_2_), channel_id=1, source_target_pairs={{0,8},{8,0},{1,9},{9,1},{2,10},{10,2},{3,11},{11,3},{4,12},{12,4},... | collective-permute-start | bytes 2359304 | tf_op jit(solution)/shard_map/gather2_1_core/ppermute | solution.py:106
  (5 other events, 23.6 us)

commit v5 on v4

--- a/solution.py
+++ b/solution.py
@@ -340,7 +340,7 @@
 def gather_rows(own, table, states):
     at = layout(OWN)
     held = {seg: (own, at[seg]) for seg in OWN}
-    news, out, token, states_out = [(own, [(seg, at[seg]) for seg in OWN])], None, (), None
+    news, out = [(own, [(seg, at[seg]) for seg in OWN])], None
     for k, plan in enumerate(GATHER):
         if k == 0:
             messages = [own] * len(plan)
@@ -355,18 +355,22 @@
         if k > 0:
             pieces = []
             for i, (x, segs) in enumerate(news):
-                pieces.extend(runs_of(x, to_other_core(x, f"gather{k}_{i}"), segs))
-            out, mark, *stored = place(out, table, pieces, f"place{k}", states)
-            states_out, states = states_out or stored, ()
-            token = token or (mark,)
+                both = runs_of(x, to_other_core(x, f"gather{k}_{i}"), segs)
+                pieces.extend(both if k == 1 else both[1::2])
+            if k == 1:
+                for x, segs in came:
+                    pieces.extend(runs_of(x, x, segs)[::2])
+                out, mark, *states = place(out, table, pieces, "place1", states)
         for x, segs in came:
             held.update({seg: (x, row) for seg, row in segs})
         news = came if k > 0 else news + came
     last = sorted((seg for _, segs in news for seg, _ in segs), key=lambda seg: START[seg[2]])
-    (x,) = build([[(SIZE[s[2]], [held[s]]) for s in last]], "copy3", after=token)
+    (x,) = build([[(SIZE[s[2]], [held[s]]) for s in last]], "copy3", after=(mark,))
     at = layout(last)
-    out, _ = place(out, table, runs_of(x, to_other_core(x, "last"), [(seg, at[seg]) for seg in last]), "place3")
-    return out, states_out
+    both = runs_of(x, to_other_core(x, "last"), [(seg, at[seg]) for seg in last])
+    out, _ = place(out, table, pieces + both[::2], "place2")
+    out, _ = place(out, table, both[1::2], "place3")
+    return out, states
 
 
 def parts_of_total(x):

time: 149 us -> 148 us (level)
  no operation moved by 1% of the time
where the time goes in v5:
time: 148 us
  waiting for transfers between devices  55.6 us (38%)
  starting transfers between devices  46.5 us (31%)
  Pallas kernels  27 us (18%)
  blocking collectives  17.8 us (12%)
    ppermute x8, waiting for transfers between devices, _send(): return lax.ppermute(x, 'ends', [(0, 1), (1, 0)])  29.4 us
    ppermute x16, waiting for transfers between devices, _send(): return lax.ppermute(x, 'dp_0', [(i, i ^ flip) for i in range(4)])  25.4 us
    all_to_all x1, blocking collectives, parts_of_total(): return lax.all_to_all(jnp.broadcast_to(x, (n, *x.shape)), axes, 0, 0)  17.8 us
    ppermute x12, starting transfers between devices, to_other_core(): return lax.ppermute(x, 'dp_1', [(0, 1), (1, 0)])  16.5 us
    ppermute x8, starting transfers between devices, _send(): return lax.ppermute(x, 'ends', [(0, 1), (1, 0)])  14.8 us
    ppermute x16, starting transfers between devices, _send(): return lax.ppermute(x, 'dp_0', [(i, i ^ flip) for i in range(4)])  13.4 us
    pallas_call x3, Pallas kernels, place(): pl.pallas_call(kernel, out_shape=[jax.ShapeDtypeStruct((2048, width), jnp...  10.4 us
    pallas_call x4, Pallas kernels, fetch(): pl.pallas_call(kernel, out_shape=[pltpu.VMEM((rows, width), jnp.bfloat16)...  10.1 us
  transfers between devices with their start and end apart: 37, of which 13 were waited for; matrix products, arithmetic and copies ran while one was open for 0% of the time, Pallas kernels for 12%

profile of v5, /device:TPU:1, one launch (start us, length us, event | category | flops | bytes accessed | tf_op | source)
XLA Modules:
  0.0 148.1 jit_solution(15902891875459083921)
XLA Ops:
  0.8 2.2 %fetch0.1.refs_0_ = bf16[384,3072]{1,0:T(8,128)(2,1)S(1)} custom-call(s32[16]{0:T(128)S(1)} %stack.67.table_ref, bf16[2048,3072]{1,0:T(8,128)(2,1)} %bitcast.27), custom_call_target="tpu_custom_call" | custom-call | bytes 4718592 | tf_op jit(solution)/shard_map/fetch0/pallas_call | solution.py:164
  3.0 1.5 %collective-permute-start = (bf16[384,3072]{1,0:T(8,128)(2,1)S(1)}, bf16[384,3072]{1,0:T(8,128)(2,1)S(1)}, u32[]{:S(2)}, u32[]{:S(2)}) collective-permute-start(bf16[384,3072]{1,0:T(8,128)(2,1)S(1)} %fetch0.1.refs_0_), channel_id=1, source_target_pairs={{0,8},{8,0},{1,9},{9,1},{2,10},{10,2},{3,11},{11,3},{4,12},{12,4},... | collective-permute-start | bytes 7077896 | tf_op jit(solution)/shard_map/first_0_core/ppermute | solution.py:106
  4.5 2.2 %fetch1.1.refs_0_ = bf16[384,3072]{1,0:T(8,128)(2,1)S(1)} custom-call(s32[16]{0:T(128)S(1)} %stack.67.table_ref, bf16[2048,3072]{1,0:T(8,128)(2,1)} %bitcast.28, bf16[384,3072]{1,0:T(8,128)(2,1)S(1)} %fetch0.1.refs_0_), custom_call_target="tpu_custom_call" | custom-call | bytes 4718592 | tf_op jit(solution)/shard_map/fetch1/pallas_call | solution.py:164
  6.7 2.8 %fetch2.1 = (bf16[192,3072]{1,0:T(8,128)(2,1)S(1)}, bf16[320,3072]{1,0:T(8,128)(2,1)S(1)}, bf16[128,3072]{1,0:T(8,128)(2,1)S(1)}) custom-call(s32[16]{0:T(128)S(1)} %stack.67.table_ref, bf16[2048,3072]{1,0:T(8,128)(2,1)} %bitcast.29, bf16[384,3072]{1,0:T(8,128)(2,1)S(1)} %fetch1.1.refs_0_), custom_call_target="tpu_custom_call" | custom-call | bytes 7864320 | tf_op jit(solution)/shard_map/fetch2/pallas_call | solution.py:164
  10.6 2.9 %collective-permute-start.4 = (bf16[64,3072]{1,0:T(8,128)(2,1)S(1)}, bf16[64,3072]{1,0:T(8,128)(2,1)S(1)}, u32[]{:S(2)}, u32[]{:S(2)}) collective-permute-start(bf16[64,3072]{1,0:T(8,128)(2,1)S(1)} %get-tuple-element.50), channel_id=1, source_target_pairs={{0,48},{16,32},{32,16},{48,0},{1,49},{17,33},{33,17},{49,1},{2,50}... | collective-permute-start | bytes 1179656 | tf_op jit(solution)/shard_map/reduce0_p3/ppermute | solution.py:101
  13.6 3.6 %collective-permute-start.9 = (bf16[64,3072]{1,0:T(8,128)(2,1)S(1)}, bf16[64,3072]{1,0:T(8,128)(2,1)S(1)}, u32[]{:S(2)}, u32[]{:S(2)}) collective-permute-start(bf16[64,3072]{1,0:T(8,128)(2,1)S(1)} %get-tuple-element.44.refs_0_), channel_id=1, source_target_pairs={{0,64},{64,0},{1,65},{65,1},{2,66},{66,2},{3,67},{67,3},{4,68},{68... | collective-permute-start | bytes 1179656 | tf_op jit(solution)/shard_map/reduce0_z/ppermute | solution.py:99
  18.1 4.8 %collective-permute-done.4.refs_2_.refs_3_ = bf16[64,3072]{1,0:T(8,128)(2,1)S(1)} collective-permute-done((bf16[64,3072]{1,0:T(8,128)(2,1)S(1)}, bf16[64,3072]{1,0:T(8,128)(2,1)S(1)}, u32[]{:S(2)}, u32[]{:S(2)}) %collective-permute-start.4) | collective-permute-done | bytes 393248 | tf_op jit(solution)/shard_map/reduce0_p3/ppermute | solution.py:101
  22.9 3.5 %collective-permute-start.5 = (bf16[64,3072]{1,0:T(8,128)(2,1)S(1)}, bf16[64,3072]{1,0:T(8,128)(2,1)S(1)}, u32[]{:S(2)}, u32[]{:S(2)}) collective-permute-start(bf16[64,3072]{1,0:T(8,128)(2,1)S(1)} %get-tuple-element.51), channel_id=1, source_target_pairs={{0,64},{64,0},{1,65},{65,1},{2,66},{66,2},{3,67},{67,3},{4,68},{68... | collective-permute-start | bytes 1179656 | tf_op jit(solution)/shard_map/reduce1_z/ppermute | solution.py:99
  26.4 1.5 %collective-permute-start.1 = (bf16[128,3072]{1,0:T(8,128)(2,1)S(1)}, bf16[128,3072]{1,0:T(8,128)(2,1)S(1)}, u32[]{:S(2)}, u32[]{:S(2)}) collective-permute-start(bf16[128,3072]{1,0:T(8,128)(2,1)S(1)} %get-tuple-element.46), channel_id=1, source_target_pairs={{0,8},{8,0},{1,9},{9,1},{2,10},{10,2},{3,11},{11,3},{4,12},{12,4},... | collective-permute-start | bytes 2359304 | tf_op jit(solution)/shard_map/second_2_core/ppermute | solution.py:106
  28.0 2.8 %fetch3.1 = (bf16[192,3072]{1,0:T(8,128)(2,1)S(1)}, bf16[320,3072]{1,0:T(8,128)(2,1)S(1)}, bf16[128,3072]{1,0:T(8,128)(2,1)S(1)}) custom-call(s32[16]{0:T(128)S(1)} %stack.67.table_ref, bf16[2048,3072]{1,0:T(8,128)(2,1)} %bitcast.30, bf16[64,3072]{1,0:T(8,128)(2,1)S(1)} %get-tuple-element.44.refs_0_), custom_call_target="tpu_custom_call" | custom-call | bytes 7864320 | tf_op jit(solution)/shard_map/fetch3/pallas_call | solution.py:164
  31.2 2.7 %collective-permute-start.10 = (bf16[64,3072]{1,0:T(8,128)(2,1)S(1)}, bf16[64,3072]{1,0:T(8,128)(2,1)S(1)}, u32[]{:S(2)}, u32[]{:S(2)}) collective-permute-start(bf16[64,3072]{1,0:T(8,128)(2,1)S(1)} %get-tuple-element.56), channel_id=1, source_target_pairs={{0,48},{16,32},{32,16},{48,0},{1,49},{17,33},{33,17},{49,1},{2,50}... | collective-permute-start | bytes 1179656 | tf_op jit(solution)/shard_map/reduce2_p3/ppermute | solution.py:101
  34.8 2.4 %collective-permute-start.13 = (bf16[64,3072]{1,0:T(8,128)(2,1)S(1)}, bf16[64,3072]{1,0:T(8,128)(2,1)S(1)}, u32[]{:S(2)}, u32[]{:S(2)}) collective-permute-start(bf16[64,3072]{1,0:T(8,128)(2,1)S(1)} %get-tuple-element.59), channel_id=1, source_target_pairs={{0,64},{64,0},{1,65},{65,1},{2,66},{66,2},{3,67},{67,3},{4,68},{68... | collective-permute-start | bytes 1179656 | tf_op jit(solution)/shard_map/reduce2_z/ppermute | solution.py:99
  39.0 3.5 %collective-permute-done.10.refs_3_ = bf16[64,3072]{1,0:T(8,128)(2,1)S(1)} collective-permute-done((bf16[64,3072]{1,0:T(8,128)(2,1)S(1)}, bf16[64,3072]{1,0:T(8,128)(2,1)S(1)}, u32[]{:S(2)}, u32[]{:S(2)}) %collective-permute-start.10) | collective-permute-done | bytes 393248 | tf_op jit(solution)/shard_map/reduce2_p3/ppermute | solution.py:101
  42.9 4.1 %collective-permute-done.12.refs_5_ = bf16[64,3072]{1,0:T(8,128)(2,1)S(1)} collective-permute-done((bf16[64,3072]{1,0:T(8,128)(2,1)S(1)}, bf16[64,3072]{1,0:T(8,128)(2,1)S(1)}, u32[]{:S(2)}, u32[]{:S(2)}) %collective-permute-start.12) | collective-permute-done | bytes 393248 | tf_op jit(solution)/shard_map/reduce2_p1/ppermute | solution.py:101
  47.0 2.7 %collective-permute-start.7 = (bf16[64,3072]{1,0:T(8,128)(2,1)S(1)}, bf16[64,3072]{1,0:T(8,128)(2,1)S(1)}, u32[]{:S(2)}, u32[]{:S(2)}) collective-permute-start(bf16[64,3072]{1,0:T(8,128)(2,1)S(1)} %get-tuple-element.53), channel_id=1, source_target_pairs={{0,48},{16,32},{32,16},{48,0},{1,49},{17,33},{33,17},{49,1},{2,50}... | collective-permute-start | bytes 1179656 | tf_op jit(solution)/shard_map/reduce3_p3/ppermute | solution.py:101
  50.3 5.1 %collective-permute-done.15.refs_6_ = bf16[64,3072]{1,0:T(8,128)(2,1)S(1)} collective-permute-done((bf16[64,3072]{1,0:T(8,128)(2,1)S(1)}, bf16[64,3072]{1,0:T(8,128)(2,1)S(1)}, u32[]{:S(2)}, u32[]{:S(2)}) %collective-permute-start.15) | collective-permute-done | bytes 393248 | tf_op jit(solution)/shard_map/reduce3_p1/ppermute | solution.py:101
  55.4 2.2 %collective-permute-done.7.refs_3_ = bf16[64,3072]{1,0:T(8,128)(2,1)S(1)} collective-permute-done((bf16[64,3072]{1,0:T(8,128)(2,1)S(1)}, bf16[64,3072]{1,0:T(8,128)(2,1)S(1)}, u32[]{:S(2)}, u32[]{:S(2)}) %collective-permute-start.7) | collective-permute-done | bytes 393248 | tf_op jit(solution)/shard_map/reduce3_p3/ppermute | solution.py:101
  57.6 4.2 %collective-permute-done.17.refs_8_ = bf16[32,3072]{1,0:T(8,128)(2,1)S(1)} collective-permute-done((bf16[32,3072]{1,0:T(8,128)(2,1)S(1)}, bf16[32,3072]{1,0:T(8,128)(2,1)S(1)}, u32[]{:S(2)}, u32[]{:S(2)}) %collective-permute-start.17) | collective-permute-done | bytes 196640 | tf_op jit(solution)/shard_map/reduce4_p3/ppermute | solution.py:101
  64.4 1.8 %collective-permute-start.19 = (f32[1,128]{1,0:T(1,128)S(1)}, f32[1,128]{1,0:T(1,128)S(1)}, u32[]{:S(2)}, u32[]{:S(2)}) collective-permute-start(f32[1,128]{1,0:T(1,128)S(1)} %bitcast.34), channel_id=1, source_target_pairs={{0,8},{8,0},{1,9},{9,1},{2,10},{10,2},{3,11},{11,3},{4,12},{12,4},... | collective-permute-start | bytes 1544 | tf_op jit(solution)/shard_map/ppermute | solution.py:378
  67.0 17.8 %all_to_all.5.parts_ref = f32[64,1,128]{2,1,0:T(1,128)S(1)} all-to-all(f32[64,1,128]{2,1,0:T(1,128)S(1)} %broadcast_in_dim.16), channel_id=1, replica_groups=mesh['ends'=2,'dp_0'=4,'dp_1'=2,'tp_0'=2,'tp_1'=4] {'ends','dp_0','tp_0'..., dimensions={0} | all-to-all | bytes 65536 | tf_op jit(solution)/shard_map/all_to_all | solution.py:381
  84.8 3.3 %adamw.1 = (bf16[128,3072]{1,0:T(8,128)(2,1)S(1)}, f32[128,3072]{1,0:T(8,128)S(1)}, f32[128,3072]{1,0:T(8,128)S(1)}, f32[128,3072]{1,0:T(8,128)S(1)}) custom-call(f32[64,1,128]{2,1,0:T(1,128)S(1)} %all_to_all.5.parts_ref, f32[128,3072]{1,0:T(8,128)} %get-tuple-element.66.refs_0_, f32[128,3072]{1,0:T(8,128)} %bitcast.31, f32[128,3072]{1,0:T(8,128)} %bitcast.32, ...), custom_call_target="tpu_custom_call" | custom-call | bytes 11796480 | tf_op jit(solution)/shard_map/adamw/pallas_call | solution.py:424
  90.3 16.7 %collective-permute-done.21.refs_1_.refs_2_ = bf16[128,3072]{1,0:T(8,128)(2,1)S(1)} collective-permute-done((bf16[128,3072]{1,0:T(8,128)(2,1)S(1)}, bf16[128,3072]{1,0:T(8,128)(2,1)S(1)}, u32[]{:S(2)}, u32[]{:S(2)}) %collective-permute-start.21) | collective-permute-done | bytes 786464 | tf_op jit(solution)/shard_map/gather0_z/ppermute | solution.py:99
  107.7 2.0 %collective-permute-start.27 = (bf16[128,3072]{1,0:T(8,128)(2,1)S(1)}, bf16[128,3072]{1,0:T(8,128)(2,1)S(1)}, u32[]{:S(2)}, u32[]{:S(2)}) collective-permute-start(bf16[128,3072]{1,0:T(8,128)(2,1)S(1)} %get-tuple-element.68), channel_id=1, source_target_pairs={{0,64},{64,0},{1,65},{65,1},{2,66},{66,2},{3,67},{67,3},{4,68},{68... | collective-permute-start | bytes 2359304 | tf_op jit(solution)/shard_map/gather1_z/ppermute | solution.py:99
  110.5 3.9 %collective-permute-start.20 = (bf16[128,3072]{1,0:T(8,128)(2,1)S(1)}, bf16[128,3072]{1,0:T(8,128)(2,1)S(1)}, u32[]{:S(2)}, u32[]{:S(2)}) collective-permute-start(bf16[128,3072]{1,0:T(8,128)(2,1)S(1)} %get-tuple-element.67.refs_0_), channel_id=1, source_target_pairs={{0,8},{8,0},{1,9},{9,1},{2,10},{10,2},{3,11},{11,3},{4,12},{12,4},... | collective-permute-start | bytes 2359304 | tf_op jit(solution)/shard_map/gather1_0_core/ppermute | solution.py:106
  114.4 10.7 %collective-permute-done.27.refs_8_.refs_0_ = bf16[128,3072]{1,0:T(8,128)(2,1)S(1)} collective-permute-done((bf16[128,3072]{1,0:T(8,128)(2,1)S(1)}, bf16[128,3072]{1,0:T(8,128)(2,1)S(1)}, u32[]{:S(2)}, u32[]{:S(2)}) %collective-permute-start.27) | collective-permute-done | bytes 786464 | tf_op jit(solution)/shard_map/gather1_z/ppermute | solution.py:99
  125.1 4.1 %collective-permute-start.24 = (bf16[128,3072]{1,0:T(8,128)(2,1)S(1)}, bf16[128,3072]{1,0:T(8,128)(2,1)S(1)}, u32[]{:S(2)}, u32[]{:S(2)}) collective-permute-start(bf16[128,3072]{1,0:T(8,128)(2,1)S(1)} %collective-permute-done.23.refs_2_.refs_4_), channel_id=1, source_target_pairs={{0,8},{8,0},{1,9},{9,1},{2,10},{10,2},{3,11},{11,3},{4,12},{12,4},... | collective-permute-start | bytes 2359304 | tf_op jit(solution)/shard_map/gather1_2_core/ppermute | solution.py:106
  129.7 1.6 %collective-permute-start.32 = (bf16[64,3072]{1,0:T(8,128)(2,1)S(1)}, bf16[64,3072]{1,0:T(8,128)(2,1)S(1)}, u32[]{:S(2)}, u32[]{:S(2)}) collective-permute-start(bf16[64,3072]{1,0:T(8,128)(2,1)S(1)} %get-tuple-element.77), channel_id=1, source_target_pairs={{0,64},{64,0},{1,65},{65,1},{2,66},{66,2},{3,67},{67,3},{4,68},{68... | collective-permute-start | bytes 1179656 | tf_op jit(solution)/shard_map/gather2_z/ppermute | solution.py:99
  132.2 1.6 %collective-permute-start.34 = (bf16[128,3072]{1,0:T(8,128)(2,1)S(1)}, bf16[128,3072]{1,0:T(8,128)(2,1)S(1)}, u32[]{:S(2)}, u32[]{:S(2)}) collective-permute-start(bf16[128,3072]{1,0:T(8,128)(2,1)S(1)} %collective-permute-done.27.refs_8_.refs_0_), channel_id=1, source_target_pairs={{0,8},{8,0},{1,9},{9,1},{2,10},{10,2},{3,11},{11,3},{4,12},{12,4},... | collective-permute-start | bytes 2359304 | tf_op jit(solution)/shard_map/gather2_0_core/ppermute | solution.py:106
  133.9 5.5 %place1.1 = (bf16[2048,3072]{1,0:T(8,128)(2,1)}, bf16[8,128]{1,0:T(8,128)(2,1)S(1)}, f32[128,3072]{1,0:T(8,128)}, f32[128,3072]{1,0:T(8,128)}, f32[128,3072]{1,0:T(8,128)}) custom-call(s32[16]{0:T(128)S(1)} %stack.67.table_ref, bf16[128,3072]{1,0:T(8,128)(2,1)S(1)} %get-tuple-element.67.refs_0_, bf16[128,3072]{1,0:T(8,128)(2,1)S(1)} %collective-permute-done.20.refs_1_, ...), custom_call_target="tpu_custom_call" | custom-call | bytes 17301504 | tf_op jit(solution)/shard_map/place1/pallas_call | solution.py:272
  140.7 2.2 %collective-permute-start.33 = (bf16[128,3072]{1,0:T(8,128)(2,1)S(1)}, bf16[128,3072]{1,0:T(8,128)(2,1)S(1)}, u32[]{:S(2)}, u32[]{:S(2)}) collective-permute-start(bf16[128,3072]{1,0:T(8,128)(2,1)S(1)} %copy3.1.refs_3_), channel_id=1, source_target_pairs={{0,8},{8,0},{1,9},{9,1},{2,10},{10,2},{3,11},{11,3},{4,12},{12,4},... | collective-permute-start | bytes 2359304 | tf_op jit(solution)/shard_map/last_core/ppermute | solution.py:106
  143.0 2.9 %place2.1 = (bf16[2048,3072]{1,0:T(8,128)(2,1)}, bf16[8,128]{1,0:T(8,128)(2,1)}) custom-call(s32[16]{0:T(128)S(1)} %stack.67.table_ref, bf16[128,3072]{1,0:T(8,128)(2,1)S(1)} %collective-permute-done.34.refs_0_, bf16[128,3072]{1,0:T(8,128)(2,1)S(1)} %collective-permute-done.35.refs_1_, ...), custom_call_target="tpu_custom_call", output_to_operand_aliasing={{0}: (5, {})} | custom-call | bytes 6291456 | tf_op jit(solution)/shard_map/place2/pallas_call | solution.py:272
  145.9 2.0 %place3.1 = (bf16[2048,3072]{1,0:T(8,128)(2,1)}, bf16[8,128]{1,0:T(8,128)(2,1)}) custom-call(s32[16]{0:T(128)S(1)} %stack.67.table_ref, bf16[128,3072]{1,0:T(8,128)(2,1)S(1)} %collective-permute-done.33.refs_0_, bf16[2048,3072]{1,0:T(8,128)(2,1)} %get-tuple-element.79.refs_1_), custom_call_target="tpu_custom_call", output_to_operand_aliasing={{0}: (2, {})} | custom-call | bytes 1572864 | tf_op jit(solution)/shard_map/place3/pallas_call | solution.py:272
  (63 shorter events, 15.9 us)
Async XLA Ops:
  3.0 7.1 %collective-permute-start = (bf16[384,3072]{1,0:T(8,128)(2,1)S(1)}, bf16[384,3072]{1,0:T(8,128)(2,1)S(1)}, u32[]{:S(2)}, u32[]{:S(2)}) collective-permute-start(bf16[384,3072]{1,0:T(8,128)(2,1)S(1)} %fetch0.1.refs_0_), channel_id=1, source_target_pairs={{0,8},{8,0},{1,9},{9,1},{2,10},{10,2},{3,11},{11,3},{4,12},{12,4},... | collective-permute-start | bytes 7077896 | tf_op jit(solution)/shard_map/first_0_core/ppermute | solution.py:106
  9.5 21.7 %collective-permute-start.3 = (bf16[320,3072]{1,0:T(8,128)(2,1)S(1)}, bf16[320,3072]{1,0:T(8,128)(2,1)S(1)}, u32[]{:S(2)}, u32[]{:S(2)}) collective-permute-start(bf16[320,3072]{1,0:T(8,128)(2,1)S(1)} %get-tuple-element.49), channel_id=1, source_target_pairs={{0,8},{8,0},{1,9},{9,1},{2,10},{10,2},{3,11},{11,3},{4,12},{12,4},... | collective-permute-start | bytes 5898248 | tf_op jit(solution)/shard_map/second_1_core/ppermute | solution.py:106
  9.6 7.6 %collective-permute-start.8 = (bf16[192,3072]{1,0:T(8,128)(2,1)S(1)}, bf16[192,3072]{1,0:T(8,128)(2,1)S(1)}, u32[]{:S(2)}, u32[]{:S(2)}) collective-permute-start(bf16[192,3072]{1,0:T(8,128)(2,1)S(1)} %get-tuple-element.55), channel_id=1, source_target_pairs={{0,8},{8,0},{1,9},{9,1},{2,10},{10,2},{3,11},{11,3},{4,12},{12,4},... | collective-permute-start | bytes 3538952 | tf_op jit(solution)/shard_map/second_0_core/ppermute | solution.py:106
  10.6 12.3 %collective-permute-start.4 = (bf16[64,3072]{1,0:T(8,128)(2,1)S(1)}, bf16[64,3072]{1,0:T(8,128)(2,1)S(1)}, u32[]{:S(2)}, u32[]{:S(2)}) collective-permute-start(bf16[64,3072]{1,0:T(8,128)(2,1)S(1)} %get-tuple-element.50), channel_id=1, source_target_pairs={{0,48},{16,32},{32,16},{48,0},{1,49},{17,33},{33,17},{49,1},{2,50}... | collective-permute-start | bytes 1179656 | tf_op jit(solution)/shard_map/reduce0_p3/ppermute | solution.py:101
  13.5 12.8 %collective-permute-start.6 = (bf16[64,3072]{1,0:T(8,128)(2,1)S(1)}, bf16[64,3072]{1,0:T(8,128)(2,1)S(1)}, u32[]{:S(2)}, u32[]{:S(2)}) collective-permute-start(bf16[64,3072]{1,0:T(8,128)(2,1)S(1)} %get-tuple-element.52), channel_id=1, source_target_pairs={{0,16},{16,0},{32,48},{48,32},{1,17},{17,1},{33,49},{49,33},{2,18}... | collective-permute-start | bytes 1179656 | tf_op jit(solution)/shard_map/reduce0_p1/ppermute | solution.py:101
  13.6 14.4 %collective-permute-start.9 = (bf16[64,3072]{1,0:T(8,128)(2,1)S(1)}, bf16[64,3072]{1,0:T(8,128)(2,1)S(1)}, u32[]{:S(2)}, u32[]{:S(2)}) collective-permute-start(bf16[64,3072]{1,0:T(8,128)(2,1)S(1)} %get-tuple-element.44.refs_0_), channel_id=1, source_target_pairs={{0,64},{64,0},{1,65},{65,1},{2,66},{66,2},{3,67},{67,3},{4,68},{68... | collective-permute-start | bytes 1179656 | tf_op jit(solution)/shard_map/reduce0_z/ppermute | solution.py:99
  17.2 16.8 %collective-permute-start.11 = (bf16[64,3072]{1,0:T(8,128)(2,1)S(1)}, bf16[64,3072]{1,0:T(8,128)(2,1)S(1)}, u32[]{:S(2)}, u32[]{:S(2)}) collective-permute-start(bf16[64,3072]{1,0:T(8,128)(2,1)S(1)} %get-tuple-element.57), channel_id=1, source_target_pairs={{0,48},{16,32},{32,16},{48,0},{1,49},{17,33},{33,17},{49,1},{2,50}... | collective-permute-start | bytes 1179656 | tf_op jit(solution)/shard_map/reduce1_p3/ppermute | solution.py:101
  22.9 12.0 %collective-permute-start.5 = (bf16[64,3072]{1,0:T(8,128)(2,1)S(1)}, bf16[64,3072]{1,0:T(8,128)(2,1)S(1)}, u32[]{:S(2)}, u32[]{:S(2)}) collective-permute-start(bf16[64,3072]{1,0:T(8,128)(2,1)S(1)} %get-tuple-element.51), channel_id=1, source_target_pairs={{0,64},{64,0},{1,65},{65,1},{2,66},{66,2},{3,67},{67,3},{4,68},{68... | collective-permute-start | bytes 1179656 | tf_op jit(solution)/shard_map/reduce1_z/ppermute | solution.py:99
  26.4 23.9 %collective-permute-start.1 = (bf16[128,3072]{1,0:T(8,128)(2,1)S(1)}, bf16[128,3072]{1,0:T(8,128)(2,1)S(1)}, u32[]{:S(2)}, u32[]{:S(2)}) collective-permute-start(bf16[128,3072]{1,0:T(8,128)(2,1)S(1)} %get-tuple-element.46), channel_id=1, source_target_pairs={{0,8},{8,0},{1,9},{9,1},{2,10},{10,2},{3,11},{11,3},{4,12},{12,4},... | collective-permute-start | bytes 2359304 | tf_op jit(solution)/shard_map/second_2_core/ppermute | solution.py:106
  27.9 10.7 %collective-permute-start.2 = (bf16[64,3072]{1,0:T(8,128)(2,1)S(1)}, bf16[64,3072]{1,0:T(8,128)(2,1)S(1)}, u32[]{:S(2)}, u32[]{:S(2)}) collective-permute-start(bf16[64,3072]{1,0:T(8,128)(2,1)S(1)} %get-tuple-element.47), channel_id=1, source_target_pairs={{0,16},{16,0},{32,48},{48,32},{1,17},{17,1},{33,49},{49,33},{2,18}... | collective-permute-start | bytes 1179656 | tf_op jit(solution)/shard_map/reduce1_p1/ppermute | solution.py:101
  31.2 11.2 %collective-permute-start.10 = (bf16[64,3072]{1,0:T(8,128)(2,1)S(1)}, bf16[64,3072]{1,0:T(8,128)(2,1)S(1)}, u32[]{:S(2)}, u32[]{:S(2)}) collective-permute-start(bf16[64,3072]{1,0:T(8,128)(2,1)S(1)} %get-tuple-element.56), channel_id=1, source_target_pairs={{0,48},{16,32},{32,16},{48,0},{1,49},{17,33},{33,17},{49,1},{2,50}... | collective-permute-start | bytes 1179656 | tf_op jit(solution)/shard_map/reduce2_p3/ppermute | solution.py:101
  34.0 13.0 %collective-permute-start.12 = (bf16[64,3072]{1,0:T(8,128)(2,1)S(1)}, bf16[64,3072]{1,0:T(8,128)(2,1)S(1)}, u32[]{:S(2)}, u32[]{:S(2)}) collective-permute-start(bf16[64,3072]{1,0:T(8,128)(2,1)S(1)} %get-tuple-element.58), channel_id=1, source_target_pairs={{0,16},{16,0},{32,48},{48,32},{1,17},{17,1},{33,49},{49,33},{2,18}... | collective-permute-start | bytes 1179656 | tf_op jit(solution)/shard_map/reduce2_p1/ppermute | solution.py:101
  34.8 14.9 %collective-permute-start.13 = (bf16[64,3072]{1,0:T(8,128)(2,1)S(1)}, bf16[64,3072]{1,0:T(8,128)(2,1)S(1)}, u32[]{:S(2)}, u32[]{:S(2)}) collective-permute-start(bf16[64,3072]{1,0:T(8,128)(2,1)S(1)} %get-tuple-element.59), channel_id=1, source_target_pairs={{0,64},{64,0},{1,65},{65,1},{2,66},{66,2},{3,67},{67,3},{4,68},{68... | collective-permute-start | bytes 1179656 | tf_op jit(solution)/shard_map/reduce2_z/ppermute | solution.py:99
  38.6 16.9 %collective-permute-start.15 = (bf16[64,3072]{1,0:T(8,128)(2,1)S(1)}, bf16[64,3072]{1,0:T(8,128)(2,1)S(1)}, u32[]{:S(2)}, u32[]{:S(2)}) collective-permute-start(bf16[64,3072]{1,0:T(8,128)(2,1)S(1)} %get-tuple-element.61), channel_id=1, source_target_pairs={{0,16},{16,0},{32,48},{48,32},{1,17},{17,1},{33,49},{49,33},{2,18}... | collective-permute-start | bytes 1179656 | tf_op jit(solution)/shard_map/reduce3_p1/ppermute | solution.py:101
  42.4 13.0 %collective-permute-start.16 = (bf16[64,3072]{1,0:T(8,128)(2,1)S(1)}, bf16[64,3072]{1,0:T(8,128)(2,1)S(1)}, u32[]{:S(2)}, u32[]{:S(2)}) collective-permute-start(bf16[64,3072]{1,0:T(8,128)(2,1)S(1)} %get-tuple-element.62), channel_id=1, source_target_pairs={{0,64},{64,0},{1,65},{65,1},{2,66},{66,2},{3,67},{67,3},{4,68},{68... | collective-permute-start | bytes 1179656 | tf_op jit(solution)/shard_map/reduce3_z/ppermute | solution.py:99
  47.0 10.6 %collective-permute-start.7 = (bf16[64,3072]{1,0:T(8,128)(2,1)S(1)}, bf16[64,3072]{1,0:T(8,128)(2,1)S(1)}, u32[]{:S(2)}, u32[]{:S(2)}) collective-permute-start(bf16[64,3072]{1,0:T(8,128)(2,1)S(1)} %get-tuple-element.53), channel_id=1, source_target_pairs={{0,48},{16,32},{32,16},{48,0},{1,49},{17,33},{33,17},{49,1},{2,50}... | collective-permute-start | bytes 1179656 | tf_op jit(solution)/shard_map/reduce3_p3/ppermute | solution.py:101
  50.1 12.9 %collective-permute-start.14 = (bf16[64,3072]{1,0:T(8,128)(2,1)S(1)}, bf16[64,3072]{1,0:T(8,128)(2,1)S(1)}, u32[]{:S(2)}, u32[]{:S(2)}) collective-permute-start(bf16[64,3072]{1,0:T(8,128)(2,1)S(1)} %get-tuple-element.60), channel_id=1, source_target_pairs={{0,64},{64,0},{1,65},{65,1},{2,66},{66,2},{3,67},{67,3},{4,68},{68... | collective-permute-start | bytes 1179656 | tf_op jit(solution)/shard_map/reduce4_z/ppermute | solution.py:99
  50.3 11.6 %collective-permute-start.17 = (bf16[32,3072]{1,0:T(8,128)(2,1)S(1)}, bf16[32,3072]{1,0:T(8,128)(2,1)S(1)}, u32[]{:S(2)}, u32[]{:S(2)}) collective-permute-start(bf16[32,3072]{1,0:T(8,128)(2,1)S(1)} %get-tuple-element.63), channel_id=1, source_target_pairs={{0,48},{16,32},{32,16},{48,0},{1,49},{17,33},{33,17},{49,1},{2,50}... | collective-permute-start | bytes 589832 | tf_op jit(solution)/shard_map/reduce4_p3/ppermute | solution.py:101
  88.1 18.9 %collective-permute-start.21 = (bf16[128,3072]{1,0:T(8,128)(2,1)S(1)}, bf16[128,3072]{1,0:T(8,128)(2,1)S(1)}, u32[]{:S(2)}, u32[]{:S(2)}) collective-permute-start(bf16[128,3072]{1,0:T(8,128)(2,1)S(1)} %get-tuple-element.67.refs_0_), channel_id=1, source_target_pairs={{0,64},{64,0},{1,65},{65,1},{2,66},{66,2},{3,67},{67,3},{4,68},{68... | collective-permute-start | bytes 2359304 | tf_op jit(solution)/shard_map/gather0_z/ppermute | solution.py:99
  89.2 17.8 %collective-permute-start.23 = (bf16[128,3072]{1,0:T(8,128)(2,1)S(1)}, bf16[128,3072]{1,0:T(8,128)(2,1)S(1)}, u32[]{:S(2)}, u32[]{:S(2)}) collective-permute-start(bf16[128,3072]{1,0:T(8,128)(2,1)S(1)} %get-tuple-element.67.refs_0_), channel_id=1, source_target_pairs={{0,16},{16,0},{32,48},{48,32},{1,17},{17,1},{33,49},{49,33},{2,18}... | collective-permute-start | bytes 2359304 | tf_op jit(solution)/shard_map/gather0_p1/ppermute | solution.py:101
  89.6 18.0 %collective-permute-start.25 = (bf16[128,3072]{1,0:T(8,128)(2,1)S(1)}, bf16[128,3072]{1,0:T(8,128)(2,1)S(1)}, u32[]{:S(2)}, u32[]{:S(2)}) collective-permute-start(bf16[128,3072]{1,0:T(8,128)(2,1)S(1)} %get-tuple-element.67.refs_0_), channel_id=1, source_target_pairs={{0,48},{16,32},{32,16},{48,0},{1,49},{17,33},{33,17},{49,1},{2,50}... | collective-permute-start | bytes 2359304 | tf_op jit(solution)/shard_map/gather0_p3/ppermute | solution.py:101
  107.7 17.4 %collective-permute-start.27 = (bf16[128,3072]{1,0:T(8,128)(2,1)S(1)}, bf16[128,3072]{1,0:T(8,128)(2,1)S(1)}, u32[]{:S(2)}, u32[]{:S(2)}) collective-permute-start(bf16[128,3072]{1,0:T(8,128)(2,1)S(1)} %get-tuple-element.68), channel_id=1, source_target_pairs={{0,64},{64,0},{1,65},{65,1},{2,66},{66,2},{3,67},{67,3},{4,68},{68... | collective-permute-start | bytes 2359304 | tf_op jit(solution)/shard_map/gather1_z/ppermute | solution.py:99
  109.7 19.5 %collective-permute-start.28 = (bf16[128,3072]{1,0:T(8,128)(2,1)S(1)}, bf16[128,3072]{1,0:T(8,128)(2,1)S(1)}, u32[]{:S(2)}, u32[]{:S(2)}) collective-permute-start(bf16[128,3072]{1,0:T(8,128)(2,1)S(1)} %get-tuple-element.69), channel_id=1, source_target_pairs={{0,16},{16,0},{32,48},{48,32},{1,17},{17,1},{33,49},{49,33},{2,18}... | collective-permute-start | bytes 2359304 | tf_op jit(solution)/shard_map/gather1_p1/ppermute | solution.py:101
  109.7 20.0 %collective-permute-start.29 = (bf16[128,3072]{1,0:T(8,128)(2,1)S(1)}, bf16[128,3072]{1,0:T(8,128)(2,1)S(1)}, u32[]{:S(2)}, u32[]{:S(2)}) collective-permute-start(bf16[128,3072]{1,0:T(8,128)(2,1)S(1)} %get-tuple-element.70), channel_id=1, source_target_pairs={{0,48},{16,32},{32,16},{48,0},{1,49},{17,33},{33,17},{49,1},{2,50}... | collective-permute-start | bytes 2359304 | tf_op jit(solution)/shard_map/gather1_p3/ppermute | solution.py:101
  110.5 20.8 %collective-permute-start.20 = (bf16[128,3072]{1,0:T(8,128)(2,1)S(1)}, bf16[128,3072]{1,0:T(8,128)(2,1)S(1)}, u32[]{:S(2)}, u32[]{:S(2)}) collective-permute-start(bf16[128,3072]{1,0:T(8,128)(2,1)S(1)} %get-tuple-element.67.refs_0_), channel_id=1, source_target_pairs={{0,8},{8,0},{1,9},{9,1},{2,10},{10,2},{3,11},{11,3},{4,12},{12,4},... | collective-permute-start | bytes 2359304 | tf_op jit(solution)/shard_map/gather1_0_core/ppermute | solution.py:106
  114.4 16.9 %collective-permute-start.22 = (bf16[128,3072]{1,0:T(8,128)(2,1)S(1)}, bf16[128,3072]{1,0:T(8,128)(2,1)S(1)}, u32[]{:S(2)}, u32[]{:S(2)}) collective-permute-start(bf16[128,3072]{1,0:T(8,128)(2,1)S(1)} %collective-permute-done.21.refs_1_.refs_2_), channel_id=1, source_target_pairs={{0,8},{8,0},{1,9},{9,1},{2,10},{10,2},{3,11},{11,3},{4,12},{12,4},... | collective-permute-start | bytes 2359304 | tf_op jit(solution)/shard_map/gather1_1_core/ppermute | solution.py:106
  125.1 7.1 %collective-permute-start.24 = (bf16[128,3072]{1,0:T(8,128)(2,1)S(1)}, bf16[128,3072]{1,0:T(8,128)(2,1)S(1)}, u32[]{:S(2)}, u32[]{:S(2)}) collective-permute-start(bf16[128,3072]{1,0:T(8,128)(2,1)S(1)} %collective-permute-done.23.refs_2_.refs_4_), channel_id=1, source_target_pairs={{0,8},{8,0},{1,9},{9,1},{2,10},{10,2},{3,11},{11,3},{4,12},{12,4},... | collective-permute-start | bytes 2359304 | tf_op jit(solution)/shard_map/gather1_2_core/ppermute | solution.py:106
  129.7 11.0 %collective-permute-start.32 = (bf16[64,3072]{1,0:T(8,128)(2,1)S(1)}, bf16[64,3072]{1,0:T(8,128)(2,1)S(1)}, u32[]{:S(2)}, u32[]{:S(2)}) collective-permute-start(bf16[64,3072]{1,0:T(8,128)(2,1)S(1)} %get-tuple-element.77), channel_id=1, source_target_pairs={{0,64},{64,0},{1,65},{65,1},{2,66},{66,2},{3,67},{67,3},{4,68},{68... | collective-permute-start | bytes 1179656 | tf_op jit(solution)/shard_map/gather2_z/ppermute | solution.py:99
  131.3 8.1 %collective-permute-start.30 = (bf16[32,3072]{1,0:T(8,128)(2,1)S(1)}, bf16[32,3072]{1,0:T(8,128)(2,1)S(1)}, u32[]{:S(2)}, u32[]{:S(2)}) collective-permute-start(bf16[32,3072]{1,0:T(8,128)(2,1)S(1)} %get-tuple-element.75), channel_id=1, source_target_pairs={{0,16},{16,0},{32,48},{48,32},{1,17},{17,1},{33,49},{49,33},{2,18}... | collective-permute-start | bytes 589832 | tf_op jit(solution)/shard_map/gather2_p1/ppermute | solution.py:101
  131.3 8.6 %collective-permute-start.31 = (bf16[32,3072]{1,0:T(8,128)(2,1)S(1)}, bf16[32,3072]{1,0:T(8,128)(2,1)S(1)}, u32[]{:S(2)}, u32[]{:S(2)}) collective-permute-start(bf16[32,3072]{1,0:T(8,128)(2,1)S(1)} %get-tuple-element.76), channel_id=1, source_target_pairs={{0,48},{16,32},{32,16},{48,0},{1,49},{17,33},{33,17},{49,1},{2,50}... | collective-permute-start | bytes 589832 | tf_op jit(solution)/shard_map/gather2_p3/ppermute | solution.py:101
  132.2 10.8 %collective-permute-start.34 = (bf16[128,3072]{1,0:T(8,128)(2,1)S(1)}, bf16[128,3072]{1,0:T(8,128)(2,1)S(1)}, u32[]{:S(2)}, u32[]{:S(2)}) collective-permute-start(bf16[128,3072]{1,0:T(8,128)(2,1)S(1)} %collective-permute-done.27.refs_8_.refs_0_), channel_id=1, source_target_pairs={{0,8},{8,0},{1,9},{9,1},{2,10},{10,2},{3,11},{11,3},{4,12},{12,4},... | collective-permute-start | bytes 2359304 | tf_op jit(solution)/shard_map/gather2_0_core/ppermute | solution.py:106
  133.8 9.1 %collective-permute-start.35 = (bf16[128,3072]{1,0:T(8,128)(2,1)S(1)}, bf16[128,3072]{1,0:T(8,128)(2,1)S(1)}, u32[]{:S(2)}, u32[]{:S(2)}) collective-permute-start(bf16[128,3072]{1,0:T(8,128)(2,1)S(1)} %collective-permute-done.28.refs_9_.refs_1_), channel_id=1, source_target_pairs={{0,8},{8,0},{1,9},{9,1},{2,10},{10,2},{3,11},{11,3},{4,12},{12,4},... | collective-permute-start | bytes 2359304 | tf_op jit(solution)/shard_map/gather2_1_core/ppermute | solution.py:106
  (5 other events, 22.3 us)

commit v6 on v5

--- a/solution.py
+++ b/solution.py
@@ -305,13 +305,14 @@
     others = fetch(grad, table, first, 1, None, "fetch0")
     owns = fetch(grad, table, first, 0, others[0], "fetch1")
     cross(first, others, owns, "first")
-    others = fetch(grad, table, second, 1, owns[0], "fetch2")
+    others = fetch(grad, table, second[:-1], 1, owns[0], "fetch2")
     for rounds in BUILT_TOGETHER:
         plan = [item for k in rounds for item in REDUCE[k].items()]
         lists = [[(SIZE[seg[2]], held[seg]) for seg in segs] for _, segs in plan]
         messages = build(lists, f"sum{rounds[0]}")
         if rounds[0] == 0:
             owns = fetch(grad, table, second, 0, messages[0], "fetch3")
+            others += fetch(grad, table, second[-1:], 1, owns[0], "fetch4")
             cross(second, others, owns, "second")
         for k, ((link, segs), x) in enumerate(zip(plan, messages)):
             at = layout(segs)

time: 148 us -> 146 us (0.986)
  waiting for transfers between devices: 55.6 us -> 49.8 us
  starting transfers between devices: 46.5 us -> 52.1 us
  blocking collectives: 17.8 us -> 14.4 us
    ppermute x16, waiting for transfers between devices: 25.4 us -> 20.8 us  [_send(): return lax.ppermute(x, 'dp_0', [(i, i ^ flip) for i in range(4)])]
    all_to_all x1, blocking collectives: 17.8 us -> 14.4 us  [parts_of_total(): return lax.all_to_all(jnp.broadcast_to(x, (n, *x.shape)), axes, 0, 0)]
    ppermute x1, starting transfers between devices: 1.78 us -> 3.76 us  [parts_of_total(): x = x + lax.ppermute(x, 'dp_1', [(0, 1), (1, 0)])]
    ppermute x16, starting transfers between devices: 13.4 us -> 15.3 us  [_send(): return lax.ppermute(x, 'dp_0', [(i, i ^ flip) for i in range(4)])]
    pallas_call x4 -> x5, Pallas kernels: 10.1 us -> 11.5 us  [fetch(): pl.pallas_call(kernel, out_shape=[pltpu.VMEM((rows, width), jnp.bfloat16)...]
  transfers between devices with their start and end apart: 37 -> 37, of which waited for: 13 -> 12; matrix products, arithmetic and copies ran while one was open for 0% -> 0% of each run, Pallas kernels for 12% -> 13%
where the time goes in v6:
time: 146 us
  starting transfers between devices  52.1 us (36%)
  waiting for transfers between devices  49.8 us (34%)
  Pallas kernels  28.4 us (19%)
  blocking collectives  14.4 us (10%)
    ppermute x8, waiting for transfers between devices, _send(): return lax.ppermute(x, 'ends', [(0, 1), (1, 0)])  28.2 us
    ppermute x16, waiting for transfers between devices, _send(): return lax.ppermute(x, 'dp_0', [(i, i ^ flip) for i in range(4)])  20.8 us
    ppermute x12, starting transfers between devices, to_other_core(): return lax.ppermute(x, 'dp_1', [(0, 1), (1, 0)])  17.5 us
    ppermute x8, starting transfers between devices, _send(): return lax.ppermute(x, 'ends', [(0, 1), (1, 0)])  15.5 us
    ppermute x16, starting transfers between devices, _send(): return lax.ppermute(x, 'dp_0', [(i, i ^ flip) for i in range(4)])  15.3 us
    all_to_all x1, blocking collectives, parts_of_total(): return lax.all_to_all(jnp.broadcast_to(x, (n, *x.shape)), axes, 0, 0)  14.4 us
    pallas_call x5, Pallas kernels, fetch(): pl.pallas_call(kernel, out_shape=[pltpu.VMEM((rows, width), jnp.bfloat16)...  11.5 us
    pallas_call x3, Pallas kernels, place(): pl.pallas_call(kernel, out_shape=[jax.ShapeDtypeStruct((2048, width), jnp...  10.4 us
  transfers between devices with their start and end apart: 37, of which 12 were waited for; matrix products, arithmetic and copies ran while one was open for 0% of the time, Pallas kernels for 13%

profile of v6, /device:TPU:1, one launch (start us, length us, event | category | flops | bytes accessed | tf_op | source)
XLA Modules:
  0.0 146.0 jit_solution(4048840702228220753)
XLA Ops:
  0.8 2.2 %fetch0.1.refs_0_ = bf16[384,3072]{1,0:T(8,128)(2,1)S(1)} custom-call(s32[16]{0:T(128)S(1)} %stack.67.table_ref, bf16[2048,3072]{1,0:T(8,128)(2,1)} %bitcast.27), custom_call_target="tpu_custom_call" | custom-call | bytes 4718592 | tf_op jit(solution)/shard_map/fetch0/pallas_call | solution.py:164
  3.0 1.5 %collective-permute-start = (bf16[384,3072]{1,0:T(8,128)(2,1)S(1)}, bf16[384,3072]{1,0:T(8,128)(2,1)S(1)}, u32[]{:S(2)}, u32[]{:S(2)}) collective-permute-start(bf16[384,3072]{1,0:T(8,128)(2,1)S(1)} %fetch0.1.refs_0_), channel_id=1, source_target_pairs={{0,8},{8,0},{1,9},{9,1},{2,10},{10,2},{3,11},{11,3},{4,12},{12,4},... | collective-permute-start | bytes 7077896 | tf_op jit(solution)/shard_map/first_0_core/ppermute | solution.py:106
  4.5 2.2 %fetch1.1.refs_0_ = bf16[384,3072]{1,0:T(8,128)(2,1)S(1)} custom-call(s32[16]{0:T(128)S(1)} %stack.67.table_ref, bf16[2048,3072]{1,0:T(8,128)(2,1)} %bitcast.28, bf16[384,3072]{1,0:T(8,128)(2,1)S(1)} %fetch0.1.refs_0_), custom_call_target="tpu_custom_call" | custom-call | bytes 4718592 | tf_op jit(solution)/shard_map/fetch1/pallas_call | solution.py:164
  6.7 2.6 %fetch2.1 = (bf16[192,3072]{1,0:T(8,128)(2,1)S(1)}, bf16[320,3072]{1,0:T(8,128)(2,1)S(1)}) custom-call(s32[16]{0:T(128)S(1)} %stack.67.table_ref, bf16[2048,3072]{1,0:T(8,128)(2,1)} %bitcast.29, bf16[384,3072]{1,0:T(8,128)(2,1)S(1)} %fetch1.1.refs_0_), custom_call_target="tpu_custom_call" | custom-call | bytes 6291456 | tf_op jit(solution)/shard_map/fetch2/pallas_call | solution.py:164
  10.4 2.9 %collective-permute-start.4 = (bf16[64,3072]{1,0:T(8,128)(2,1)S(1)}, bf16[64,3072]{1,0:T(8,128)(2,1)S(1)}, u32[]{:S(2)}, u32[]{:S(2)}) collective-permute-start(bf16[64,3072]{1,0:T(8,128)(2,1)S(1)} %get-tuple-element.49), channel_id=1, source_target_pairs={{0,48},{16,32},{32,16},{48,0},{1,49},{17,33},{33,17},{49,1},{2,50}... | collective-permute-start | bytes 1179656 | tf_op jit(solution)/shard_map/reduce0_p3/ppermute | solution.py:101
  13.3 3.6 %collective-permute-start.9 = (bf16[64,3072]{1,0:T(8,128)(2,1)S(1)}, bf16[64,3072]{1,0:T(8,128)(2,1)S(1)}, u32[]{:S(2)}, u32[]{:S(2)}) collective-permute-start(bf16[64,3072]{1,0:T(8,128)(2,1)S(1)} %get-tuple-element.43.refs_0_), channel_id=1, source_target_pairs={{0,64},{64,0},{1,65},{65,1},{2,66},{66,2},{3,67},{67,3},{4,68},{68... | collective-permute-start | bytes 1179656 | tf_op jit(solution)/shard_map/reduce0_z/ppermute | solution.py:99
  17.8 4.8 %collective-permute-done.4.refs_2_.refs_3_ = bf16[64,3072]{1,0:T(8,128)(2,1)S(1)} collective-permute-done((bf16[64,3072]{1,0:T(8,128)(2,1)S(1)}, bf16[64,3072]{1,0:T(8,128)(2,1)S(1)}, u32[]{:S(2)}, u32[]{:S(2)}) %collective-permute-start.4) | collective-permute-done | bytes 393248 | tf_op jit(solution)/shard_map/reduce0_p3/ppermute | solution.py:101
  22.6 3.5 %collective-permute-start.5 = (bf16[64,3072]{1,0:T(8,128)(2,1)S(1)}, bf16[64,3072]{1,0:T(8,128)(2,1)S(1)}, u32[]{:S(2)}, u32[]{:S(2)}) collective-permute-start(bf16[64,3072]{1,0:T(8,128)(2,1)S(1)} %get-tuple-element.50), channel_id=1, source_target_pairs={{0,64},{64,0},{1,65},{65,1},{2,66},{66,2},{3,67},{67,3},{4,68},{68... | collective-permute-start | bytes 1179656 | tf_op jit(solution)/shard_map/reduce1_z/ppermute | solution.py:99
  26.1 2.8 %fetch3.1 = (bf16[192,3072]{1,0:T(8,128)(2,1)S(1)}, bf16[320,3072]{1,0:T(8,128)(2,1)S(1)}, bf16[128,3072]{1,0:T(8,128)(2,1)S(1)}) custom-call(s32[16]{0:T(128)S(1)} %stack.67.table_ref, bf16[2048,3072]{1,0:T(8,128)(2,1)} %bitcast.30, bf16[64,3072]{1,0:T(8,128)(2,1)S(1)} %get-tuple-element.43.refs_0_), custom_call_target="tpu_custom_call" | custom-call | bytes 7864320 | tf_op jit(solution)/shard_map/fetch3/pallas_call | solution.py:164
  29.5 2.7 %collective-permute-start.10 = (bf16[64,3072]{1,0:T(8,128)(2,1)S(1)}, bf16[64,3072]{1,0:T(8,128)(2,1)S(1)}, u32[]{:S(2)}, u32[]{:S(2)}) collective-permute-start(bf16[64,3072]{1,0:T(8,128)(2,1)S(1)} %get-tuple-element.54), channel_id=1, source_target_pairs={{0,48},{16,32},{32,16},{48,0},{1,49},{17,33},{33,17},{49,1},{2,50}... | collective-permute-start | bytes 1179656 | tf_op jit(solution)/shard_map/reduce2_p3/ppermute | solution.py:101
  32.2 1.7 %fetch4.1 = bf16[128,3072]{1,0:T(8,128)(2,1)S(1)} custom-call(s32[16]{0:T(128)S(1)} %stack.67.table_ref, bf16[2048,3072]{1,0:T(8,128)(2,1)} %bitcast.31, bf16[192,3072]{1,0:T(8,128)(2,1)S(1)} %get-tuple-element.45.refs_0_), custom_call_target="tpu_custom_call" | custom-call | bytes 1572864 | tf_op jit(solution)/shard_map/fetch4/pallas_call | solution.py:164
  34.8 2.5 %collective-permute-start.1 = (bf16[128,3072]{1,0:T(8,128)(2,1)S(1)}, bf16[128,3072]{1,0:T(8,128)(2,1)S(1)}, u32[]{:S(2)}, u32[]{:S(2)}) collective-permute-start(bf16[128,3072]{1,0:T(8,128)(2,1)S(1)} %fetch4.1), channel_id=1, source_target_pairs={{0,8},{8,0},{1,9},{9,1},{2,10},{10,2},{3,11},{11,3},{4,12},{12,4},... | collective-permute-start | bytes 2359304 | tf_op jit(solution)/shard_map/second_2_core/ppermute | solution.py:106
  39.5 3.3 %collective-permute-start.16 = (bf16[64,3072]{1,0:T(8,128)(2,1)S(1)}, bf16[64,3072]{1,0:T(8,128)(2,1)S(1)}, u32[]{:S(2)}, u32[]{:S(2)}) collective-permute-start(bf16[64,3072]{1,0:T(8,128)(2,1)S(1)} %get-tuple-element.60), channel_id=1, source_target_pairs={{0,64},{64,0},{1,65},{65,1},{2,66},{66,2},{3,67},{67,3},{4,68},{68... | collective-permute-start | bytes 1179656 | tf_op jit(solution)/shard_map/reduce3_z/ppermute | solution.py:99
  42.8 3.8 %collective-permute-done.12.refs_5_ = bf16[64,3072]{1,0:T(8,128)(2,1)S(1)} collective-permute-done((bf16[64,3072]{1,0:T(8,128)(2,1)S(1)}, bf16[64,3072]{1,0:T(8,128)(2,1)S(1)}, u32[]{:S(2)}, u32[]{:S(2)}) %collective-permute-start.12) | collective-permute-done | bytes 393248 | tf_op jit(solution)/shard_map/reduce2_p1/ppermute | solution.py:101
  46.6 2.5 %collective-permute-start.7 = (bf16[64,3072]{1,0:T(8,128)(2,1)S(1)}, bf16[64,3072]{1,0:T(8,128)(2,1)S(1)}, u32[]{:S(2)}, u32[]{:S(2)}) collective-permute-start(bf16[64,3072]{1,0:T(8,128)(2,1)S(1)} %get-tuple-element.52), channel_id=1, source_target_pairs={{0,48},{16,32},{32,16},{48,0},{1,49},{17,33},{33,17},{49,1},{2,50}... | collective-permute-start | bytes 1179656 | tf_op jit(solution)/shard_map/reduce3_p3/ppermute | solution.py:101
  49.9 5.1 %collective-permute-done.15.refs_6_ = bf16[64,3072]{1,0:T(8,128)(2,1)S(1)} collective-permute-done((bf16[64,3072]{1,0:T(8,128)(2,1)S(1)}, bf16[64,3072]{1,0:T(8,128)(2,1)S(1)}, u32[]{:S(2)}, u32[]{:S(2)}) %collective-permute-start.15) | collective-permute-done | bytes 393248 | tf_op jit(solution)/shard_map/reduce3_p1/ppermute | solution.py:101
  55.0 2.5 %collective-permute-start.17 = (bf16[32,3072]{1,0:T(8,128)(2,1)S(1)}, bf16[32,3072]{1,0:T(8,128)(2,1)S(1)}, u32[]{:S(2)}, u32[]{:S(2)}) collective-permute-start(bf16[32,3072]{1,0:T(8,128)(2,1)S(1)} %get-tuple-element.61), channel_id=1, source_target_pairs={{0,48},{16,32},{32,16},{48,0},{1,49},{17,33},{33,17},{49,1},{2,50}... | collective-permute-start | bytes 589832 | tf_op jit(solution)/shard_map/reduce4_p3/ppermute | solution.py:101
  57.5 4.2 %collective-permute-done.17.refs_8_ = bf16[32,3072]{1,0:T(8,128)(2,1)S(1)} collective-permute-done((bf16[32,3072]{1,0:T(8,128)(2,1)S(1)}, bf16[32,3072]{1,0:T(8,128)(2,1)S(1)}, u32[]{:S(2)}, u32[]{:S(2)}) %collective-permute-start.17) | collective-permute-done | bytes 196640 | tf_op jit(solution)/shard_map/reduce4_p3/ppermute | solution.py:101
  63.7 3.8 %collective-permute-start.19 = (f32[1,128]{1,0:T(1,128)S(1)}, f32[1,128]{1,0:T(1,128)S(1)}, u32[]{:S(2)}, u32[]{:S(2)}) collective-permute-start(f32[1,128]{1,0:T(1,128)S(1)} %bitcast.35), channel_id=1, source_target_pairs={{0,8},{8,0},{1,9},{9,1},{2,10},{10,2},{3,11},{11,3},{4,12},{12,4},... | collective-permute-start | bytes 1544 | tf_op jit(solution)/shard_map/ppermute | solution.py:379
  68.3 14.4 %all_to_all.5.parts_ref = f32[64,1,128]{2,1,0:T(1,128)S(1)} all-to-all(f32[64,1,128]{2,1,0:T(1,128)S(1)} %broadcast_in_dim.16), channel_id=1, replica_groups=mesh['ends'=2,'dp_0'=4,'dp_1'=2,'tp_0'=2,'tp_1'=4] {'ends','dp_0','tp_0'..., dimensions={0} | all-to-all | bytes 65536 | tf_op jit(solution)/shard_map/all_to_all | solution.py:382
  82.7 3.3 %adamw.1 = (bf16[128,3072]{1,0:T(8,128)(2,1)S(1)}, f32[128,3072]{1,0:T(8,128)S(1)}, f32[128,3072]{1,0:T(8,128)S(1)}, f32[128,3072]{1,0:T(8,128)S(1)}) custom-call(f32[64,1,128]{2,1,0:T(1,128)S(1)} %all_to_all.5.parts_ref, f32[128,3072]{1,0:T(8,128)} %get-tuple-element.64.refs_0_, f32[128,3072]{1,0:T(8,128)} %bitcast.32, f32[128,3072]{1,0:T(8,128)} %bitcast.33, ...), custom_call_target="tpu_custom_call" | custom-call | bytes 11796480 | tf_op jit(solution)/shard_map/adamw/pallas_call | solution.py:425
  88.2 16.7 %collective-permute-done.21.refs_1_.refs_2_ = bf16[128,3072]{1,0:T(8,128)(2,1)S(1)} collective-permute-done((bf16[128,3072]{1,0:T(8,128)(2,1)S(1)}, bf16[128,3072]{1,0:T(8,128)(2,1)S(1)}, u32[]{:S(2)}, u32[]{:S(2)}) %collective-permute-start.21) | collective-permute-done | bytes 786464 | tf_op jit(solution)/shard_map/gather0_z/ppermute | solution.py:99
  105.6 2.0 %collective-permute-start.27 = (bf16[128,3072]{1,0:T(8,128)(2,1)S(1)}, bf16[128,3072]{1,0:T(8,128)(2,1)S(1)}, u32[]{:S(2)}, u32[]{:S(2)}) collective-permute-start(bf16[128,3072]{1,0:T(8,128)(2,1)S(1)} %get-tuple-element.66), channel_id=1, source_target_pairs={{0,64},{64,0},{1,65},{65,1},{2,66},{66,2},{3,67},{67,3},{4,68},{68... | collective-permute-start | bytes 2359304 | tf_op jit(solution)/shard_map/gather1_z/ppermute | solution.py:99
  108.4 3.9 %collective-permute-start.20 = (bf16[128,3072]{1,0:T(8,128)(2,1)S(1)}, bf16[128,3072]{1,0:T(8,128)(2,1)S(1)}, u32[]{:S(2)}, u32[]{:S(2)}) collective-permute-start(bf16[128,3072]{1,0:T(8,128)(2,1)S(1)} %get-tuple-element.65.refs_0_), channel_id=1, source_target_pairs={{0,8},{8,0},{1,9},{9,1},{2,10},{10,2},{3,11},{11,3},{4,12},{12,4},... | collective-permute-start | bytes 2359304 | tf_op jit(solution)/shard_map/gather1_0_core/ppermute | solution.py:106
  112.3 10.7 %collective-permute-done.27.refs_8_.refs_0_ = bf16[128,3072]{1,0:T(8,128)(2,1)S(1)} collective-permute-done((bf16[128,3072]{1,0:T(8,128)(2,1)S(1)}, bf16[128,3072]{1,0:T(8,128)(2,1)S(1)}, u32[]{:S(2)}, u32[]{:S(2)}) %collective-permute-start.27) | collective-permute-done | bytes 786464 | tf_op jit(solution)/shard_map/gather1_z/ppermute | solution.py:99
  123.0 4.1 %collective-permute-start.24 = (bf16[128,3072]{1,0:T(8,128)(2,1)S(1)}, bf16[128,3072]{1,0:T(8,128)(2,1)S(1)}, u32[]{:S(2)}, u32[]{:S(2)}) collective-permute-start(bf16[128,3072]{1,0:T(8,128)(2,1)S(1)} %collective-permute-done.23.refs_2_.refs_4_), channel_id=1, source_target_pairs={{0,8},{8,0},{1,9},{9,1},{2,10},{10,2},{3,11},{11,3},{4,12},{12,4},... | collective-permute-start | bytes 2359304 | tf_op jit(solution)/shard_map/gather1_2_core/ppermute | solution.py:106
  127.6 1.6 %collective-permute-start.32 = (bf16[64,3072]{1,0:T(8,128)(2,1)S(1)}, bf16[64,3072]{1,0:T(8,128)(2,1)S(1)}, u32[]{:S(2)}, u32[]{:S(2)}) collective-permute-start(bf16[64,3072]{1,0:T(8,128)(2,1)S(1)} %get-tuple-element.75), channel_id=1, source_target_pairs={{0,64},{64,0},{1,65},{65,1},{2,66},{66,2},{3,67},{67,3},{4,68},{68... | collective-permute-start | bytes 1179656 | tf_op jit(solution)/shard_map/gather2_z/ppermute | solution.py:99
  130.1 1.6 %collective-permute-start.34 = (bf16[128,3072]{1,0:T(8,128)(2,1)S(1)}, bf16[128,3072]{1,0:T(8,128)(2,1)S(1)}, u32[]{:S(2)}, u32[]{:S(2)}) collective-permute-start(bf16[128,3072]{1,0:T(8,128)(2,1)S(1)} %collective-permute-done.27.refs_8_.refs_0_), channel_id=1, source_target_pairs={{0,8},{8,0},{1,9},{9,1},{2,10},{10,2},{3,11},{11,3},{4,12},{12,4},... | collective-permute-start | bytes 2359304 | tf_op jit(solution)/shard_map/gather2_0_core/ppermute | solution.py:106
  131.8 5.5 %place1.1 = (bf16[2048,3072]{1,0:T(8,128)(2,1)}, bf16[8,128]{1,0:T(8,128)(2,1)S(1)}, f32[128,3072]{1,0:T(8,128)}, f32[128,3072]{1,0:T(8,128)}, f32[128,3072]{1,0:T(8,128)}) custom-call(s32[16]{0:T(128)S(1)} %stack.67.table_ref, bf16[128,3072]{1,0:T(8,128)(2,1)S(1)} %get-tuple-element.65.refs_0_, bf16[128,3072]{1,0:T(8,128)(2,1)S(1)} %collective-permute-done.20.refs_1_, ...), custom_call_target="tpu_custom_call" | custom-call | bytes 17301504 | tf_op jit(solution)/shard_map/place1/pallas_call | solution.py:272
  138.6 2.2 %collective-permute-start.33 = (bf16[128,3072]{1,0:T(8,128)(2,1)S(1)}, bf16[128,3072]{1,0:T(8,128)(2,1)S(1)}, u32[]{:S(2)}, u32[]{:S(2)}) collective-permute-start(bf16[128,3072]{1,0:T(8,128)(2,1)S(1)} %copy3.1.refs_3_), channel_id=1, source_target_pairs={{0,8},{8,0},{1,9},{9,1},{2,10},{10,2},{3,11},{11,3},{4,12},{12,4},... | collective-permute-start | bytes 2359304 | tf_op jit(solution)/shard_map/last_core/ppermute | solution.py:106
  140.9 2.9 %place2.1 = (bf16[2048,3072]{1,0:T(8,128)(2,1)}, bf16[8,128]{1,0:T(8,128)(2,1)}) custom-call(s32[16]{0:T(128)S(1)} %stack.67.table_ref, bf16[128,3072]{1,0:T(8,128)(2,1)S(1)} %collective-permute-done.34.refs_0_, bf16[128,3072]{1,0:T(8,128)(2,1)S(1)} %collective-permute-done.35.refs_1_, ...), custom_call_target="tpu_custom_call", output_to_operand_aliasing={{0}: (5, {})} | custom-call | bytes 6291456 | tf_op jit(solution)/shard_map/place2/pallas_call | solution.py:272
  143.8 2.0 %place3.1 = (bf16[2048,3072]{1,0:T(8,128)(2,1)}, bf16[8,128]{1,0:T(8,128)(2,1)}) custom-call(s32[16]{0:T(128)S(1)} %stack.67.table_ref, bf16[128,3072]{1,0:T(8,128)(2,1)S(1)} %collective-permute-done.33.refs_0_, bf16[2048,3072]{1,0:T(8,128)(2,1)} %get-tuple-element.77.refs_1_), custom_call_target="tpu_custom_call", output_to_operand_aliasing={{0}: (2, {})} | custom-call | bytes 1572864 | tf_op jit(solution)/shard_map/place3/pallas_call | solution.py:272
  (64 shorter events, 15.7 us)
Async XLA Ops:
  3.0 6.9 %collective-permute-start = (bf16[384,3072]{1,0:T(8,128)(2,1)S(1)}, bf16[384,3072]{1,0:T(8,128)(2,1)S(1)}, u32[]{:S(2)}, u32[]{:S(2)}) collective-permute-start(bf16[384,3072]{1,0:T(8,128)(2,1)S(1)} %fetch0.1.refs_0_), channel_id=1, source_target_pairs={{0,8},{8,0},{1,9},{9,1},{2,10},{10,2},{3,11},{11,3},{4,12},{12,4},... | collective-permute-start | bytes 7077896 | tf_op jit(solution)/shard_map/first_0_core/ppermute | solution.py:106
  9.2 24.6 %collective-permute-start.3 = (bf16[320,3072]{1,0:T(8,128)(2,1)S(1)}, bf16[320,3072]{1,0:T(8,128)(2,1)S(1)}, u32[]{:S(2)}, u32[]{:S(2)}) collective-permute-start(bf16[320,3072]{1,0:T(8,128)(2,1)S(1)} %get-tuple-element.48), channel_id=1, source_target_pairs={{0,8},{8,0},{1,9},{9,1},{2,10},{10,2},{3,11},{11,3},{4,12},{12,4},... | collective-permute-start | bytes 5898248 | tf_op jit(solution)/shard_map/second_1_core/ppermute | solution.py:106
  9.3 7.6 %collective-permute-start.8 = (bf16[192,3072]{1,0:T(8,128)(2,1)S(1)}, bf16[192,3072]{1,0:T(8,128)(2,1)S(1)}, u32[]{:S(2)}, u32[]{:S(2)}) collective-permute-start(bf16[192,3072]{1,0:T(8,128)(2,1)S(1)} %get-tuple-element.53), channel_id=1, source_target_pairs={{0,8},{8,0},{1,9},{9,1},{2,10},{10,2},{3,11},{11,3},{4,12},{12,4},... | collective-permute-start | bytes 3538952 | tf_op jit(solution)/shard_map/second_0_core/ppermute | solution.py:106
  10.4 12.3 %collective-permute-start.4 = (bf16[64,3072]{1,0:T(8,128)(2,1)S(1)}, bf16[64,3072]{1,0:T(8,128)(2,1)S(1)}, u32[]{:S(2)}, u32[]{:S(2)}) collective-permute-start(bf16[64,3072]{1,0:T(8,128)(2,1)S(1)} %get-tuple-element.49), channel_id=1, source_target_pairs={{0,48},{16,32},{32,16},{48,0},{1,49},{17,33},{33,17},{49,1},{2,50}... | collective-permute-start | bytes 1179656 | tf_op jit(solution)/shard_map/reduce0_p3/ppermute | solution.py:101
  13.3 15.7 %collective-permute-start.6 = (bf16[64,3072]{1,0:T(8,128)(2,1)S(1)}, bf16[64,3072]{1,0:T(8,128)(2,1)S(1)}, u32[]{:S(2)}, u32[]{:S(2)}) collective-permute-start(bf16[64,3072]{1,0:T(8,128)(2,1)S(1)} %get-tuple-element.51), channel_id=1, source_target_pairs={{0,16},{16,0},{32,48},{48,32},{1,17},{17,1},{33,49},{49,33},{2,18}... | collective-permute-start | bytes 1179656 | tf_op jit(solution)/shard_map/reduce0_p1/ppermute | solution.py:101
  13.3 15.8 %collective-permute-start.9 = (bf16[64,3072]{1,0:T(8,128)(2,1)S(1)}, bf16[64,3072]{1,0:T(8,128)(2,1)S(1)}, u32[]{:S(2)}, u32[]{:S(2)}) collective-permute-start(bf16[64,3072]{1,0:T(8,128)(2,1)S(1)} %get-tuple-element.43.refs_0_), channel_id=1, source_target_pairs={{0,64},{64,0},{1,65},{65,1},{2,66},{66,2},{3,67},{67,3},{4,68},{68... | collective-permute-start | bytes 1179656 | tf_op jit(solution)/shard_map/reduce0_z/ppermute | solution.py:99
  16.9 17.9 %collective-permute-start.11 = (bf16[64,3072]{1,0:T(8,128)(2,1)S(1)}, bf16[64,3072]{1,0:T(8,128)(2,1)S(1)}, u32[]{:S(2)}, u32[]{:S(2)}) collective-permute-start(bf16[64,3072]{1,0:T(8,128)(2,1)S(1)} %get-tuple-element.55), channel_id=1, source_target_pairs={{0,48},{16,32},{32,16},{48,0},{1,49},{17,33},{33,17},{49,1},{2,50}... | collective-permute-start | bytes 1179656 | tf_op jit(solution)/shard_map/reduce1_p3/ppermute | solution.py:101
  22.6 12.2 %collective-permute-start.5 = (bf16[64,3072]{1,0:T(8,128)(2,1)S(1)}, bf16[64,3072]{1,0:T(8,128)(2,1)S(1)}, u32[]{:S(2)}, u32[]{:S(2)}) collective-permute-start(bf16[64,3072]{1,0:T(8,128)(2,1)S(1)} %get-tuple-element.50), channel_id=1, source_target_pairs={{0,64},{64,0},{1,65},{65,1},{2,66},{66,2},{3,67},{67,3},{4,68},{68... | collective-permute-start | bytes 1179656 | tf_op jit(solution)/shard_map/reduce1_z/ppermute | solution.py:99
  29.0 9.2 %collective-permute-start.2 = (bf16[64,3072]{1,0:T(8,128)(2,1)S(1)}, bf16[64,3072]{1,0:T(8,128)(2,1)S(1)}, u32[]{:S(2)}, u32[]{:S(2)}) collective-permute-start(bf16[64,3072]{1,0:T(8,128)(2,1)S(1)} %get-tuple-element.46), channel_id=1, source_target_pairs={{0,16},{16,0},{32,48},{48,32},{1,17},{17,1},{33,49},{49,33},{2,18}... | collective-permute-start | bytes 1179656 | tf_op jit(solution)/shard_map/reduce1_p1/ppermute | solution.py:101
  29.5 10.0 %collective-permute-start.10 = (bf16[64,3072]{1,0:T(8,128)(2,1)S(1)}, bf16[64,3072]{1,0:T(8,128)(2,1)S(1)}, u32[]{:S(2)}, u32[]{:S(2)}) collective-permute-start(bf16[64,3072]{1,0:T(8,128)(2,1)S(1)} %get-tuple-element.54), channel_id=1, source_target_pairs={{0,48},{16,32},{32,16},{48,0},{1,49},{17,33},{33,17},{49,1},{2,50}... | collective-permute-start | bytes 1179656 | tf_op jit(solution)/shard_map/reduce2_p3/ppermute | solution.py:101
  33.9 12.7 %collective-permute-start.12 = (bf16[64,3072]{1,0:T(8,128)(2,1)S(1)}, bf16[64,3072]{1,0:T(8,128)(2,1)S(1)}, u32[]{:S(2)}, u32[]{:S(2)}) collective-permute-start(bf16[64,3072]{1,0:T(8,128)(2,1)S(1)} %get-tuple-element.56), channel_id=1, source_target_pairs={{0,16},{16,0},{32,48},{48,32},{1,17},{17,1},{33,49},{49,33},{2,18}... | collective-permute-start | bytes 1179656 | tf_op jit(solution)/shard_map/reduce2_p1/ppermute | solution.py:101
  34.8 14.3 %collective-permute-start.13 = (bf16[64,3072]{1,0:T(8,128)(2,1)S(1)}, bf16[64,3072]{1,0:T(8,128)(2,1)S(1)}, u32[]{:S(2)}, u32[]{:S(2)}) collective-permute-start(bf16[64,3072]{1,0:T(8,128)(2,1)S(1)} %get-tuple-element.57), channel_id=1, source_target_pairs={{0,64},{64,0},{1,65},{65,1},{2,66},{66,2},{3,67},{67,3},{4,68},{68... | collective-permute-start | bytes 1179656 | tf_op jit(solution)/shard_map/reduce2_z/ppermute | solution.py:99
  34.8 22.7 %collective-permute-start.1 = (bf16[128,3072]{1,0:T(8,128)(2,1)S(1)}, bf16[128,3072]{1,0:T(8,128)(2,1)S(1)}, u32[]{:S(2)}, u32[]{:S(2)}) collective-permute-start(bf16[128,3072]{1,0:T(8,128)(2,1)S(1)} %fetch4.1), channel_id=1, source_target_pairs={{0,8},{8,0},{1,9},{9,1},{2,10},{10,2},{3,11},{11,3},{4,12},{12,4},... | collective-permute-start | bytes 2359304 | tf_op jit(solution)/shard_map/second_2_core/ppermute | solution.py:106
  38.1 16.9 %collective-permute-start.15 = (bf16[64,3072]{1,0:T(8,128)(2,1)S(1)}, bf16[64,3072]{1,0:T(8,128)(2,1)S(1)}, u32[]{:S(2)}, u32[]{:S(2)}) collective-permute-start(bf16[64,3072]{1,0:T(8,128)(2,1)S(1)} %get-tuple-element.59), channel_id=1, source_target_pairs={{0,16},{16,0},{32,48},{48,32},{1,17},{17,1},{33,49},{49,33},{2,18}... | collective-permute-start | bytes 1179656 | tf_op jit(solution)/shard_map/reduce3_p1/ppermute | solution.py:101
  39.5 18.0 %collective-permute-start.16 = (bf16[64,3072]{1,0:T(8,128)(2,1)S(1)}, bf16[64,3072]{1,0:T(8,128)(2,1)S(1)}, u32[]{:S(2)}, u32[]{:S(2)}) collective-permute-start(bf16[64,3072]{1,0:T(8,128)(2,1)S(1)} %get-tuple-element.60), channel_id=1, source_target_pairs={{0,64},{64,0},{1,65},{65,1},{2,66},{66,2},{3,67},{67,3},{4,68},{68... | collective-permute-start | bytes 1179656 | tf_op jit(solution)/shard_map/reduce3_z/ppermute | solution.py:99
  46.6 11.0 %collective-permute-start.7 = (bf16[64,3072]{1,0:T(8,128)(2,1)S(1)}, bf16[64,3072]{1,0:T(8,128)(2,1)S(1)}, u32[]{:S(2)}, u32[]{:S(2)}) collective-permute-start(bf16[64,3072]{1,0:T(8,128)(2,1)S(1)} %get-tuple-element.52), channel_id=1, source_target_pairs={{0,48},{16,32},{32,16},{48,0},{1,49},{17,33},{33,17},{49,1},{2,50}... | collective-permute-start | bytes 1179656 | tf_op jit(solution)/shard_map/reduce3_p3/ppermute | solution.py:101
  49.5 12.8 %collective-permute-start.14 = (bf16[64,3072]{1,0:T(8,128)(2,1)S(1)}, bf16[64,3072]{1,0:T(8,128)(2,1)S(1)}, u32[]{:S(2)}, u32[]{:S(2)}) collective-permute-start(bf16[64,3072]{1,0:T(8,128)(2,1)S(1)} %get-tuple-element.58), channel_id=1, source_target_pairs={{0,64},{64,0},{1,65},{65,1},{2,66},{66,2},{3,67},{67,3},{4,68},{68... | collective-permute-start | bytes 1179656 | tf_op jit(solution)/shard_map/reduce4_z/ppermute | solution.py:99
  55.0 6.7 %collective-permute-start.17 = (bf16[32,3072]{1,0:T(8,128)(2,1)S(1)}, bf16[32,3072]{1,0:T(8,128)(2,1)S(1)}, u32[]{:S(2)}, u32[]{:S(2)}) collective-permute-start(bf16[32,3072]{1,0:T(8,128)(2,1)S(1)} %get-tuple-element.61), channel_id=1, source_target_pairs={{0,48},{16,32},{32,16},{48,0},{1,49},{17,33},{33,17},{49,1},{2,50}... | collective-permute-start | bytes 589832 | tf_op jit(solution)/shard_map/reduce4_p3/ppermute | solution.py:101
  86.0 18.9 %collective-permute-start.21 = (bf16[128,3072]{1,0:T(8,128)(2,1)S(1)}, bf16[128,3072]{1,0:T(8,128)(2,1)S(1)}, u32[]{:S(2)}, u32[]{:S(2)}) collective-permute-start(bf16[128,3072]{1,0:T(8,128)(2,1)S(1)} %get-tuple-element.65.refs_0_), channel_id=1, source_target_pairs={{0,64},{64,0},{1,65},{65,1},{2,66},{66,2},{3,67},{67,3},{4,68},{68... | collective-permute-start | bytes 2359304 | tf_op jit(solution)/shard_map/gather0_z/ppermute | solution.py:99
  87.1 17.8 %collective-permute-start.23 = (bf16[128,3072]{1,0:T(8,128)(2,1)S(1)}, bf16[128,3072]{1,0:T(8,128)(2,1)S(1)}, u32[]{:S(2)}, u32[]{:S(2)}) collective-permute-start(bf16[128,3072]{1,0:T(8,128)(2,1)S(1)} %get-tuple-element.65.refs_0_), channel_id=1, source_target_pairs={{0,16},{16,0},{32,48},{48,32},{1,17},{17,1},{33,49},{49,33},{2,18}... | collective-permute-start | bytes 2359304 | tf_op jit(solution)/shard_map/gather0_p1/ppermute | solution.py:101
  87.5 18.0 %collective-permute-start.25 = (bf16[128,3072]{1,0:T(8,128)(2,1)S(1)}, bf16[128,3072]{1,0:T(8,128)(2,1)S(1)}, u32[]{:S(2)}, u32[]{:S(2)}) collective-permute-start(bf16[128,3072]{1,0:T(8,128)(2,1)S(1)} %get-tuple-element.65.refs_0_), channel_id=1, source_target_pairs={{0,48},{16,32},{32,16},{48,0},{1,49},{17,33},{33,17},{49,1},{2,50}... | collective-permute-start | bytes 2359304 | tf_op jit(solution)/shard_map/gather0_p3/ppermute | solution.py:101
  105.6 17.4 %collective-permute-start.27 = (bf16[128,3072]{1,0:T(8,128)(2,1)S(1)}, bf16[128,3072]{1,0:T(8,128)(2,1)S(1)}, u32[]{:S(2)}, u32[]{:S(2)}) collective-permute-start(bf16[128,3072]{1,0:T(8,128)(2,1)S(1)} %get-tuple-element.66), channel_id=1, source_target_pairs={{0,64},{64,0},{1,65},{65,1},{2,66},{66,2},{3,67},{67,3},{4,68},{68... | collective-permute-start | bytes 2359304 | tf_op jit(solution)/shard_map/gather1_z/ppermute | solution.py:99
  107.6 19.5 %collective-permute-start.28 = (bf16[128,3072]{1,0:T(8,128)(2,1)S(1)}, bf16[128,3072]{1,0:T(8,128)(2,1)S(1)}, u32[]{:S(2)}, u32[]{:S(2)}) collective-permute-start(bf16[128,3072]{1,0:T(8,128)(2,1)S(1)} %get-tuple-element.67), channel_id=1, source_target_pairs={{0,16},{16,0},{32,48},{48,32},{1,17},{17,1},{33,49},{49,33},{2,18}... | collective-permute-start | bytes 2359304 | tf_op jit(solution)/shard_map/gather1_p1/ppermute | solution.py:101
  107.6 20.0 %collective-permute-start.29 = (bf16[128,3072]{1,0:T(8,128)(2,1)S(1)}, bf16[128,3072]{1,0:T(8,128)(2,1)S(1)}, u32[]{:S(2)}, u32[]{:S(2)}) collective-permute-start(bf16[128,3072]{1,0:T(8,128)(2,1)S(1)} %get-tuple-element.68), channel_id=1, source_target_pairs={{0,48},{16,32},{32,16},{48,0},{1,49},{17,33},{33,17},{49,1},{2,50}... | collective-permute-start | bytes 2359304 | tf_op jit(solution)/shard_map/gather1_p3/ppermute | solution.py:101
  108.4 20.8 %collective-permute-start.20 = (bf16[128,3072]{1,0:T(8,128)(2,1)S(1)}, bf16[128,3072]{1,0:T(8,128)(2,1)S(1)}, u32[]{:S(2)}, u32[]{:S(2)}) collective-permute-start(bf16[128,3072]{1,0:T(8,128)(2,1)S(1)} %get-tuple-element.65.refs_0_), channel_id=1, source_target_pairs={{0,8},{8,0},{1,9},{9,1},{2,10},{10,2},{3,11},{11,3},{4,12},{12,4},... | collective-permute-start | bytes 2359304 | tf_op jit(solution)/shard_map/gather1_0_core/ppermute | solution.py:106
  112.3 16.9 %collective-permute-start.22 = (bf16[128,3072]{1,0:T(8,128)(2,1)S(1)}, bf16[128,3072]{1,0:T(8,128)(2,1)S(1)}, u32[]{:S(2)}, u32[]{:S(2)}) collective-permute-start(bf16[128,3072]{1,0:T(8,128)(2,1)S(1)} %collective-permute-done.21.refs_1_.refs_2_), channel_id=1, source_target_pairs={{0,8},{8,0},{1,9},{9,1},{2,10},{10,2},{3,11},{11,3},{4,12},{12,4},... | collective-permute-start | bytes 2359304 | tf_op jit(solution)/shard_map/gather1_1_core/ppermute | solution.py:106
  123.0 7.1 %collective-permute-start.24 = (bf16[128,3072]{1,0:T(8,128)(2,1)S(1)}, bf16[128,3072]{1,0:T(8,128)(2,1)S(1)}, u32[]{:S(2)}, u32[]{:S(2)}) collective-permute-start(bf16[128,3072]{1,0:T(8,128)(2,1)S(1)} %collective-permute-done.23.refs_2_.refs_4_), channel_id=1, source_target_pairs={{0,8},{8,0},{1,9},{9,1},{2,10},{10,2},{3,11},{11,3},{4,12},{12,4},... | collective-permute-start | bytes 2359304 | tf_op jit(solution)/shard_map/gather1_2_core/ppermute | solution.py:106
  127.6 11.0 %collective-permute-start.32 = (bf16[64,3072]{1,0:T(8,128)(2,1)S(1)}, bf16[64,3072]{1,0:T(8,128)(2,1)S(1)}, u32[]{:S(2)}, u32[]{:S(2)}) collective-permute-start(bf16[64,3072]{1,0:T(8,128)(2,1)S(1)} %get-tuple-element.75), channel_id=1, source_target_pairs={{0,64},{64,0},{1,65},{65,1},{2,66},{66,2},{3,67},{67,3},{4,68},{68... | collective-permute-start | bytes 1179656 | tf_op jit(solution)/shard_map/gather2_z/ppermute | solution.py:99
  129.2 8.1 %collective-permute-start.30 = (bf16[32,3072]{1,0:T(8,128)(2,1)S(1)}, bf16[32,3072]{1,0:T(8,128)(2,1)S(1)}, u32[]{:S(2)}, u32[]{:S(2)}) collective-permute-start(bf16[32,3072]{1,0:T(8,128)(2,1)S(1)} %get-tuple-element.73), channel_id=1, source_target_pairs={{0,16},{16,0},{32,48},{48,32},{1,17},{17,1},{33,49},{49,33},{2,18}... | collective-permute-start | bytes 589832 | tf_op jit(solution)/shard_map/gather2_p1/ppermute | solution.py:101
  129.2 8.6 %collective-permute-start.31 = (bf16[32,3072]{1,0:T(8,128)(2,1)S(1)}, bf16[32,3072]{1,0:T(8,128)(2,1)S(1)}, u32[]{:S(2)}, u32[]{:S(2)}) collective-permute-start(bf16[32,3072]{1,0:T(8,128)(2,1)S(1)} %get-tuple-element.74), channel_id=1, source_target_pairs={{0,48},{16,32},{32,16},{48,0},{1,49},{17,33},{33,17},{49,1},{2,50}... | collective-permute-start | bytes 589832 | tf_op jit(solution)/shard_map/gather2_p3/ppermute | solution.py:101
  130.1 10.8 %collective-permute-start.34 = (bf16[128,3072]{1,0:T(8,128)(2,1)S(1)}, bf16[128,3072]{1,0:T(8,128)(2,1)S(1)}, u32[]{:S(2)}, u32[]{:S(2)}) collective-permute-start(bf16[128,3072]{1,0:T(8,128)(2,1)S(1)} %collective-permute-done.27.refs_8_.refs_0_), channel_id=1, source_target_pairs={{0,8},{8,0},{1,9},{9,1},{2,10},{10,2},{3,11},{11,3},{4,12},{12,4},... | collective-permute-start | bytes 2359304 | tf_op jit(solution)/shard_map/gather2_0_core/ppermute | solution.py:106
  131.7 9.1 %collective-permute-start.35 = (bf16[128,3072]{1,0:T(8,128)(2,1)S(1)}, bf16[128,3072]{1,0:T(8,128)(2,1)S(1)}, u32[]{:S(2)}, u32[]{:S(2)}) collective-permute-start(bf16[128,3072]{1,0:T(8,128)(2,1)S(1)} %collective-permute-done.28.refs_9_.refs_1_), channel_id=1, source_target_pairs={{0,8},{8,0},{1,9},{9,1},{2,10},{10,2},{3,11},{11,3},{4,12},{12,4},... | collective-permute-start | bytes 2359304 | tf_op jit(solution)/shard_map/gather2_1_core/ppermute | solution.py:106
  (5 other events, 22.7 us)
